TPU v7x, 128 devices: a whole 4x4x4 slice. The times are simulated.
128 devices in a mesh: cp: 8 (over x_hi, y), grp: 16 (over z, x_lo, core).
Axes of the slice: x: 4 (x_hi: 2, x_lo: 2; x = x_hi * 2 + x_lo), y: 4, z: 4, core: 2. Of those that a mesh axis runs over, the one named last changes fastest.
Arguments:
- queries: bfloat16 [32, 1024, 2048], P('grp', 'cp'), may hold values from -108 to 108
- keys: bfloat16 [32, 1024, 2048], P('grp', 'cp'), may hold values from -4 to 4
- values: bfloat16 [32, 1024, 2048], P('grp', 'cp'), may hold values from -6 to 6
- lengths: int32 [32], P('grp'), may hold values from 256 to 1024
- frame_map: bfloat16 [2048, 2176], replicated, may hold values from -0.125 to 0.125
- proj_weight: bfloat16 [2176, 4096], P('grp', 'cp'), may hold values from -0.125 to 0.125
- head_weight: bfloat16 [4096, 256], P('cp'), may hold values from -0.375 to 0.375
- act_embed: float32 [7, 4096], P(None, 'cp'), may hold values from -0.5 to 0.5
- actions: int32 [32, 7], P('grp'), may hold values from 0 to 255
- action_mask: int32 [32, 7], P('grp'), may hold values 0 or 1
- group_ids: int32 [32], P('grp'), may hold values from 0 to 3
- rewards: float32 [32], P('grp'), may hold values from -6 to 6
Outputs:
- logprobs: float32 [32, 7], P('grp')
- grad_proj: bfloat16 [2176, 4096], P('grp', 'cp')
- grad_head: bfloat16 [4096, 256], P('cp')
All inputs are finite; a program needn't handle non-finite values. No bound on the sum of `action_mask` on one device may be relied on, other than what follows from the above.
Results may differ from a plain program's by a relative error of at most 0.018.
Values may be sent and summed in bfloat16 or wider, within the bound.
No kernel may reach another device: no remote copies, remote signals or barrier semaphores. Data moves between devices by JAX's collectives and lax.ppermute only.
A program may use at most 128 MiB of HBM per device.

v0:
```python
import functools
import math

import jax
import jax.numpy as jnp
from jax import lax
from jax.experimental import pallas as pl
from jax.experimental.pallas import tpu as pltpu
from jax.sharding import Mesh
from jax.sharding import PartitionSpec as P


F32, BF16 = jnp.float32, jnp.bfloat16
HD = 128
HEADS_HERE = 4
COLS = 512
ATT = 2048
VIS = 2176
ROWS = 136
HID_HERE = 1024
SEQ = 1024
CHUNKS = 2
CH = SEQ // CHUNKS
NBINS = 256
SQRT_HALF = 0.7071067811865476
INV_ROOT_TAU = 0.3989422804014327
NEG_LARGE = -1e30
EXP2_SCALE = math.log2(math.e) / math.sqrt(HD)
VMEM_LIMIT = 67043328


def params(dims=1):
    return pltpu.CompilerParams(
        dimension_semantics=("arbitrary",) * dims, vmem_limit_bytes=VMEM_LIMIT
    )


def cost(flops, nbytes, trans=0):
    return pl.CostEstimate(flops=flops, bytes_accessed=nbytes, transcendentals=trans)


def shifted(x, axis, by):
    count = lax.axis_size(axis)
    return lax.ppermute(x, axis, [(i, (i + by) % count) for i in range(count)])


def dealt(x, axes):
    return lax.all_to_all(x, axes, 0, 0, tiled=True)


def pack_kernel(q_ref, k_ref, v_ref, o_ref):
    for i, ref in enumerate((q_ref, k_ref, v_ref)):
        for j in range(2):
            o_ref[j, i] = ref[0, :, j * COLS : (j + 1) * COLS]


def pack(q, k, v):
    spec = pl.BlockSpec((1, 128, 2 * COLS), lambda i: (i // 2, 0, i % 2))
    return pl.pallas_call(
        pack_kernel,
        out_shape=jax.ShapeDtypeStruct((8, 3, 128, COLS), BF16),
        grid=(4,),
        in_specs=[spec] * 3,
        out_specs=pl.BlockSpec((2, 3, 128, COLS), lambda i: (i, 0, 0, 0)),
        compiler_params=params(),
        cost_estimate=cost(0, 6 << 20),
        name="pack",
    )(q, k, v)


def attend_kernel(len_ref, q_ref, k_ref, v_ref, *rest):
    o_ref = rest[-1]
    k = k_ref[...].reshape(SEQ, HD)
    v = v_ref[...].reshape(SEQ, HD)
    at = lax.broadcasted_iota(jnp.int32, (1, SEQ), 1)
    bias = jnp.where(at < len_ref[0], 0.0, NEG_LARGE)
    for r in range(CH // 256):
        q = q_ref[2 * r : 2 * r + 2].reshape(256, HD)
        s = lax.dot_general(q, k, (((1,), (1,)), ((), ())), preferred_element_type=F32)
        s = s + bias
        top = jnp.max(s, axis=-1, keepdims=True)
        p = jnp.exp2((s - top) * EXP2_SCALE)
        total = jnp.sum(p, axis=-1, keepdims=True)
        w = jnp.dot(p.astype(BF16), v, preferred_element_type=F32)
        o_ref[r * 256 : (r + 1) * 256, :] = (w / total).astype(BF16)


def attend(got, length, chunk, after):
    blocks = CH // 128

    def part(which, count):
        return pl.BlockSpec(
            (count, 1, 128, HD),
            lambda h, n: (chunk if which == 0 else 0, which, 0, h),
        )

    return pl.pallas_call(
        attend_kernel,
        out_shape=jax.ShapeDtypeStruct((CH, COLS), BF16),
        grid_spec=pltpu.PrefetchScalarGridSpec(
            num_scalar_prefetch=1,
            grid=(HEADS_HERE,),
            in_specs=[part(0, blocks), part(1, 8), part(2, 8)]
            + [pl.BlockSpec(memory_space=pl.ANY)] * len(after),
            out_specs=pl.BlockSpec((CH, HD), lambda h, n: (0, h)),
        ),
        compiler_params=params(),
        cost_estimate=cost(4 * CH * SEQ * COLS, 3 << 20, 4 * CH * SEQ),
        name="attend",
    )(length, got, got, got, *after)


def frames_kernel(idx_ref, a_ref, b_ref, c_ref, d_ref, fm_ref, last_ref, *rest):
    o_ref, full = rest[-2:]
    step = pl.program_id(0)

    @pl.when(step == 0)
    def _():
        for i, ref in enumerate((a_ref, b_ref, c_ref, d_ref)):
            full[:, pl.ds(pl.multiple_of(idx_ref[i] * COLS, COLS), COLS)] = ref[...]

    term = jnp.dot(full[...], fm_ref[...], preferred_element_type=F32)
    o_ref[:, pl.ds(pl.multiple_of(step * 512, 512), 512)] = term.astype(BF16)

    @pl.when(step == 3)
    def _():
        term = jnp.dot(full[...], last_ref[...], preferred_element_type=F32)
        o_ref[:, 2048:] = term.astype(BF16)


def frames_of(idx, pieces, frame_map, chunk, before, after=()):
    whole = pl.BlockSpec((CH, COLS), lambda k, n: (0, 0))
    more = [] if before is None else [before]
    return pl.pallas_call(
        frames_kernel,
        out_shape=jax.ShapeDtypeStruct((SEQ, VIS), BF16),
        grid_spec=pltpu.PrefetchScalarGridSpec(
            num_scalar_prefetch=1,
            grid=(4,),
            in_specs=[whole] * 4
            + [
                pl.BlockSpec((ATT, 512), lambda k, n: (0, k)),
                pl.BlockSpec((ATT, 128), lambda k, n: (0, 16)),
            ]
            + [pl.BlockSpec(memory_space=pl.ANY)] * (len(more) + len(after)),
            out_specs=pl.BlockSpec((CH, VIS), lambda k, n: (chunk, 0)),
            scratch_shapes=[pltpu.VMEM((CH, ATT), BF16)],
        ),
        input_output_aliases={} if before is None else {7: 0},
        compiler_params=params(),
        cost_estimate=cost(2 * CH * ATT * VIS, 13 << 20),
        name="frames",
    )(idx, *pieces, frame_map, frame_map, *more, *after)


def assemble_kernel(z_ref, x_ref, core_ref, *refs):
    o_ref = refs[-1]
    lead = core_ref[0] == 0
    for k in range(4):
        for i in range(4):
            mine, other = refs[k][i].astype(F32), refs[4 + k][i].astype(F32)
            pair = [jnp.where(lead, mine, other), jnp.where(lead, other, mine)]
            x = x_ref[i]
            row = pl.multiple_of((z_ref[k] * 2 + x % 2) * 2 * ROWS, 2 * ROWS)
            col = pl.multiple_of((x // 2) * COLS, COLS)
            o_ref[pl.ds(row, 2 * ROWS), pl.ds(col, COLS)] = jnp.concatenate(pair, axis=0).astype(
                BF16
            )


def assemble(z_order, x_order, core, own, other):
    return pl.pallas_call(
        assemble_kernel,
        out_shape=jax.ShapeDtypeStruct((VIS, HID_HERE), BF16),
        in_specs=[pl.BlockSpec(memory_space=pltpu.SMEM)] * 3
        + [pl.BlockSpec(memory_space=pltpu.VMEM)] * 8,
        compiler_params=pltpu.CompilerParams(vmem_limit_bytes=VMEM_LIMIT),
        cost_estimate=cost(1 << 20, 9 << 20),
        name="assemble",
    )(z_order, x_order, core, *own, *other)


def hidden_kernel(chunk, len_ref, f_ref, w_ref, *rest):
    slope_ref, pool_ref = rest[-2:]
    t = jnp.dot(f_ref[...], w_ref[...], preferred_element_type=F32)
    cdf = 0.5 * (1.0 + lax.erf(t * SQRT_HALF))
    at = lax.broadcasted_iota(jnp.int32, t.shape, 0) + chunk * CH
    live = at < len_ref[0]
    slope = cdf + t * jnp.exp(-0.5 * t * t) * INV_ROOT_TAU
    slope_ref[...] = jnp.where(live, slope, 0.0).astype(BF16)
    part = jnp.sum(jnp.where(live, t * cdf, 0.0), axis=0, keepdims=True)
    pool_ref[...] = jnp.broadcast_to(part, pool_ref.shape)


def hidden_of(length, frames, weight, chunk, before):
    tile = 256
    more = [] if before is None else [before]
    return pl.pallas_call(
        functools.partial(hidden_kernel, chunk),
        out_shape=(
            jax.ShapeDtypeStruct((SEQ, HID_HERE), BF16),
            jax.ShapeDtypeStruct((8, HID_HERE), F32),
        ),
        grid_spec=pltpu.PrefetchScalarGridSpec(
            num_scalar_prefetch=1,
            grid=(HID_HERE // tile,),
            in_specs=[
                pl.BlockSpec((CH, VIS), lambda j, n: (chunk, 0)),
                pl.BlockSpec((VIS, tile), lambda j, n: (0, j)),
            ]
            + [pl.BlockSpec(memory_space=pl.ANY)] * len(more),
            out_specs=(
                pl.BlockSpec((CH, tile), lambda j, n: (chunk, j)),
                pl.BlockSpec((8, tile), lambda j, n: (0, j)),
            ),
        ),
        input_output_aliases={} if before is None else {3: 0},
        compiler_params=params(),
        cost_estimate=cost(2 * CH * HID_HERE * VIS, 6 << 20, 2 * CH * HID_HERE),
        name="hidden",
    )(length, frames, weight, *more)


def grad_kernel(core_ref, f_ref, s_ref, keep_ref, send_ref, total):
    for r in range(VIS // 128):
        total[r * 128 : (r + 1) * 128, :] = lax.dot_general(
            f_ref[:, r * 128 : (r + 1) * 128],
            s_ref[...],
            (((0,), (0,)), ((), ())),
            preferred_element_type=F32,
        )
    core = core_ref[0]
    for b in range(8):
        mine = pl.multiple_of((2 * b + core) * ROWS, 8)
        other = pl.multiple_of((2 * b + 1 - core) * ROWS, 8)
        keep_ref[b, 0] = total[pl.ds(mine, ROWS), :].astype(BF16)
        send_ref[b, 0] = total[pl.ds(other, ROWS), :].astype(BF16)


def grad_of(core, frames, slope):
    out = jax.ShapeDtypeStruct((8, 2, ROWS, COLS), BF16)
    spec = pl.BlockSpec((8, 1, ROWS, COLS), lambda j, n: (0, j, 0, 0))
    return pl.pallas_call(
        grad_kernel,
        out_shape=(out, out),
        grid_spec=pltpu.PrefetchScalarGridSpec(
            num_scalar_prefetch=1,
            grid=(2,),
            in_specs=[
                pl.BlockSpec((SEQ, VIS), lambda j, n: (0, 0)),
                pl.BlockSpec((SEQ, COLS), lambda j, n: (0, j)),
            ],
            out_specs=(spec, spec),
            scratch_shapes=[pltpu.VMEM((VIS, COLS), F32)],
        ),
        compiler_params=params(),
        cost_estimate=cost(2 * SEQ * HID_HERE * VIS, 11 << 20),
        name="grad",
    )(core, frames, slope)


def logit_kernel(part_ref, act_ref, weight_ref, inv_ref, hw_ref, lp_ref, lg_ref, scale_ref):
    logits = (part_ref[0] + part_ref[1]) + (part_ref[2] + part_ref[3])
    top = jnp.max(logits, axis=-1, keepdims=True)
    down = logits - top
    log_all = down - jnp.log(jnp.sum(jnp.exp(down), axis=-1, keepdims=True))
    at = lax.broadcasted_iota(jnp.int32, logits.shape, 2)
    picked = (at == act_ref[...]).astype(F32)
    lp = jnp.sum(picked * log_all, axis=-1, keepdims=True)
    lp_ref[...] = jnp.broadcast_to(lp, lp_ref.shape)
    grad = (weight_ref[...] * (picked - jnp.exp(log_all))).astype(BF16)
    lg_ref[...] = grad
    for c in range(2):
        back = lax.dot_general(
            grad[c], hw_ref[...], (((1,), (1,)), ((), ())), preferred_element_type=F32
        )
        pool = jnp.sum(back, axis=0, keepdims=True) * inv_ref[c]
        scale_ref[c] = jnp.broadcast_to(pool, scale_ref.shape[1:])


def logit_parts(parts, acts, weights, inv, hw):
    return pl.pallas_call(
        logit_kernel,
        out_shape=(
            jax.ShapeDtypeStruct((2, 8, 128), F32),
            jax.ShapeDtypeStruct((2, 8, NBINS), BF16),
            jax.ShapeDtypeStruct((2, 8, HID_HERE), F32),
        ),
        in_specs=[pl.BlockSpec(memory_space=pltpu.VMEM)] * 3
        + [pl.BlockSpec(memory_space=pltpu.SMEM), pl.BlockSpec(memory_space=pltpu.VMEM)],
        compiler_params=pltpu.CompilerParams(vmem_limit_bytes=VMEM_LIMIT),
        cost_estimate=cost(8 << 20, 1 << 20, 8192),
        name="logit",
    )(parts, acts, weights, inv, hw)


def scale_kernel(core_ref, keep_ref, got_ref, scale_ref, head_ref, lg_ref, o_ref):
    core = core_ref[0]
    mine = scale_ref[core][0:1]
    other = scale_ref[1 - core][0:1]
    lower = jnp.concatenate([lg_ref[core].astype(F32), jnp.zeros((8, NBINS), F32)], axis=1)
    for b in range(2):
        for x in range(2):
            cols = slice(x * COLS, (x + 1) * COLS)
            top = (
                keep_ref[b, x].astype(F32) * mine[:, cols]
                + got_ref[b, x].astype(F32) * other[:, cols]
            )
            o_ref[b, x] = jnp.concatenate(
                [top, head_ref[:, cols].astype(F32), lower], axis=0
            ).astype(BF16)


def scaled(core, keep, got, scale, head_input, lgrad):
    spec = pl.BlockSpec((2, 2, ROWS, COLS), lambda i, n: (i, 0, 0, 0))
    return pl.pallas_call(
        scale_kernel,
        out_shape=jax.ShapeDtypeStruct((8, 2, ROWS + 16, COLS), BF16),
        grid_spec=pltpu.PrefetchScalarGridSpec(
            num_scalar_prefetch=1,
            grid=(4,),
            in_specs=[
                spec,
                spec,
                pl.BlockSpec((2, 8, HID_HERE), lambda i, n: (0, 0, 0)),
                pl.BlockSpec((8, HID_HERE), lambda i, n: (0, 0)),
                pl.BlockSpec((2, 8, NBINS), lambda i, n: (0, 0, 0)),
            ],
            out_specs=pl.BlockSpec((2, 2, ROWS + 16, COLS), lambda i, n: (i, 0, 0, 0)),
        ),
        compiler_params=params(),
        cost_estimate=cost(8 << 20, 7 << 20),
        name="scaled",
    )(core, keep, got, scale, head_input, lgrad)


def episode_facts(lengths, actions, action_mask, group_ids, rewards):
    three = jnp.stack([rewards, group_ids.astype(F32), lengths.astype(F32)], axis=1)
    return jnp.concatenate(
        [
            jnp.pad(three, ((0, 0), (0, 5))),
            jnp.pad(actions.astype(F32), ((0, 0), (0, 1))),
            jnp.pad(action_mask.astype(F32), ((0, 0), (0, 1))),
        ],
        axis=1,
    )


def loss_terms(every, here):
    gains, groups, masks = every[:, 0], every[:, 1], every[:, 16:24]
    member = (groups[:, None] == jnp.arange(4, dtype=F32)[None, :]).astype(F32)
    sums = jnp.sum(member * gains[:, None], axis=0)
    squares = jnp.sum(member * (gains * gains)[:, None], axis=0)
    sizes = jnp.maximum(jnp.sum(member, axis=0), 1.0)
    mean = sums / sizes
    spread = jnp.sqrt(jnp.maximum(squares / sizes - mean * mean, 1.0))
    count = jnp.maximum(jnp.sum(masks), 1.0)
    own = (here[:, 1:2] == jnp.arange(4, dtype=F32)[None, :]).astype(F32)
    advantage = (here[:, 0] - jnp.sum(own * mean[None, :], axis=1)) / jnp.sum(
        own * spread[None, :], axis=1
    )
    return -here[:, 16:24] * advantage[:, None] / count, here[:, 8:16], 1.0 / here[:, 2]


def per_device(
    queries,
    keys,
    values,
    lengths,
    frame_map,
    proj_weight,
    head_weight,
    act_embed,
    actions,
    action_mask,
    group_ids,
    rewards,
):
    xh = lax.axis_index("xh")
    y = lax.axis_index("y")
    z = lax.axis_index("z")
    xl = lax.axis_index("xl")
    core = lax.axis_index("c")
    core1 = core.reshape(1)
    length = lax.dynamic_slice_in_dim(lengths, xh, 1)

    got = dealt(pack(queries, keys, values), ("xh", "y"))

    x = xh * 2 + xl
    line = ("xh", "xl")
    row = [proj_weight] + [shifted(proj_weight, line, by) for by in (1, -1, 2)]
    x_order = (x + jnp.array([0, 3, 1, 2], jnp.int32)) % 4
    block = jnp.stack(row)
    up, down = shifted(block, "z", 1), shifted(block, "z", -1)
    half = jnp.concatenate([shifted(up[:2], "z", 1), shifted(down[2:], "z", -1)])
    z_order = (z + jnp.array([0, 3, 1, 2], jnp.int32)) % 4
    own = (block, up, down, half)
    other = [shifted(w, "c", 1) for w in own]
    weight = assemble(z_order, x_order, core1, own, other)

    first = xh == 0
    hw_other, ae_other = shifted(head_weight, "xh", 1), shifted(act_embed, "xh", 1)

    def both(mine, other, axis):
        return jnp.concatenate(
            [jnp.where(first, mine, other), jnp.where(first, other, mine)], axis=axis
        )

    hw = both(head_weight, hw_other, 0)
    embed = jnp.pad(both(act_embed, ae_other, 1), ((0, 1), (0, 0)))

    facts = episode_facts(lengths, actions, action_mask, group_ids, rewards)
    facts = jnp.concatenate([facts, shifted(facts, "c", 1)])
    pair = lax.dynamic_slice(facts.reshape(2, 2, 24), (0, xh, 0), (2, 1, 24)).reshape(2, 24)
    pair = jnp.where(core == 0, pair, pair[::-1])
    facts = jnp.concatenate([facts, shifted(facts, "xl", 1)])
    facts = jnp.concatenate([facts] + [shifted(facts, "z", by) for by in (1, 2, 3)])
    loss_weight, acts, inverse = loss_terms(facts, pair)
    wide_weight = jnp.broadcast_to(loss_weight[:, :, None], (2, 8, NBINS))
    wide_acts = jnp.broadcast_to(acts[:, :, None], (2, 8, NBINS)).astype(jnp.int32)

    idx = (y + jnp.array([0, 3, 1, 2], jnp.int32)) % 4
    a0 = attend(got, length, 0, (wide_weight, wide_acts, hw, embed, up, down))
    a1 = attend(got, length, 1, ())
    b0 = shifted(a0, "y", 1)
    c0 = shifted(a0, "y", -1)
    b1 = shifted(a1, "y", 1)
    c1 = shifted(a1, "y", -1)
    d0 = shifted(b0, "y", 1)
    d1 = shifted(c1, "y", -1)

    frames = frames_of(idx, (a0, b0, c0, d0), frame_map, 0, None, (weight,))
    slope, pool0 = hidden_of(length, frames, weight, 0, None)
    frames = frames_of(idx, (a1, b1, c1, d1), frame_map, 1, frames)
    slope, pool1 = hidden_of(length, frames, weight, 1, slope)
    pooled = (pool0 + pool1) / length.astype(F32)
    head_input = (pooled + embed).astype(BF16)
    part = jnp.dot(head_input, hw, preferred_element_type=F32)
    parts = dealt(jnp.broadcast_to(part[None], (8, 8, NBINS)), ("y", "c"))
    keep, send = grad_of(core1, frames, slope)
    arrived = shifted(send, "c", 1)

    logprob, lgrad, scale = logit_parts(
        parts.reshape(4, 2, 8, NBINS), wide_acts, wide_weight, inverse, hw
    )
    summed = scaled(core1, keep, arrived, scale, head_input, lgrad)
    dealt_out = dealt(summed.reshape(16, ROWS + 16, COLS), ("z", "xl", "xh"))
    grad_proj = jnp.sum(dealt_out[:, :ROWS].astype(F32), axis=0).astype(BF16)

    own_head = dealt_out[:, ROWS:]
    other_head = shifted(own_head, "c", 1)
    heads = jnp.stack([own_head, other_head])
    lefts = heads[:, :, :8].reshape(256, COLS)
    rights = heads[:, :, 8:, :NBINS].reshape(256, NBINS)
    grad_head = lax.dot_general(
        lefts, rights, (((0,), (0,)), ((), ())), preferred_element_type=F32
    ).astype(BF16)

    lp_mine = lax.dynamic_index_in_dim(logprob[:, :7, 0], core, 0)
    lp_other = shifted(lp_mine, "xh", 1)
    logprobs = both(lp_mine, lp_other, 0)
    return logprobs, grad_proj, grad_head


def solution(mesh):
    fine = Mesh(mesh.devices.reshape(2, 4, 4, 2, 2), ("xh", "y", "z", "xl", "c"))
    cp, grp = ("xh", "y"), ("z", "xl", "c")
    in_specs = (
        P(grp, cp, None),
        P(grp, cp, None),
        P(grp, cp, None),
        P(grp),
        P(),
        P(grp, cp),
        P(cp, None),
        P(None, cp),
        P(grp, None),
        P(grp, None),
        P(grp),
        P(grp),
    )
    out_specs = (P(grp, None), P(grp, cp), P(cp, None))
    return jax.shard_map(
        per_device, mesh=fine, in_specs=in_specs, out_specs=out_specs, check_vma=False
    )
```

profile of v0, /device:TPU:1, one launch (start us, length us, event | category | flops | bytes accessed | tf_op | source)
XLA Modules:
  0.0 249.3 jit_solution(6447783383636219023)
XLA Ops:
  0.6 3.6 %collective-permute-start.9 = (bf16[136,512]{1,0:T(8,128)(2,1)}, bf16[136,512]{1,0:T(8,128)(2,1)}, u32[]{:S(2)}, u32[]{:S(2)}) collective-permute-start(bf16[136,512]{1,0:T(8,128)(2,1)} %param.20), channel_id=1, source_target_pairs={{0,64},{2,66},{64,0},{66,2},{1,65},{3,67},{65,1},{67,3},{4,68},{6,... | collective-permute-start | bytes 417800 | tf_op jit(solution)/shard_map/ppermute | solution.py:44
  4.6 4.2 %pack.1 = bf16[8,3,128,512]{3,2,1,0:T(8,128)(2,1)} custom-call(bf16[2,128,2048]{2,1,0:T(8,128)(2,1)} %q_ref.1, bf16[2,128,2048]{2,1,0:T(8,128)(2,1)} %k_ref.1, bf16[2,128,2048]{2,1,0:T(8,128)(2,1)} %v_ref.1), custom_call_target="tpu_custom_call" | custom-call | bytes 6291456 | tf_op jit(solution)/shard_map/pack/pallas_call | solution.py:59
  8.8 5.8 %all-to-all-start = ((bf16[8,3,128,512]{3,2,1,0:T(8,128)(2,1)}), bf16[8,3,128,512]{3,2,1,0:T(8,128)(2,1)}, u32[]{:S(2)}, u32[]{:S(2)}) async-start(bf16[8,3,128,512]{3,2,1,0:T(8,128)(2,1)} %pack.1), calls=%async_computation | async-start | bytes 6291456 | tf_op jit(solution)/shard_map/all_to_all | solution.py:48
  14.9 1.5 collective-permute-start
  17.3 1.2 collective-permute-start.1
  18.6 30.8 %collective-permute-done.1 = f32[4,24]{1,0:T(4,128)S(1)} collective-permute-done((f32[4,24]{1,0:T(4,128)S(1)}, f32[4,24]{1,0:T(4,128)S(1)}, u32[]{:S(2)}, u32[]{:S(2)}) %collective-permute-start.1) | collective-permute-done | bytes 416 | tf_op jit(solution)/shard_map/ppermute | solution.py:44
  49.5 1.6 collective-permute-start.2
  51.2 3.3 %collective-permute-start.3 = (f32[8,24]{1,0:T(8,128)S(1)}, f32[8,24]{1,0:T(8,128)S(1)}, u32[]{:S(2)}, u32[]{:S(2)}) collective-permute-start(f32[8,24]{1,0:T(8,128)S(1)} %pad_maximum_fusion.2), channel_id=1, source_target_pairs={{0,8},{4,12},{8,0},{12,4},{1,9},{5,13},{9,1},{13,5},{2,10},{6,14},... | collective-permute-start | bytes 2312 | tf_op jit(solution)/shard_map/ppermute | solution.py:44
  55.9 1.8 collective-permute-start.8
  57.7 1.6 collective-permute-start.5
  59.3 1.3 collective-permute-start.6
  63.0 1.9 pad_maximum_fusion.refs_0_
  65.6 1.9 collective-permute-start.11
  68.2 6.2 %collective-permute-start.17 = (bf16[4,136,512]{2,1,0:T(8,128)(2,1)}, bf16[4,136,512]{2,1,0:T(8,128)(2,1)}, u32[]{:S(2)}, u32[]{:S(2)}) collective-permute-start(bf16[4,136,512]{2,1,0:T(8,128)(2,1)} %pad_maximum_fusion.refs_0_), channel_id=1, source_target_pairs={{0,1},{1,0},{2,3},{3,2},{4,5},{5,4},{6,7},{7,6},{8,9},{9,8},{10,11... | collective-permute-start | bytes 1671176 | tf_op jit(solution)/shard_map/ppermute | solution.py:44
  74.5 0.8 pad_maximum_fusion.1.rest_2_.hw_ref
  75.3 1.7 slice.63
  77.0 6.8 %collective-permute-start.18 = (bf16[4,136,512]{2,1,0:T(8,128)(2,1)}, bf16[4,136,512]{2,1,0:T(8,128)(2,1)}, u32[]{:S(2)}, u32[]{:S(2)}) collective-permute-start(bf16[4,136,512]{2,1,0:T(8,128)(2,1)} %collective-permute-done.10.rest_4_.refs_1_), channel_id=1, source_target_pairs={{0,1},{1,0},{2,3},{3,2},{4,5},{5,4},{6,7},{7,6},{8,9},{9,8},{10,11... | collective-permute-start | bytes 1671176 | tf_op jit(solution)/shard_map/ppermute | solution.py:44
  85.1 7.0 %attend.2.a_ref = bf16[512,512]{1,0:T(8,128)(2,1)} custom-call(s32[1]{0:T(128)} %dynamic_slice.12.len_ref, bf16[8,3,128,512]{3,2,1,0:T(8,128)(2,1)} %all-to-all-done.q_ref.k_ref.v_ref, bf16[8,3,128,512]{3,2,1,0:T(8,128)(2,1)} %all-to-all-done.q_ref.k_ref.v_ref, bf16[8,3,128,512]{3,2,1,0:T(8,128)(2,1)} %all-to-all-done.q_ref.k_ref.v_ref, ...), custom_call_target="tpu_custom_call" | custom-call | flops 1073741824 | bytes 3145728 | tf_op jit(solution)/shard_map/attend/pallas_call | solution.py:97
  92.1 1.1 collective-permute-start.12
  93.2 1.0 slice.64
  94.1 2.5 %collective-permute-start.16 = (bf16[2,136,512]{2,1,0:T(8,128)(2,1)S(1)}, bf16[2,136,512]{2,1,0:T(8,128)(2,1)S(1)}, u32[]{:S(2)}, u32[]{:S(2)}) collective-permute-start(bf16[2,136,512]{2,1,0:T(8,128)(2,1)S(1)} %slice.64), channel_id=1, source_target_pairs={{0,12},{4,0},{8,4},{12,8},{1,13},{5,1},{9,5},{13,9},{2,14},{6,2},{... | collective-permute-start | bytes 835592 | tf_op jit(solution)/shard_map/ppermute | solution.py:44
  97.2 1.7 constant_dynamic-update-slice_fusion.1
  98.9 3.5 %collective-permute-done.16 = bf16[2,136,512]{2,1,0:T(8,128)(2,1)S(1)} collective-permute-done((bf16[2,136,512]{2,1,0:T(8,128)(2,1)S(1)}, bf16[2,136,512]{2,1,0:T(8,128)(2,1)S(1)}, u32[]{:S(2)}, u32[]{:S(2)}) %collective-permute-start.16) | collective-permute-done | bytes 278560 | tf_op jit(solution)/shard_map/ppermute | solution.py:44
  103.1 1.1 collective-permute-start.20
  104.3 7.0 %attend.3.a_ref = bf16[512,512]{1,0:T(8,128)(2,1)} custom-call(s32[1]{0:T(128)} %dynamic_slice.12.len_ref, bf16[8,3,128,512]{3,2,1,0:T(8,128)(2,1)} %all-to-all-done.q_ref.k_ref.v_ref, bf16[8,3,128,512]{3,2,1,0:T(8,128)(2,1)} %all-to-all-done.q_ref.k_ref.v_ref, bf16[8,3,128,512]{3,2,1,0:T(8,128)(2,1)} %all-to-all-done.q_ref.k_ref.v_ref), custom_call_target="tpu_custom_call" | custom-call | flops 1073741824 | bytes 3145728 | tf_op jit(solution)/shard_map/attend/pallas_call | solution.py:97
  111.3 1.6 collective-permute-start.22
  112.9 1.4 collective-permute-start.13
  114.4 1.2 and_select_fusion
  115.6 5.3 %assemble.1.rest_0_.w_ref = bf16[2176,1024]{1,0:T(8,128)(2,1)} custom-call(s32[4]{0:T(128)} %get-tuple-element.45.z_ref, s32[4]{0:T(128)} %get-tuple-element.43.x_ref, s32[1]{0:T(128)} %bitcast.11.core_ref, bf16[4,136,512]{2,1,0:T(8,128)(2,1)} %pad_maximum_fusion.refs_0_, bf16[4,136,512]{2,1,0:T(8,128)(2,1)} %collective-permute-done.10.rest_4_.refs_1_, ...), custom_call_target="tpu_custom_call" | custom-call | flops 1048576 | bytes 9437184 | tf_op jit(solution)/shard_map/assemble/pallas_call | solution.py:172
  121.0 4.1 %collective-permute-done.22.c_ref = bf16[512,512]{1,0:T(8,128)(2,1)} collective-permute-done((bf16[512,512]{1,0:T(8,128)(2,1)}, bf16[512,512]{1,0:T(8,128)(2,1)}, u32[]{:S(2)}, u32[]{:S(2)}) %collective-permute-start.22) | collective-permute-done | bytes 524320 | tf_op jit(solution)/shard_map/ppermute | solution.py:44
  125.1 2.8 %collective-permute-start.23 = (bf16[512,512]{1,0:T(8,128)(2,1)}, bf16[512,512]{1,0:T(8,128)(2,1)}, u32[]{:S(2)}, u32[]{:S(2)}) collective-permute-start(bf16[512,512]{1,0:T(8,128)(2,1)} %collective-permute-done.22.c_ref), channel_id=1, source_target_pairs={{0,48},{16,0},{32,16},{48,32},{1,49},{17,1},{33,17},{49,33},{2,50}... | collective-permute-start | bytes 1572872 | tf_op jit(solution)/shard_map/ppermute | solution.py:44
  127.9 8.4 %collective-permute-done.13.c_ref = bf16[512,512]{1,0:T(8,128)(2,1)} collective-permute-done((bf16[512,512]{1,0:T(8,128)(2,1)}, bf16[512,512]{1,0:T(8,128)(2,1)}, u32[]{:S(2)}, u32[]{:S(2)}) %collective-permute-start.13) | collective-permute-done | bytes 524320 | tf_op jit(solution)/shard_map/ppermute | solution.py:44
  136.3 10.7 %frames.2.f_ref.rest_0_ = bf16[1024,2176]{1,0:T(8,128)(2,1)} custom-call(s32[4]{0:T(128)} %get-tuple-element.44.idx_ref, bf16[512,512]{1,0:T(8,128)(2,1)} %attend.2.a_ref, bf16[512,512]{1,0:T(8,128)(2,1)} %collective-permute-done.12.b_ref, bf16[512,512]{1,0:T(8,128)(2,1)} %collective-permute-done.13.c_ref, bf16[512,512]{1,0:T(8,128)(2,1)} %collective-permute-done.14.d_ref, ...), custom_call_target="tpu_custom_call" | custom-call | flops 4563402752 | bytes 13631488 | tf_op jit(solution)/shard_map/frames/pallas_call | solution.py:134
  147.1 7.7 %hidden.2 = (bf16[1024,1024]{1,0:T(8,128)(2,1)}, f32[8,1024]{1,0:T(8,128)}) custom-call(s32[1]{0:T(128)} %dynamic_slice.12.len_ref, bf16[1024,2176]{1,0:T(8,128)(2,1)} %frames.2.f_ref.rest_0_, bf16[2176,1024]{1,0:T(8,128)(2,1)} %assemble.1.rest_0_.w_ref), custom_call_target="tpu_custom_call" | custom-call | flops 2281701376 | bytes 6291456 | tf_op jit(solution)/shard_map/hidden/pallas_call | solution.py:198
  154.8 10.8 %frames.3.f_ref = bf16[1024,2176]{1,0:T(8,128)(2,1)} custom-call(s32[4]{0:T(128)} %get-tuple-element.44.idx_ref, bf16[512,512]{1,0:T(8,128)(2,1)} %attend.3.a_ref, bf16[512,512]{1,0:T(8,128)(2,1)} %collective-permute-done.21.b_ref, bf16[512,512]{1,0:T(8,128)(2,1)} %collective-permute-done.22.c_ref, ...), custom_call_target="tpu_custom_call", output_to_operand_aliasing={{}: (7, {})} | custom-call | flops 4563402752 | bytes 13631488 | tf_op jit(solution)/shard_map/frames/pallas_call | solution.py:134
  165.5 7.7 %hidden.3 = (bf16[1024,1024]{1,0:T(8,128)(2,1)}, f32[8,1024]{1,0:T(8,128)}) custom-call(s32[1]{0:T(128)} %dynamic_slice.12.len_ref, bf16[1024,2176]{1,0:T(8,128)(2,1)} %frames.3.f_ref, bf16[2176,1024]{1,0:T(8,128)(2,1)} %assemble.1.rest_0_.w_ref, bf16[1024,1024]{1,0:T(8,128)(2,1)} %get-tuple-element.13.rest_0_), custom_call_target="tpu_custom_call", output_to_operand_aliasing={{0}: (3, {})} | custom-call | flops 2281701376 | bytes 6291456 | tf_op jit(solution)/shard_map/hidden/pallas_call | solution.py:198
  173.3 9.4 %grad.1 = (bf16[8,2,136,512]{3,2,1,0:T(8,128)(2,1)}, bf16[8,2,136,512]{3,2,1,0:T(8,128)(2,1)}) custom-call(s32[1]{0:T(128)} %bitcast.11.core_ref, bf16[1024,2176]{1,0:T(8,128)(2,1)} %frames.3.f_ref, bf16[1024,1024]{1,0:T(8,128)(2,1)} %get-tuple-element.16.s_ref), custom_call_target="tpu_custom_call" | custom-call | flops 4563402752 | bytes 11534336 | tf_op jit(solution)/shard_map/grad/pallas_call | solution.py:243
  182.7 1.3 collective-permute-start.25
  186.1 1.2 fusion.13
  187.3 9.2 %all_to_all.15 = f32[8,8,256]{2,1,0:T(8,128)} all-to-all(f32[8,8,256]{2,1,0:T(8,128)S(1)} %broadcast_in_dim.8), channel_id=1, replica_groups=mesh['xh'=2,'y'=4,'z'=4,'xl'=2,'c'=2] {'y','c'}, dimensions={0} | all-to-all | bytes 131072 | tf_op jit(solution)/shard_map/all_to_all | solution.py:48
  196.5 2.3 logit.1
  198.8 4.6 %scaled.1 = bf16[8,2,152,512]{3,2,1,0:T(8,128)(2,1)} custom-call(s32[1]{0:T(128)} %bitcast.11.core_ref, bf16[8,2,136,512]{3,2,1,0:T(8,128)(2,1)} %get-tuple-element.17.keep_ref, bf16[8,2,136,512]{3,2,1,0:T(8,128)(2,1)} %collective-permute-done.25.got_ref, f32[2,8,1024]{2,1,0:T(8,128)} %get-tuple-element.19.scale_ref, bf16[8,1024]{1,0:T(8,128)(2,1)} %copy-done.1, ...), custom_call_target="tpu_custom_call" | custom-call | flops 8388608 | bytes 7340032 | tf_op jit(solution)/shard_map/scaled/pallas_call | solution.py:316
  203.4 8.0 %all-to-all-start.2 = ((bf16[16,152,512]{2,1,0:T(8,128)(2,1)}), bf16[16,152,512]{2,1,0:T(8,128)(2,1)S(1)}, u32[]{:S(2)}, u32[]{:S(2)}) async-start(bf16[16,152,512]{2,1,0:T(8,128)(2,1)} %bitcast.33), calls=%async_computation.2 | async-start | bytes 4980736 | tf_op jit(solution)/shard_map/all_to_all | solution.py:48
  211.6 2.9 %collective-permute-start.24 = (f32[1,7]{1,0:T(1,128)S(1)}, f32[1,7]{1,0:T(1,128)S(1)}, u32[]{:S(2)}, u32[]{:S(2)}) collective-permute-start(f32[1,7]{1,0:T(1,128)S(1)} %bitcast.41), channel_id=1, source_target_pairs={{0,64},{64,0},{1,65},{65,1},{2,66},{66,2},{3,67},{67,3},{4,68},{68... | collective-permute-start | bytes 92 | tf_op jit(solution)/shard_map/ppermute | solution.py:44
  214.5 29.8 %collective-permute-done.24 = f32[1,7]{1,0:T(1,128)S(1)} collective-permute-done((f32[1,7]{1,0:T(1,128)S(1)}, f32[1,7]{1,0:T(1,128)S(1)}, u32[]{:S(2)}, u32[]{:S(2)}) %collective-permute-start.24) | collective-permute-done | bytes 60 | tf_op jit(solution)/shard_map/ppermute | solution.py:44
  244.6 2.2 collective-permute-start.26
  247.4 1.0 slice_reduce_fusion
  248.4 1.0 fusion
  (95 shorter events, 11.1 us)
Async XLA Ops:
  0.6 62.3 %collective-permute-start.9 = (bf16[136,512]{1,0:T(8,128)(2,1)}, bf16[136,512]{1,0:T(8,128)(2,1)}, u32[]{:S(2)}, u32[]{:S(2)}) collective-permute-start(bf16[136,512]{1,0:T(8,128)(2,1)} %param.20), channel_id=1, source_target_pairs={{0,64},{2,66},{64,0},{66,2},{1,65},{3,67},{65,1},{67,3},{4,68},{6,... | collective-permute-start | bytes 417800 | tf_op jit(solution)/shard_map/ppermute | solution.py:44
  4.3 58.7 %collective-permute-start.7 = (bf16[136,512]{1,0:T(8,128)(2,1)}, bf16[136,512]{1,0:T(8,128)(2,1)}, u32[]{:S(2)}, u32[]{:S(2)}) collective-permute-start(bf16[136,512]{1,0:T(8,128)(2,1)} %param.20), channel_id=1, source_target_pairs={{0,2},{2,64},{64,66},{66,0},{1,3},{3,65},{65,67},{67,1},{4,6},{6,6... | collective-permute-start | bytes 417800 | tf_op jit(solution)/shard_map/ppermute | solution.py:44
  8.7 5.9 %copy-start.11 = (s32[2]{0:T(128)S(1)}, s32[2]{0:T(128)}, u32[]{:S(2)}) copy-start(s32[2]{0:T(128)} %param.18) | copy-start | bytes 28
  8.7 5.9 %copy-start.10 = (s32[2]{0:T(128)S(1)}, s32[2]{0:T(128)}, u32[]{:S(2)}) copy-start(s32[2]{0:T(128)} %param.25) | copy-start | bytes 28
  8.8 5.9 %copy-start.9 = (f32[2]{0:T(128)S(1)}, f32[2]{0:T(128)}, u32[]{:S(2)}) copy-start(f32[2]{0:T(128)} %param.26) | copy-start | bytes 28
  8.8 6.0 %copy-start.7 = (s32[2,7]{1,0:T(2,128)S(1)}, s32[2,7]{1,0:T(2,128)}, u32[]{:S(2)}) copy-start(s32[2,7]{1,0:T(2,128)} %param.23) | copy-start | bytes 172
  8.8 6.0 %copy-start.8 = (s32[2,7]{1,0:T(2,128)S(1)}, s32[2,7]{1,0:T(2,128)}, u32[]{:S(2)}) copy-start(s32[2,7]{1,0:T(2,128)} %param.24) | copy-start | bytes 172
  8.8 47.2 %copy-start.4 = (bf16[136,512]{1,0:T(8,128)(2,1)S(1)}, bf16[136,512]{1,0:T(8,128)(2,1)}, u32[]{:S(2)}) copy-start(bf16[136,512]{1,0:T(8,128)(2,1)} %param.20) | copy-start | bytes 417796
  8.8 48.9 %copy-start = (bf16[512,256]{1,0:T(8,128)(2,1)S(1)}, bf16[512,256]{1,0:T(8,128)(2,1)}, u32[]{:S(2)}) copy-start(bf16[512,256]{1,0:T(8,128)(2,1)} %param.21) | copy-start | bytes 786436
  8.8 50.5 %copy-start.5 = (f32[7,512]{1,0:T(8,128)S(1)}, f32[7,512]{1,0:T(8,128)}, u32[]{:S(2)}) copy-start(f32[7,512]{1,0:T(8,128)} %param.22) | copy-start | bytes 43012
  8.8 74.9 %all-to-all-start = ((bf16[8,3,128,512]{3,2,1,0:T(8,128)(2,1)}), bf16[8,3,128,512]{3,2,1,0:T(8,128)(2,1)}, u32[]{:S(2)}, u32[]{:S(2)}) async-start(bf16[8,3,128,512]{3,2,1,0:T(8,128)(2,1)} %pack.1), calls=%async_computation | async-start | bytes 6291456 | tf_op jit(solution)/shard_map/all_to_all | solution.py:48
  14.9 2.4 collective-permute-start
  17.3 32.1 %collective-permute-start.1 = (f32[4,24]{1,0:T(4,128)S(1)}, f32[4,24]{1,0:T(4,128)S(1)}, u32[]{:S(2)}, u32[]{:S(2)}) collective-permute-start(f32[4,24]{1,0:T(4,128)S(1)} %pad_maximum_fusion.4), channel_id=1, source_target_pairs={{0,2},{2,0},{1,3},{3,1},{4,6},{6,4},{5,7},{7,5},{8,10},{10,8},{9,1... | collective-permute-start | bytes 1160 | tf_op jit(solution)/shard_map/ppermute | solution.py:44
  49.5 6.4 %collective-permute-start.2 = (f32[8,24]{1,0:T(8,128)S(1)}, f32[8,24]{1,0:T(8,128)S(1)}, u32[]{:S(2)}, u32[]{:S(2)}) collective-permute-start(f32[8,24]{1,0:T(8,128)S(1)} %pad_maximum_fusion.2), channel_id=1, source_target_pairs={{0,4},{4,8},{8,12},{12,0},{1,5},{5,9},{9,13},{13,1},{2,6},{6,10},{... | collective-permute-start | bytes 2312 | tf_op jit(solution)/shard_map/ppermute | solution.py:44
  51.2 6.5 %collective-permute-start.3 = (f32[8,24]{1,0:T(8,128)S(1)}, f32[8,24]{1,0:T(8,128)S(1)}, u32[]{:S(2)}, u32[]{:S(2)}) collective-permute-start(f32[8,24]{1,0:T(8,128)S(1)} %pad_maximum_fusion.2), channel_id=1, source_target_pairs={{0,8},{4,12},{8,0},{12,4},{1,9},{5,13},{9,1},{13,5},{2,10},{6,14},... | collective-permute-start | bytes 2312 | tf_op jit(solution)/shard_map/ppermute | solution.py:44
  54.5 4.9 %collective-permute-start.4 = (f32[8,24]{1,0:T(8,128)S(1)}, f32[8,24]{1,0:T(8,128)S(1)}, u32[]{:S(2)}, u32[]{:S(2)}) collective-permute-start(f32[8,24]{1,0:T(8,128)S(1)} %pad_maximum_fusion.2), channel_id=1, source_target_pairs={{0,12},{4,0},{8,4},{12,8},{1,13},{5,1},{9,5},{13,9},{2,14},{6,2},{... | collective-permute-start | bytes 2312 | tf_op jit(solution)/shard_map/ppermute | solution.py:44
  55.9 7.1 %collective-permute-start.8 = (bf16[136,512]{1,0:T(8,128)(2,1)S(1)}, bf16[136,512]{1,0:T(8,128)(2,1)S(1)}, u32[]{:S(2)}, u32[]{:S(2)}) collective-permute-start(bf16[136,512]{1,0:T(8,128)(2,1)S(1)} %copy-done.4), channel_id=1, source_target_pairs={{0,66},{2,0},{64,2},{66,64},{1,67},{3,1},{65,3},{67,65},{4,70},{6,... | collective-permute-start | bytes 417800 | tf_op jit(solution)/shard_map/ppermute | solution.py:44
  57.7 16.7 %collective-permute-start.5 = (bf16[512,256]{1,0:T(8,128)(2,1)S(1)}, bf16[512,256]{1,0:T(8,128)(2,1)S(1)}, u32[]{:S(2)}, u32[]{:S(2)}) collective-permute-start(bf16[512,256]{1,0:T(8,128)(2,1)S(1)} %copy-done), channel_id=1, source_target_pairs={{0,64},{64,0},{1,65},{65,1},{2,66},{66,2},{3,67},{67,3},{4,68},{68... | collective-permute-start | bytes 786440 | tf_op jit(solution)/shard_map/ppermute | solution.py:44
  59.3 8.2 %collective-permute-start.6 = (f32[7,512]{1,0:T(8,128)S(1)}, f32[7,512]{1,0:T(8,128)S(1)}, u32[]{:S(2)}, u32[]{:S(2)}) collective-permute-start(f32[7,512]{1,0:T(8,128)S(1)} %copy-done.5), channel_id=1, source_target_pairs={{0,64},{64,0},{1,65},{65,1},{2,66},{66,2},{3,67},{67,3},{4,68},{68... | collective-permute-start | bytes 43016 | tf_op jit(solution)/shard_map/ppermute | solution.py:44
  64.9 10.4 %collective-permute-start.10 = (bf16[4,136,512]{2,1,0:T(8,128)(2,1)}, bf16[4,136,512]{2,1,0:T(8,128)(2,1)}, u32[]{:S(2)}, u32[]{:S(2)}) collective-permute-start(bf16[4,136,512]{2,1,0:T(8,128)(2,1)} %pad_maximum_fusion.refs_0_), channel_id=1, source_target_pairs={{0,4},{4,8},{8,12},{12,0},{1,5},{5,9},{9,13},{13,1},{2,6},{6,10},{... | collective-permute-start | bytes 1671176 | tf_op jit(solution)/shard_map/ppermute | solution.py:44
  65.6 18.1 %collective-permute-start.11 = (bf16[4,136,512]{2,1,0:T(8,128)(2,1)}, bf16[4,136,512]{2,1,0:T(8,128)(2,1)}, u32[]{:S(2)}, u32[]{:S(2)}) collective-permute-start(bf16[4,136,512]{2,1,0:T(8,128)(2,1)} %pad_maximum_fusion.refs_0_), channel_id=1, source_target_pairs={{0,12},{4,0},{8,4},{12,8},{1,13},{5,1},{9,5},{13,9},{2,14},{6,2},{... | collective-permute-start | bytes 1671176 | tf_op jit(solution)/shard_map/ppermute | solution.py:44
  67.6 6.8 %copy-start.2 = (f32[7,512]{1,0:T(8,128)}, f32[7,512]{1,0:T(8,128)S(1)}, u32[]{:S(2)}) copy-start(f32[7,512]{1,0:T(8,128)S(1)} %get-tuple-element.37) | copy-start | bytes 43012
  67.6 6.8 %copy-start.3 = (f32[7,512]{1,0:T(8,128)}, f32[7,512]{1,0:T(8,128)S(1)}, u32[]{:S(2)}) copy-start(f32[7,512]{1,0:T(8,128)S(1)} %get-tuple-element.38) | copy-start | bytes 43012
  68.2 43.1 %collective-permute-start.17 = (bf16[4,136,512]{2,1,0:T(8,128)(2,1)}, bf16[4,136,512]{2,1,0:T(8,128)(2,1)}, u32[]{:S(2)}, u32[]{:S(2)}) collective-permute-start(bf16[4,136,512]{2,1,0:T(8,128)(2,1)} %pad_maximum_fusion.refs_0_), channel_id=1, source_target_pairs={{0,1},{1,0},{2,3},{3,2},{4,5},{5,4},{6,7},{7,6},{8,9},{9,8},{10,11... | collective-permute-start | bytes 1671176 | tf_op jit(solution)/shard_map/ppermute | solution.py:44
  77.0 19.7 %collective-permute-start.15 = (bf16[2,136,512]{2,1,0:T(8,128)(2,1)}, bf16[2,136,512]{2,1,0:T(8,128)(2,1)}, u32[]{:S(2)}, u32[]{:S(2)}) collective-permute-start(bf16[2,136,512]{2,1,0:T(8,128)(2,1)} %slice.63), channel_id=1, source_target_pairs={{0,4},{4,8},{8,12},{12,0},{1,5},{5,9},{9,13},{13,1},{2,6},{6,10},{... | collective-permute-start | bytes 835592 | tf_op jit(solution)/shard_map/ppermute | solution.py:44
  77.0 35.9 %collective-permute-start.18 = (bf16[4,136,512]{2,1,0:T(8,128)(2,1)}, bf16[4,136,512]{2,1,0:T(8,128)(2,1)}, u32[]{:S(2)}, u32[]{:S(2)}) collective-permute-start(bf16[4,136,512]{2,1,0:T(8,128)(2,1)} %collective-permute-done.10.rest_4_.refs_1_), channel_id=1, source_target_pairs={{0,1},{1,0},{2,3},{3,2},{4,5},{5,4},{6,7},{7,6},{8,9},{9,8},{10,11... | collective-permute-start | bytes 1671176 | tf_op jit(solution)/shard_map/ppermute | solution.py:44
  92.1 22.2 %collective-permute-start.12 = (bf16[512,512]{1,0:T(8,128)(2,1)}, bf16[512,512]{1,0:T(8,128)(2,1)}, u32[]{:S(2)}, u32[]{:S(2)}) collective-permute-start(bf16[512,512]{1,0:T(8,128)(2,1)} %attend.2.a_ref), channel_id=1, source_target_pairs={{0,16},{16,32},{32,48},{48,0},{1,17},{17,33},{33,49},{49,1},{2,18}... | collective-permute-start | bytes 1572872 | tf_op jit(solution)/shard_map/ppermute | solution.py:44
  94.1 8.3 %collective-permute-start.16 = (bf16[2,136,512]{2,1,0:T(8,128)(2,1)S(1)}, bf16[2,136,512]{2,1,0:T(8,128)(2,1)S(1)}, u32[]{:S(2)}, u32[]{:S(2)}) collective-permute-start(bf16[2,136,512]{2,1,0:T(8,128)(2,1)S(1)} %slice.64), channel_id=1, source_target_pairs={{0,12},{4,0},{8,4},{12,8},{1,13},{5,1},{9,5},{13,9},{2,14},{6,2},{... | collective-permute-start | bytes 835592 | tf_op jit(solution)/shard_map/ppermute | solution.py:44
  96.7 19.0 %collective-permute-start.19 = (bf16[4,136,512]{2,1,0:T(8,128)(2,1)}, bf16[4,136,512]{2,1,0:T(8,128)(2,1)}, u32[]{:S(2)}, u32[]{:S(2)}) collective-permute-start(bf16[4,136,512]{2,1,0:T(8,128)(2,1)} %collective-permute-done.11.rest_5_.refs_2_), channel_id=1, source_target_pairs={{0,1},{1,0},{2,3},{3,2},{4,5},{5,4},{6,7},{7,6},{8,9},{9,8},{10,11... | collective-permute-start | bytes 1671176 | tf_op jit(solution)/shard_map/ppermute | solution.py:44
  103.1 12.5 %collective-permute-start.20 = (bf16[4,136,512]{2,1,0:T(8,128)(2,1)}, bf16[4,136,512]{2,1,0:T(8,128)(2,1)}, u32[]{:S(2)}, u32[]{:S(2)}) collective-permute-start(bf16[4,136,512]{2,1,0:T(8,128)(2,1)} %constant_dynamic-update-slice_fusion.refs_3_), channel_id=1, source_target_pairs={{0,1},{1,0},{2,3},{3,2},{4,5},{5,4},{6,7},{7,6},{8,9},{9,8},{10,11... | collective-permute-start | bytes 1671176 | tf_op jit(solution)/shard_map/ppermute | solution.py:44
  111.3 13.8 %collective-permute-start.22 = (bf16[512,512]{1,0:T(8,128)(2,1)}, bf16[512,512]{1,0:T(8,128)(2,1)}, u32[]{:S(2)}, u32[]{:S(2)}) collective-permute-start(bf16[512,512]{1,0:T(8,128)(2,1)} %attend.3.a_ref), channel_id=1, source_target_pairs={{0,48},{16,0},{32,16},{48,32},{1,49},{17,1},{33,17},{49,33},{2,50}... | collective-permute-start | bytes 1572872 | tf_op jit(solution)/shard_map/ppermute | solution.py:44
  112.9 23.4 %collective-permute-start.13 = (bf16[512,512]{1,0:T(8,128)(2,1)}, bf16[512,512]{1,0:T(8,128)(2,1)}, u32[]{:S(2)}, u32[]{:S(2)}) collective-permute-start(bf16[512,512]{1,0:T(8,128)(2,1)} %attend.2.a_ref), channel_id=1, source_target_pairs={{0,48},{16,0},{32,16},{48,32},{1,49},{17,1},{33,17},{49,33},{2,50}... | collective-permute-start | bytes 1572872 | tf_op jit(solution)/shard_map/ppermute | solution.py:44
  114.3 22.1 %collective-permute-start.14 = (bf16[512,512]{1,0:T(8,128)(2,1)}, bf16[512,512]{1,0:T(8,128)(2,1)}, u32[]{:S(2)}, u32[]{:S(2)}) collective-permute-start(bf16[512,512]{1,0:T(8,128)(2,1)} %collective-permute-done.12.b_ref), channel_id=1, source_target_pairs={{0,16},{16,32},{32,48},{48,0},{1,17},{17,33},{33,49},{49,1},{2,18}... | collective-permute-start | bytes 1572872 | tf_op jit(solution)/shard_map/ppermute | solution.py:44
  121.0 33.8 %collective-permute-start.21 = (bf16[512,512]{1,0:T(8,128)(2,1)}, bf16[512,512]{1,0:T(8,128)(2,1)}, u32[]{:S(2)}, u32[]{:S(2)}) collective-permute-start(bf16[512,512]{1,0:T(8,128)(2,1)} %attend.3.a_ref), channel_id=1, source_target_pairs={{0,16},{16,32},{32,48},{48,0},{1,17},{17,33},{33,49},{49,1},{2,18}... | collective-permute-start | bytes 1572872 | tf_op jit(solution)/shard_map/ppermute | solution.py:44
  125.1 29.7 %collective-permute-start.23 = (bf16[512,512]{1,0:T(8,128)(2,1)}, bf16[512,512]{1,0:T(8,128)(2,1)}, u32[]{:S(2)}, u32[]{:S(2)}) collective-permute-start(bf16[512,512]{1,0:T(8,128)(2,1)} %collective-permute-done.22.c_ref), channel_id=1, source_target_pairs={{0,48},{16,0},{32,16},{48,32},{1,49},{17,1},{33,17},{49,33},{2,50}... | collective-permute-start | bytes 1572872 | tf_op jit(solution)/shard_map/ppermute | solution.py:44
  182.7 16.1 %collective-permute-start.25 = (bf16[8,2,136,512]{3,2,1,0:T(8,128)(2,1)}, bf16[8,2,136,512]{3,2,1,0:T(8,128)(2,1)}, u32[]{:S(2)}, u32[]{:S(2)}) collective-permute-start(bf16[8,2,136,512]{3,2,1,0:T(8,128)(2,1)} %get-tuple-element.18), channel_id=1, source_target_pairs={{0,1},{1,0},{2,3},{3,2},{4,5},{5,4},{6,7},{7,6},{8,9},{9,8},{10,11... | collective-permute-start | bytes 6684680 | tf_op jit(solution)/shard_map/ppermute | solution.py:44
  185.5 0.6 copy-start.1
  203.4 8.0 %copy-start.6 = (f32[2,8,128]{2,1,0:T(8,128)S(1)}, f32[2,8,128]{2,1,0:T(8,128)}, u32[]{:S(2)}) copy-start(f32[2,8,128]{2,1,0:T(8,128)} %get-tuple-element.15) | copy-start | bytes 24580
  203.4 41.0 %all-to-all-start.2 = ((bf16[16,152,512]{2,1,0:T(8,128)(2,1)}), bf16[16,152,512]{2,1,0:T(8,128)(2,1)S(1)}, u32[]{:S(2)}, u32[]{:S(2)}) async-start(bf16[16,152,512]{2,1,0:T(8,128)(2,1)} %bitcast.33), calls=%async_computation.2 | async-start | bytes 4980736 | tf_op jit(solution)/shard_map/all_to_all | solution.py:48
  211.6 32.8 %collective-permute-start.24 = (f32[1,7]{1,0:T(1,128)S(1)}, f32[1,7]{1,0:T(1,128)S(1)}, u32[]{:S(2)}, u32[]{:S(2)}) collective-permute-start(f32[1,7]{1,0:T(1,128)S(1)} %bitcast.41), channel_id=1, source_target_pairs={{0,64},{64,0},{1,65},{65,1},{2,66},{66,2},{3,67},{67,3},{4,68},{68... | collective-permute-start | bytes 92 | tf_op jit(solution)/shard_map/ppermute | solution.py:44
  244.6 3.8 %collective-permute-start.26 = (bf16[16,16,512]{2,0,1:T(8,128)(2,1)S(1)}, bf16[16,16,512]{2,0,1:T(8,128)(2,1)S(1)}, u32[]{:S(2)}, u32[]{:S(2)}) collective-permute-start(bf16[16,16,512]{2,0,1:T(8,128)(2,1)S(1)} %copy.49), channel_id=1, source_target_pairs={{0,1},{1,0},{2,3},{3,2},{4,5},{5,4},{6,7},{7,6},{8,9},{9,8},{10,11... | collective-permute-start | bytes 786440 | tf_op jit(solution)/shard_map/ppermute | solution.py:44
where the time goes:
time: 251 us; the launch traced here: 249 us
  waiting for transfers between devices  77 us (31%)
  Pallas kernels  76.8 us (31%)
  starting transfers between devices  64.2 us (26%)
  other arithmetic  9.35 us (4%)
  blocking collectives  9.25 us (4%)
  local copies, waits for them, and re-layouts  8.29 us (3%)
    ppermute x27, waiting for transfers between devices, shifted(): return lax.ppermute(x, axis, [(i, (i + by) % count) for i in range(count)])  77 us
    ppermute x27, starting transfers between devices, shifted(): return lax.ppermute(x, axis, [(i, (i + by) % count) for i in range(count)])  50.4 us
    pallas_call x2, Pallas kernels, frames_of(): pl.pallas_call(frames_kernel, out_shape=jax.ShapeDtypeStruct((SEQ, VIS),...  21.5 us
    pallas_call x2, Pallas kernels, hidden_of(): pl.pallas_call(functools.partial(hidden_kernel, chunk), out_shape=(jax.Sh...  15.4 us
    pallas_call x2, Pallas kernels, attend(): pl.pallas_call(attend_kernel, out_shape=jax.ShapeDtypeStruct((CH, COLS),...  14 us
    all_to_all x2, starting transfers between devices, dealt(): return lax.all_to_all(x, axes, 0, 0, tiled=True)  13.8 us
    pallas_call x1, Pallas kernels, grad_of(): pl.pallas_call(grad_kernel, out_shape=(out, out), grid_spec=pltpu.Prefetc...  9.43 us
    all_to_all x1, blocking collectives, dealt(): return lax.all_to_all(x, axes, 0, 0, tiled=True)  9.25 us
  transfers between devices with their start and end apart: 29, of which 6 were waited for; matrix products, arithmetic and copies ran while one was open for 7% of the time, Pallas kernels for 18%

commit v1 on v0

--- a/solution.py
+++ b/solution.py
@@ -110,8 +110,8 @@
     )(length, got, got, got, *after)
 
 
-def frames_kernel(idx_ref, a_ref, b_ref, c_ref, d_ref, fm_ref, last_ref, *rest):
-    o_ref, full = rest[-2:]
+def chunk_kernel(chunk, idx_ref, len_ref, a_ref, b_ref, c_ref, d_ref, fm_ref, last_ref, w_ref, *rest):
+    o_ref, slope_ref, pool_ref, full = rest[-4:]
     step = pl.program_id(0)
 
     @pl.when(step == 0)
@@ -119,50 +119,79 @@
         for i, ref in enumerate((a_ref, b_ref, c_ref, d_ref)):
             full[:, pl.ds(pl.multiple_of(idx_ref[i] * COLS, COLS), COLS)] = ref[...]
 
-    term = jnp.dot(full[...], fm_ref[...], preferred_element_type=F32)
-    o_ref[:, pl.ds(pl.multiple_of(step * 512, 512), 512)] = term.astype(BF16)
+    @pl.when(step < 4)
+    def _():
+        term = jnp.dot(full[...], fm_ref[...], preferred_element_type=F32)
+        o_ref[:, pl.ds(pl.multiple_of(step * 512, 512), 512)] = term.astype(BF16)
 
     @pl.when(step == 3)
     def _():
         term = jnp.dot(full[...], last_ref[...], preferred_element_type=F32)
         o_ref[:, 2048:] = term.astype(BF16)
 
-
-def frames_of(idx, pieces, frame_map, chunk, before, after=()):
-    whole = pl.BlockSpec((CH, COLS), lambda k, n: (0, 0))
-    more = [] if before is None else [before]
-    return pl.pallas_call(
-        frames_kernel,
-        out_shape=jax.ShapeDtypeStruct((SEQ, VIS), BF16),
+    @pl.when(step >= 4)
+    def _():
+        total = jnp.zeros((1, slope_ref.shape[1]), F32)
+        for r in range(CH // 256):
+            rows = slice(r * 256, (r + 1) * 256)
+            t = jnp.dot(o_ref[rows, :], w_ref[...], preferred_element_type=F32)
+            cdf = 0.5 * (1.0 + lax.erf(t * SQRT_HALF))
+            at = lax.broadcasted_iota(jnp.int32, (256, 1), 0) + (chunk * CH + r * 256)
+            live = (at < len_ref[0]).astype(F32)
+            slope = cdf + t * jnp.exp(-0.5 * t * t) * INV_ROOT_TAU
+            slope_ref[rows, :] = (live * slope).astype(BF16)
+            total = total + jnp.sum(live * (t * cdf), axis=0, keepdims=True)
+        pool_ref[...] = jnp.broadcast_to(total, pool_ref.shape)
+
+
+def chunk_of(idx, length, pieces, frame_map, weight, chunk, before):
+    tile = 256
+    whole = pl.BlockSpec((CH, COLS), lambda k, n, m: (0, 0))
+
+    def late(k):
+        return jnp.maximum(k - 4, 0)
+
+    return pl.pallas_call(
+        functools.partial(chunk_kernel, chunk),
+        out_shape=(
+            jax.ShapeDtypeStruct((SEQ, VIS), BF16),
+            jax.ShapeDtypeStruct((SEQ, HID_HERE), BF16),
+            jax.ShapeDtypeStruct((8, HID_HERE), F32),
+        ),
         grid_spec=pltpu.PrefetchScalarGridSpec(
-            num_scalar_prefetch=1,
-            grid=(4,),
+            num_scalar_prefetch=2,
+            grid=(4 + HID_HERE // tile,),
             in_specs=[whole] * 4
             + [
-                pl.BlockSpec((ATT, 512), lambda k, n: (0, k)),
-                pl.BlockSpec((ATT, 128), lambda k, n: (0, 16)),
+                pl.BlockSpec((ATT, 512), lambda k, n, m: (0, jnp.minimum(k, 3))),
+                pl.BlockSpec((ATT, 128), lambda k, n, m: (0, 16)),
+                pl.BlockSpec((VIS, tile), lambda k, n, m: (0, late(k))),
             ]
-            + [pl.BlockSpec(memory_space=pl.ANY)] * (len(more) + len(after)),
-            out_specs=pl.BlockSpec((CH, VIS), lambda k, n: (chunk, 0)),
+            + [pl.BlockSpec(memory_space=pl.ANY)] * len(before),
+            out_specs=(
+                pl.BlockSpec((CH, VIS), lambda k, n, m: (chunk, 0)),
+                pl.BlockSpec((CH, tile), lambda k, n, m: (chunk, late(k))),
+                pl.BlockSpec((8, tile), lambda k, n, m: (0, late(k))),
+            ),
             scratch_shapes=[pltpu.VMEM((CH, ATT), BF16)],
         ),
-        input_output_aliases={} if before is None else {7: 0},
+        input_output_aliases={9: 0, 10: 1} if before else {},
         compiler_params=params(),
-        cost_estimate=cost(2 * CH * ATT * VIS, 13 << 20),
-        name="frames",
-    )(idx, *pieces, frame_map, frame_map, *more, *after)
+        cost_estimate=cost(2 * CH * VIS * (ATT + HID_HERE), 20 << 20, 2 * CH * HID_HERE),
+        name="chunk",
+    )(idx, length, *pieces, frame_map, frame_map, weight, *before)
 
 
 def assemble_kernel(z_ref, x_ref, core_ref, *refs):
     o_ref = refs[-1]
     lead = core_ref[0] == 0
     for k in range(4):
+        x = x_ref[k]
+        col = pl.multiple_of((x // 2) * COLS, COLS)
         for i in range(4):
             mine, other = refs[k][i].astype(F32), refs[4 + k][i].astype(F32)
             pair = [jnp.where(lead, mine, other), jnp.where(lead, other, mine)]
-            x = x_ref[i]
-            row = pl.multiple_of((z_ref[k] * 2 + x % 2) * 2 * ROWS, 2 * ROWS)
-            col = pl.multiple_of((x // 2) * COLS, COLS)
+            row = pl.multiple_of((z_ref[i] * 2 + x % 2) * 2 * ROWS, 2 * ROWS)
             o_ref[pl.ds(row, 2 * ROWS), pl.ds(col, COLS)] = jnp.concatenate(pair, axis=0).astype(
                 BF16
             )
@@ -178,47 +207,6 @@
         cost_estimate=cost(1 << 20, 9 << 20),
         name="assemble",
     )(z_order, x_order, core, *own, *other)
-
-
-def hidden_kernel(chunk, len_ref, f_ref, w_ref, *rest):
-    slope_ref, pool_ref = rest[-2:]
-    t = jnp.dot(f_ref[...], w_ref[...], preferred_element_type=F32)
-    cdf = 0.5 * (1.0 + lax.erf(t * SQRT_HALF))
-    at = lax.broadcasted_iota(jnp.int32, t.shape, 0) + chunk * CH
-    live = at < len_ref[0]
-    slope = cdf + t * jnp.exp(-0.5 * t * t) * INV_ROOT_TAU
-    slope_ref[...] = jnp.where(live, slope, 0.0).astype(BF16)
-    part = jnp.sum(jnp.where(live, t * cdf, 0.0), axis=0, keepdims=True)
-    pool_ref[...] = jnp.broadcast_to(part, pool_ref.shape)
-
-
-def hidden_of(length, frames, weight, chunk, before):
-    tile = 256
-    more = [] if before is None else [before]
-    return pl.pallas_call(
-        functools.partial(hidden_kernel, chunk),
-        out_shape=(
-            jax.ShapeDtypeStruct((SEQ, HID_HERE), BF16),
-            jax.ShapeDtypeStruct((8, HID_HERE), F32),
-        ),
-        grid_spec=pltpu.PrefetchScalarGridSpec(
-            num_scalar_prefetch=1,
-            grid=(HID_HERE // tile,),
-            in_specs=[
-                pl.BlockSpec((CH, VIS), lambda j, n: (chunk, 0)),
-                pl.BlockSpec((VIS, tile), lambda j, n: (0, j)),
-            ]
-            + [pl.BlockSpec(memory_space=pl.ANY)] * len(more),
-            out_specs=(
-                pl.BlockSpec((CH, tile), lambda j, n: (chunk, j)),
-                pl.BlockSpec((8, tile), lambda j, n: (0, j)),
-            ),
-        ),
-        input_output_aliases={} if before is None else {3: 0},
-        compiler_params=params(),
-        cost_estimate=cost(2 * CH * HID_HERE * VIS, 6 << 20, 2 * CH * HID_HERE),
-        name="hidden",
-    )(length, frames, weight, *more)
 
 
 def grad_kernel(core_ref, f_ref, s_ref, keep_ref, send_ref, total):
@@ -259,26 +247,52 @@
     )(core, frames, slope)
 
 
-def logit_kernel(part_ref, act_ref, weight_ref, inv_ref, hw_ref, lp_ref, lg_ref, scale_ref):
-    logits = (part_ref[0] + part_ref[1]) + (part_ref[2] + part_ref[3])
-    top = jnp.max(logits, axis=-1, keepdims=True)
-    down = logits - top
-    log_all = down - jnp.log(jnp.sum(jnp.exp(down), axis=-1, keepdims=True))
-    at = lax.broadcasted_iota(jnp.int32, logits.shape, 2)
-    picked = (at == act_ref[...]).astype(F32)
-    lp = jnp.sum(picked * log_all, axis=-1, keepdims=True)
-    lp_ref[...] = jnp.broadcast_to(lp, lp_ref.shape)
-    grad = (weight_ref[...] * (picked - jnp.exp(log_all))).astype(BF16)
-    lg_ref[...] = grad
+def logit_kernel(at_ref, part_ref, fact_ref, hw_ref, lp_ref, lg_ref, scale_ref):
+    facts = fact_ref[...]
+    lane = lax.broadcasted_iota(jnp.int32, (1, 128), 1)
+    line = lane.astype(F32)
+
+    def column(rows, i):
+        return jnp.sum(jnp.where(lane == i, rows, 0.0), axis=1, keepdims=True)
+
+    gains, groups = column(facts, 0), column(facts, 1)
+    member = (groups == line).astype(F32)
+    sums = jnp.sum(member * gains, axis=0, keepdims=True)
+    squares = jnp.sum(member * (gains * gains), axis=0, keepdims=True)
+    sizes = jnp.maximum(jnp.sum(member, axis=0, keepdims=True), 1.0)
+    mean = sums / sizes
+    spread = jnp.sqrt(jnp.maximum(squares / sizes - mean * mean, 1.0))
+    masks = jnp.where((lane >= 16) & (lane < 24), facts, 0.0)
+    count = jnp.maximum(jnp.sum(jnp.sum(masks, axis=1, keepdims=True), axis=0, keepdims=True), 1.0)
+    action = lax.broadcasted_iota(jnp.int32, (8, 128), 0)
+    bins = lax.broadcasted_iota(jnp.int32, (8, NBINS), 1).astype(F32)
     for c in range(2):
+        here = fact_ref[pl.ds(at_ref[c], 1), :]
+        own = (column(here, 1) == line).astype(F32)
+        advantage = (column(here, 0) - jnp.sum(own * mean, axis=1, keepdims=True)) / jnp.sum(
+            own * spread, axis=1, keepdims=True
+        )
+        rows = jnp.broadcast_to(here, (8, 128))
+        act = jnp.sum(jnp.where(lane == action + 8, rows, 0.0), axis=1, keepdims=True)
+        mask = jnp.sum(jnp.where(lane == action + 16, rows, 0.0), axis=1, keepdims=True)
+        weight = -mask * advantage / count
+
+        logits = (part_ref[0, c] + part_ref[1, c]) + (part_ref[2, c] + part_ref[3, c])
+        down = logits - jnp.max(logits, axis=-1, keepdims=True)
+        log_all = down - jnp.log(jnp.sum(jnp.exp(down), axis=-1, keepdims=True))
+        picked = (bins == act).astype(F32)
+        lp = jnp.sum(picked * log_all, axis=-1, keepdims=True)
+        lp_ref[c] = jnp.broadcast_to(lp, lp_ref.shape[1:])
+        grad = (weight * (picked - jnp.exp(log_all))).astype(BF16)
+        lg_ref[c] = grad
         back = lax.dot_general(
-            grad[c], hw_ref[...], (((1,), (1,)), ((), ())), preferred_element_type=F32
+            grad, hw_ref[...], (((1,), (1,)), ((), ())), preferred_element_type=F32
         )
-        pool = jnp.sum(back, axis=0, keepdims=True) * inv_ref[c]
+        pool = jnp.sum(back, axis=0, keepdims=True) / column(here, 2)
         scale_ref[c] = jnp.broadcast_to(pool, scale_ref.shape[1:])
 
 
-def logit_parts(parts, acts, weights, inv, hw):
+def logit_parts(at, parts, facts, hw):
     return pl.pallas_call(
         logit_kernel,
         out_shape=(
@@ -286,12 +300,12 @@
             jax.ShapeDtypeStruct((2, 8, NBINS), BF16),
             jax.ShapeDtypeStruct((2, 8, HID_HERE), F32),
         ),
-        in_specs=[pl.BlockSpec(memory_space=pltpu.VMEM)] * 3
-        + [pl.BlockSpec(memory_space=pltpu.SMEM), pl.BlockSpec(memory_space=pltpu.VMEM)],
+        in_specs=[pl.BlockSpec(memory_space=pltpu.SMEM)]
+        + [pl.BlockSpec(memory_space=pltpu.VMEM)] * 3,
         compiler_params=pltpu.CompilerParams(vmem_limit_bytes=VMEM_LIMIT),
         cost_estimate=cost(8 << 20, 1 << 20, 8192),
         name="logit",
-    )(parts, acts, weights, inv, hw)
+    )(at, parts, facts, hw)
 
 
 def scale_kernel(core_ref, keep_ref, got_ref, scale_ref, head_ref, lg_ref, o_ref):
@@ -340,26 +354,10 @@
         [
             jnp.pad(three, ((0, 0), (0, 5))),
             jnp.pad(actions.astype(F32), ((0, 0), (0, 1))),
-            jnp.pad(action_mask.astype(F32), ((0, 0), (0, 1))),
+            jnp.pad(action_mask.astype(F32), ((0, 0), (0, 105))),
         ],
         axis=1,
     )
-
-
-def loss_terms(every, here):
-    gains, groups, masks = every[:, 0], every[:, 1], every[:, 16:24]
-    member = (groups[:, None] == jnp.arange(4, dtype=F32)[None, :]).astype(F32)
-    sums = jnp.sum(member * gains[:, None], axis=0)
-    squares = jnp.sum(member * (gains * gains)[:, None], axis=0)
-    sizes = jnp.maximum(jnp.sum(member, axis=0), 1.0)
-    mean = sums / sizes
-    spread = jnp.sqrt(jnp.maximum(squares / sizes - mean * mean, 1.0))
-    count = jnp.maximum(jnp.sum(masks), 1.0)
-    own = (here[:, 1:2] == jnp.arange(4, dtype=F32)[None, :]).astype(F32)
-    advantage = (here[:, 0] - jnp.sum(own * mean[None, :], axis=1)) / jnp.sum(
-        own * spread[None, :], axis=1
-    )
-    return -here[:, 16:24] * advantage[:, None] / count, here[:, 8:16], 1.0 / here[:, 2]
 
 
 def per_device(
@@ -388,12 +386,12 @@
 
     x = xh * 2 + xl
     line = ("xh", "xl")
-    row = [proj_weight] + [shifted(proj_weight, line, by) for by in (1, -1, 2)]
+    row = [proj_weight] + [shifted(proj_weight, "z", by) for by in (1, -1, 2)]
+    z_order = (z + jnp.array([0, 3, 1, 2], jnp.int32)) % 4
+    block = jnp.stack(row)
+    up, down = shifted(block, line, 1), shifted(block, line, -1)
+    half = jnp.concatenate([shifted(up[:2], line, 1), shifted(down[2:], line, -1)])
     x_order = (x + jnp.array([0, 3, 1, 2], jnp.int32)) % 4
-    block = jnp.stack(row)
-    up, down = shifted(block, "z", 1), shifted(block, "z", -1)
-    half = jnp.concatenate([shifted(up[:2], "z", 1), shifted(down[2:], "z", -1)])
-    z_order = (z + jnp.array([0, 3, 1, 2], jnp.int32)) % 4
     own = (block, up, down, half)
     other = [shifted(w, "c", 1) for w in own]
     weight = assemble(z_order, x_order, core1, own, other)
@@ -410,17 +408,12 @@
     embed = jnp.pad(both(act_embed, ae_other, 1), ((0, 1), (0, 0)))
 
     facts = episode_facts(lengths, actions, action_mask, group_ids, rewards)
-    facts = jnp.concatenate([facts, shifted(facts, "c", 1)])
-    pair = lax.dynamic_slice(facts.reshape(2, 2, 24), (0, xh, 0), (2, 1, 24)).reshape(2, 24)
-    pair = jnp.where(core == 0, pair, pair[::-1])
-    facts = jnp.concatenate([facts, shifted(facts, "xl", 1)])
-    facts = jnp.concatenate([facts] + [shifted(facts, "z", by) for by in (1, 2, 3)])
-    loss_weight, acts, inverse = loss_terms(facts, pair)
-    wide_weight = jnp.broadcast_to(loss_weight[:, :, None], (2, 8, NBINS))
-    wide_acts = jnp.broadcast_to(acts[:, :, None], (2, 8, NBINS)).astype(jnp.int32)
+    facts = jnp.broadcast_to(facts[None], (16, 2, 128))
+    facts = dealt(facts, ("z", "xl", "c"))
+    places = (z * 2 + xl) * 4 + xh + 2 * jnp.arange(2, dtype=jnp.int32)
 
     idx = (y + jnp.array([0, 3, 1, 2], jnp.int32)) % 4
-    a0 = attend(got, length, 0, (wide_weight, wide_acts, hw, embed, up, down))
+    a0 = attend(got, length, 0, ())
     a1 = attend(got, length, 1, ())
     b0 = shifted(a0, "y", 1)
     c0 = shifted(a0, "y", -1)
@@ -429,10 +422,10 @@
     d0 = shifted(b0, "y", 1)
     d1 = shifted(c1, "y", -1)
 
-    frames = frames_of(idx, (a0, b0, c0, d0), frame_map, 0, None, (weight,))
-    slope, pool0 = hidden_of(length, frames, weight, 0, None)
-    frames = frames_of(idx, (a1, b1, c1, d1), frame_map, 1, frames)
-    slope, pool1 = hidden_of(length, frames, weight, 1, slope)
+    *done, pool0 = chunk_of(idx, length, (a0, b0, c0, d0), frame_map, weight, 0, ())
+    frames, slope, pool1 = chunk_of(
+        idx, length, (a1, b1, c1, d1), frame_map, weight, 1, tuple(done)
+    )
     pooled = (pool0 + pool1) / length.astype(F32)
     head_input = (pooled + embed).astype(BF16)
     part = jnp.dot(head_input, hw, preferred_element_type=F32)
@@ -441,7 +434,7 @@
     arrived = shifted(send, "c", 1)
 
     logprob, lgrad, scale = logit_parts(
-        parts.reshape(4, 2, 8, NBINS), wide_acts, wide_weight, inverse, hw
+        places, parts.reshape(4, 2, 8, NBINS), facts.reshape(32, 128), hw
     )
     summed = scaled(core1, keep, arrived, scale, head_input, lgrad)
     dealt_out = dealt(summed.reshape(16, ROWS + 16, COLS), ("z", "xl", "xh"))

time: 251 us -> 243 us (0.968)
  waiting for transfers between devices: 77 us -> 91.2 us
  blocking collectives: 9.25 us -> 0 us
  starting transfers between devices: 64.2 us -> 56.1 us
  Pallas kernels: 76.8 us -> 73.2 us
    ppermute x27 -> x22, starting transfers between devices: 50.4 us -> 31.3 us  [shifted(): return lax.ppermute(x, axis, [(i, (i + by) % count) for i in range(count)])]
    all_to_all x2 -> x4, starting transfers between devices: 13.8 us -> 24.8 us  [dealt(): return lax.all_to_all(x, axes, 0, 0, tiled=True)]
    all_to_all x1 -> x0, blocking collectives: 9.25 us -> none  [dealt(): return lax.all_to_all(x, axes, 0, 0, tiled=True)]
    ppermute x27 -> x22, waiting for transfers between devices: 77 us -> 84.9 us  [shifted(): return lax.ppermute(x, axis, [(i, (i + by) % count) for i in range(count)])]
    all_to_all x2 -> x4, waiting for transfers between devices: 0.01 us -> 6.25 us  [dealt(): return lax.all_to_all(x, axes, 0, 0, tiled=True)]
    pallas_call x4 -> x2, Pallas kernels: 36.9 us -> 33.3 us  [chunk_of(): pl.pallas_call(functools.partial(chunk_kernel, chunk), out_shape=(jax.Sha...]
  transfers between devices with their start and end apart: 29 -> 26, of which waited for: 6 -> 9; matrix products, arithmetic and copies ran while one was open for 7% -> 7% of each run, Pallas kernels for 18% -> 16%
where the time goes in v1:
time: 243 us; the launch traced here: 241 us
  waiting for transfers between devices  91.2 us (38%)
  Pallas kernels  73.2 us (30%)
  starting transfers between devices  56.1 us (23%)
  other arithmetic  10.2 us (4%)
  local copies, waits for them, and re-layouts  7.96 us (3%)
    ppermute x22, waiting for transfers between devices, shifted(): return lax.ppermute(x, axis, [(i, (i + by) % count) for i in range(count)])  84.9 us
    pallas_call x2, Pallas kernels, chunk_of(): pl.pallas_call(functools.partial(chunk_kernel, chunk), out_shape=(jax.Sha...  33.3 us
    ppermute x22, starting transfers between devices, shifted(): return lax.ppermute(x, axis, [(i, (i + by) % count) for i in range(count)])  31.3 us
    all_to_all x4, starting transfers between devices, dealt(): return lax.all_to_all(x, axes, 0, 0, tiled=True)  24.8 us
    pallas_call x2, Pallas kernels, attend(): pl.pallas_call(attend_kernel, out_shape=jax.ShapeDtypeStruct((CH, COLS),...  14 us
    pallas_call x1, Pallas kernels, grad_of(): pl.pallas_call(grad_kernel, out_shape=(out, out), grid_spec=pltpu.Prefetc...  9.49 us
    all_to_all x4, waiting for transfers between devices, dealt(): return lax.all_to_all(x, axes, 0, 0, tiled=True)  6.25 us
    pallas_call x1, Pallas kernels, assemble(): pl.pallas_call(assemble_kernel, out_shape=jax.ShapeDtypeStruct((VIS, HID_...  5.35 us
  transfers between devices with their start and end apart: 26, of which 9 were waited for; matrix products, arithmetic and copies ran while one was open for 7% of the time, Pallas kernels for 16%

profile of v1, /device:TPU:1, one launch (start us, length us, event | category | flops | bytes accessed | tf_op | source)
XLA Modules:
  0.0 241.2 jit_solution(712896320302139193)
XLA Ops:
  0.6 4.2 %pack.1 = bf16[8,3,128,512]{3,2,1,0:T(8,128)(2,1)} custom-call(bf16[2,128,2048]{2,1,0:T(8,128)(2,1)} %q_ref.1, bf16[2,128,2048]{2,1,0:T(8,128)(2,1)} %k_ref.1, bf16[2,128,2048]{2,1,0:T(8,128)(2,1)} %v_ref.1), custom_call_target="tpu_custom_call" | custom-call | bytes 6291456 | tf_op jit(solution)/shard_map/pack/pallas_call | solution.py:59
  4.8 7.6 %all-to-all-start = ((bf16[8,3,128,512]{3,2,1,0:T(8,128)(2,1)}), bf16[8,3,128,512]{3,2,1,0:T(8,128)(2,1)}, u32[]{:S(2)}, u32[]{:S(2)}) async-start(bf16[8,3,128,512]{3,2,1,0:T(8,128)(2,1)} %pack.1), calls=%async_computation | async-start | bytes 6291456 | tf_op jit(solution)/shard_map/all_to_all | solution.py:48
  12.4 1.7 collective-permute-start.3
  14.1 2.2 collective-permute-start.4
  16.3 1.2 collective-permute-start.5
  17.6 1.9 collective-permute-done.3
  19.5 4.2 %collective-permute-done.5 = bf16[136,512]{1,0:T(8,128)(2,1)S(1)} collective-permute-done((bf16[136,512]{1,0:T(8,128)(2,1)S(1)}, bf16[136,512]{1,0:T(8,128)(2,1)S(1)}, u32[]{:S(2)}, u32[]{:S(2)}) %collective-permute-start.5) | collective-permute-done | bytes 139296 | tf_op jit(solution)/shard_map/ppermute | solution.py:44
  23.6 0.9 pad_maximum_fusion.refs_0_
  24.8 2.4 collective-permute-start.7
  27.8 2.0 collective-permute-start.10
  29.8 32.7 %collective-permute-done.6.refs_1_ = bf16[4,136,512]{2,1,0:T(8,128)(2,1)} collective-permute-done((bf16[4,136,512]{2,1,0:T(8,128)(2,1)}, bf16[4,136,512]{2,1,0:T(8,128)(2,1)}, u32[]{:S(2)}, u32[]{:S(2)}) %collective-permute-start.6) | collective-permute-done | bytes 557088 | tf_op jit(solution)/shard_map/ppermute | solution.py:44
  62.5 1.7 slice.28
  64.7 7.0 %attend.2.a_ref = bf16[512,512]{1,0:T(8,128)(2,1)} custom-call(s32[1]{0:T(128)} %dynamic_slice.9.len_ref, bf16[8,3,128,512]{3,2,1,0:T(8,128)(2,1)} %all-to-all-done.q_ref.k_ref.v_ref, bf16[8,3,128,512]{3,2,1,0:T(8,128)(2,1)} %all-to-all-done.q_ref.k_ref.v_ref, bf16[8,3,128,512]{3,2,1,0:T(8,128)(2,1)} %all-to-all-done.q_ref.k_ref.v_ref), custom_call_target="tpu_custom_call" | custom-call | flops 1073741824 | bytes 3145728 | tf_op jit(solution)/shard_map/attend/pallas_call | solution.py:97
  71.7 1.2 collective-permute-start
  72.9 1.0 slice.29
  73.9 3.0 %collective-permute-start.9 = (bf16[2,136,512]{2,1,0:T(8,128)(2,1)S(1)}, bf16[2,136,512]{2,1,0:T(8,128)(2,1)S(1)}, u32[]{:S(2)}, u32[]{:S(2)}) collective-permute-start(bf16[2,136,512]{2,1,0:T(8,128)(2,1)S(1)} %slice.29), channel_id=1, source_target_pairs={{0,66},{2,0},{64,2},{66,64},{1,67},{3,1},{65,3},{67,65},{4,70},{6,... | collective-permute-start | bytes 835592 | tf_op jit(solution)/shard_map/ppermute | solution.py:44
  77.5 1.7 constant_dynamic-update-slice_fusion.1
  79.2 3.5 %collective-permute-done.9 = bf16[2,136,512]{2,1,0:T(8,128)(2,1)S(1)} collective-permute-done((bf16[2,136,512]{2,1,0:T(8,128)(2,1)S(1)}, bf16[2,136,512]{2,1,0:T(8,128)(2,1)S(1)}, u32[]{:S(2)}, u32[]{:S(2)}) %collective-permute-start.9) | collective-permute-done | bytes 278560 | tf_op jit(solution)/shard_map/ppermute | solution.py:44
  83.4 1.1 collective-permute-start.13
  84.5 7.0 %attend.3.a_ref = bf16[512,512]{1,0:T(8,128)(2,1)} custom-call(s32[1]{0:T(128)} %dynamic_slice.9.len_ref, bf16[8,3,128,512]{3,2,1,0:T(8,128)(2,1)} %all-to-all-done.q_ref.k_ref.v_ref, bf16[8,3,128,512]{3,2,1,0:T(8,128)(2,1)} %all-to-all-done.q_ref.k_ref.v_ref, bf16[8,3,128,512]{3,2,1,0:T(8,128)(2,1)} %all-to-all-done.q_ref.k_ref.v_ref), custom_call_target="tpu_custom_call" | custom-call | flops 1073741824 | bytes 3145728 | tf_op jit(solution)/shard_map/attend/pallas_call | solution.py:97
  91.5 1.5 collective-permute-start.15
  93.0 1.2 collective-permute-start.1
  94.5 1.2 and_select_fusion.1
  95.7 5.3 %assemble.1.w_ref = bf16[2176,1024]{1,0:T(8,128)(2,1)} custom-call(s32[4]{0:T(128)} %get-tuple-element.35.z_ref, s32[4]{0:T(128)} %get-tuple-element.33.x_ref, s32[1]{0:T(128)} %bitcast.core_ref, bf16[4,136,512]{2,1,0:T(8,128)(2,1)} %pad_maximum_fusion.refs_0_, bf16[4,136,512]{2,1,0:T(8,128)(2,1)} %collective-permute-done.6.refs_1_, ...), custom_call_target="tpu_custom_call" | custom-call | flops 1048576 | bytes 9437184 | tf_op jit(solution)/shard_map/assemble/pallas_call | solution.py:201
  101.1 4.3 %collective-permute-done.15.c_ref = bf16[512,512]{1,0:T(8,128)(2,1)} collective-permute-done((bf16[512,512]{1,0:T(8,128)(2,1)}, bf16[512,512]{1,0:T(8,128)(2,1)}, u32[]{:S(2)}, u32[]{:S(2)}) %collective-permute-start.15) | collective-permute-done | bytes 524320 | tf_op jit(solution)/shard_map/ppermute | solution.py:44
  105.3 2.7 %collective-permute-start.16 = (bf16[512,512]{1,0:T(8,128)(2,1)}, bf16[512,512]{1,0:T(8,128)(2,1)}, u32[]{:S(2)}, u32[]{:S(2)}) collective-permute-start(bf16[512,512]{1,0:T(8,128)(2,1)} %collective-permute-done.15.c_ref), channel_id=1, source_target_pairs={{0,48},{16,0},{32,16},{48,32},{1,49},{17,1},{33,17},{49,33},{2,50}... | collective-permute-start | bytes 1572872 | tf_op jit(solution)/shard_map/ppermute | solution.py:44
  108.0 8.5 %collective-permute-done.1.c_ref = bf16[512,512]{1,0:T(8,128)(2,1)} collective-permute-done((bf16[512,512]{1,0:T(8,128)(2,1)}, bf16[512,512]{1,0:T(8,128)(2,1)}, u32[]{:S(2)}, u32[]{:S(2)}) %collective-permute-start.1) | collective-permute-done | bytes 524320 | tf_op jit(solution)/shard_map/ppermute | solution.py:44
  116.6 16.7 %chunk.2 = (bf16[1024,2176]{1,0:T(8,128)(2,1)}, bf16[1024,1024]{1,0:T(8,128)(2,1)}, f32[8,1024]{1,0:T(8,128)}) custom-call(s32[4]{0:T(128)} %get-tuple-element.34.idx_ref, s32[1]{0:T(128)} %dynamic_slice.9.len_ref, bf16[512,512]{1,0:T(8,128)(2,1)} %attend.2.a_ref, bf16[512,512]{1,0:T(8,128)(2,1)} %collective-permute-done.b_ref, ...), custom_call_target="tpu_custom_call" | custom-call | flops 6845104128 | bytes 20971520 | tf_op jit(solution)/shard_map/chunk/pallas_call | solution.py:154
  133.3 16.6 %chunk.3 = (bf16[1024,2176]{1,0:T(8,128)(2,1)}, bf16[1024,1024]{1,0:T(8,128)(2,1)}, f32[8,1024]{1,0:T(8,128)}) custom-call(s32[4]{0:T(128)} %get-tuple-element.34.idx_ref, s32[1]{0:T(128)} %dynamic_slice.9.len_ref, bf16[512,512]{1,0:T(8,128)(2,1)} %attend.3.a_ref, ...), custom_call_target="tpu_custom_call", output_to_operand_aliasing={{0}: (9, {}), {1}: (10, {})} | custom-call | flops 6845104128 | bytes 20971520 | tf_op jit(solution)/shard_map/chunk/pallas_call | solution.py:154
  149.9 9.5 %grad.1 = (bf16[8,2,136,512]{3,2,1,0:T(8,128)(2,1)}, bf16[8,2,136,512]{3,2,1,0:T(8,128)(2,1)}) custom-call(s32[1]{0:T(128)} %bitcast.core_ref, bf16[1024,2176]{1,0:T(8,128)(2,1)} %get-tuple-element.19.f_ref, bf16[1024,1024]{1,0:T(8,128)(2,1)} %get-tuple-element.20.s_ref), custom_call_target="tpu_custom_call" | custom-call | flops 4563402752 | bytes 11534336 | tf_op jit(solution)/shard_map/grad/pallas_call | solution.py:231
  159.4 1.3 collective-permute-start.20
  160.7 1.9 collective-permute-start.17
  162.6 1.0 collective-permute-start.18
  167.8 6.4 %all-to-all-start.2 = ((f32[16,2,128]{2,1,0:T(2,128)}), f32[16,2,128]{2,1,0:T(2,128)}, u32[]{:S(2)}, u32[]{:S(2)}) async-start(f32[16,2,128]{2,1,0:T(2,128)} %broadcast_in_dim.5), calls=%async_computation.2 | async-start | bytes 32768 | tf_op jit(solution)/shard_map/all_to_all | solution.py:48
  174.9 0.7 broadcast_select_fusion.3
  175.6 1.0 broadcast_select_fusion.1
  176.6 0.9 fusion.8.head_ref
  178.3 1.8 all-to-all-done.2
  180.7 4.6 %all-to-all-start.1 = ((f32[8,8,256]{2,1,0:T(8,128)}), f32[8,8,256]{2,1,0:T(8,128)}, u32[]{:S(2)}, u32[]{:S(2)}) async-start(f32[8,8,256]{2,1,0:T(8,128)} %broadcast_in_dim.4), calls=%async_computation.1 | async-start | bytes 131072 | tf_op jit(solution)/shard_map/all_to_all | solution.py:48
  185.9 4.4 %all-to-all-done.1 = f32[8,8,256]{2,1,0:T(8,128)} async-done(((f32[8,8,256]{2,1,0:T(8,128)}), f32[8,8,256]{2,1,0:T(8,128)}, u32[]{:S(2)}, u32[]{:S(2)}) %all-to-all-start.1) | async-done | bytes 65568 | tf_op jit(solution)/shard_map/all_to_all | solution.py:48
  190.3 2.3 logit.1
  192.6 4.6 %scaled.1 = bf16[8,2,152,512]{3,2,1,0:T(8,128)(2,1)} custom-call(s32[1]{0:T(128)} %bitcast.core_ref, bf16[8,2,136,512]{3,2,1,0:T(8,128)(2,1)} %get-tuple-element.21.keep_ref, bf16[8,2,136,512]{3,2,1,0:T(8,128)(2,1)} %collective-permute-done.20.got_ref, f32[2,8,1024]{2,1,0:T(8,128)} %get-tuple-element.23.scale_ref, bf16[8,1024]{1,0:T(8,128)(2,1)} %copy-done.1, ...), custom_call_target="tpu_custom_call" | custom-call | flops 8388608 | bytes 7340032 | tf_op jit(solution)/shard_map/scaled/pallas_call | solution.py:330
  197.2 6.1 %all-to-all-start.3 = ((bf16[16,152,512]{2,1,0:T(8,128)(2,1)}), bf16[16,152,512]{2,1,0:T(8,128)(2,1)S(1)}, u32[]{:S(2)}, u32[]{:S(2)}) async-start(bf16[16,152,512]{2,1,0:T(8,128)(2,1)} %bitcast.30), calls=%async_computation.3 | async-start | bytes 4980736 | tf_op jit(solution)/shard_map/all_to_all | solution.py:48
  203.4 2.9 %collective-permute-start.19 = (f32[1,7]{1,0:T(1,128)S(1)}, f32[1,7]{1,0:T(1,128)S(1)}, u32[]{:S(2)}, u32[]{:S(2)}) collective-permute-start(f32[1,7]{1,0:T(1,128)S(1)} %bitcast.36), channel_id=1, source_target_pairs={{0,64},{64,0},{1,65},{65,1},{2,66},{66,2},{3,67},{67,3},{4,68},{68... | collective-permute-start | bytes 92 | tf_op jit(solution)/shard_map/ppermute | solution.py:44
  206.4 29.8 %collective-permute-done.19 = f32[1,7]{1,0:T(1,128)S(1)} collective-permute-done((f32[1,7]{1,0:T(1,128)S(1)}, f32[1,7]{1,0:T(1,128)S(1)}, u32[]{:S(2)}, u32[]{:S(2)}) %collective-permute-start.19) | collective-permute-done | bytes 60 | tf_op jit(solution)/shard_map/ppermute | solution.py:44
  236.4 2.2 collective-permute-start.21
  239.2 1.0 slice_reduce_fusion
  240.2 1.0 fusion
  (52 shorter events, 10.0 us)
Async XLA Ops:
  4.8 7.6 %copy-start.2 = (bf16[136,512]{1,0:T(8,128)(2,1)S(1)}, bf16[136,512]{1,0:T(8,128)(2,1)}, u32[]{:S(2)}) copy-start(bf16[136,512]{1,0:T(8,128)(2,1)} %param.20) | copy-start | bytes 417796
  4.8 22.4 %copy-start.4 = (s32[2]{0:T(128)S(1)}, s32[2]{0:T(128)}, u32[]{:S(2)}) copy-start(s32[2]{0:T(128)} %param.18) | copy-start | bytes 28
  4.8 59.9 %all-to-all-start = ((bf16[8,3,128,512]{3,2,1,0:T(8,128)(2,1)}), bf16[8,3,128,512]{3,2,1,0:T(8,128)(2,1)}, u32[]{:S(2)}, u32[]{:S(2)}) async-start(bf16[8,3,128,512]{3,2,1,0:T(8,128)(2,1)} %pack.1), calls=%async_computation | async-start | bytes 6291456 | tf_op jit(solution)/shard_map/all_to_all | solution.py:48
  12.4 7.0 %collective-permute-start.3 = (bf16[136,512]{1,0:T(8,128)(2,1)S(1)}, bf16[136,512]{1,0:T(8,128)(2,1)S(1)}, u32[]{:S(2)}, u32[]{:S(2)}) collective-permute-start(bf16[136,512]{1,0:T(8,128)(2,1)S(1)} %copy-done.2), channel_id=1, source_target_pairs={{0,4},{4,8},{8,12},{12,0},{1,5},{5,9},{9,13},{13,1},{2,6},{6,10},{... | collective-permute-start | bytes 417800 | tf_op jit(solution)/shard_map/ppermute | solution.py:44
  14.1 5.3 %collective-permute-start.4 = (bf16[136,512]{1,0:T(8,128)(2,1)S(1)}, bf16[136,512]{1,0:T(8,128)(2,1)S(1)}, u32[]{:S(2)}, u32[]{:S(2)}) collective-permute-start(bf16[136,512]{1,0:T(8,128)(2,1)S(1)} %copy-done.2), channel_id=1, source_target_pairs={{0,12},{4,0},{8,4},{12,8},{1,13},{5,1},{9,5},{13,9},{2,14},{6,2},{... | collective-permute-start | bytes 417800 | tf_op jit(solution)/shard_map/ppermute | solution.py:44
  16.3 7.3 %collective-permute-start.5 = (bf16[136,512]{1,0:T(8,128)(2,1)S(1)}, bf16[136,512]{1,0:T(8,128)(2,1)S(1)}, u32[]{:S(2)}, u32[]{:S(2)}) collective-permute-start(bf16[136,512]{1,0:T(8,128)(2,1)S(1)} %copy-done.2), channel_id=1, source_target_pairs={{0,8},{4,12},{8,0},{12,4},{1,9},{5,13},{9,1},{13,5},{2,10},{6,14},... | collective-permute-start | bytes 417800 | tf_op jit(solution)/shard_map/ppermute | solution.py:44
  24.5 38.0 %collective-permute-start.6 = (bf16[4,136,512]{2,1,0:T(8,128)(2,1)}, bf16[4,136,512]{2,1,0:T(8,128)(2,1)}, u32[]{:S(2)}, u32[]{:S(2)}) collective-permute-start(bf16[4,136,512]{2,1,0:T(8,128)(2,1)} %pad_maximum_fusion.refs_0_), channel_id=1, source_target_pairs={{0,2},{2,64},{64,66},{66,0},{1,3},{3,65},{65,67},{67,1},{4,6},{6,6... | collective-permute-start | bytes 1671176 | tf_op jit(solution)/shard_map/ppermute | solution.py:44
  24.8 48.1 %collective-permute-start.7 = (bf16[4,136,512]{2,1,0:T(8,128)(2,1)}, bf16[4,136,512]{2,1,0:T(8,128)(2,1)}, u32[]{:S(2)}, u32[]{:S(2)}) collective-permute-start(bf16[4,136,512]{2,1,0:T(8,128)(2,1)} %pad_maximum_fusion.refs_0_), channel_id=1, source_target_pairs={{0,66},{2,0},{64,2},{66,64},{1,67},{3,1},{65,3},{67,65},{4,70},{6,... | collective-permute-start | bytes 1671176 | tf_op jit(solution)/shard_map/ppermute | solution.py:44
  27.8 63.7 %collective-permute-start.10 = (bf16[4,136,512]{2,1,0:T(8,128)(2,1)}, bf16[4,136,512]{2,1,0:T(8,128)(2,1)}, u32[]{:S(2)}, u32[]{:S(2)}) collective-permute-start(bf16[4,136,512]{2,1,0:T(8,128)(2,1)} %pad_maximum_fusion.refs_0_), channel_id=1, source_target_pairs={{0,1},{1,0},{2,3},{3,2},{4,5},{5,4},{6,7},{7,6},{8,9},{9,8},{10,11... | collective-permute-start | bytes 1671176 | tf_op jit(solution)/shard_map/ppermute | solution.py:44
  64.2 12.7 %collective-permute-start.8 = (bf16[2,136,512]{2,1,0:T(8,128)(2,1)}, bf16[2,136,512]{2,1,0:T(8,128)(2,1)}, u32[]{:S(2)}, u32[]{:S(2)}) collective-permute-start(bf16[2,136,512]{2,1,0:T(8,128)(2,1)} %slice.28), channel_id=1, source_target_pairs={{0,2},{2,64},{64,66},{66,0},{1,3},{3,65},{65,67},{67,1},{4,6},{6,6... | collective-permute-start | bytes 835592 | tf_op jit(solution)/shard_map/ppermute | solution.py:44
  64.2 28.8 %collective-permute-start.11 = (bf16[4,136,512]{2,1,0:T(8,128)(2,1)}, bf16[4,136,512]{2,1,0:T(8,128)(2,1)}, u32[]{:S(2)}, u32[]{:S(2)}) collective-permute-start(bf16[4,136,512]{2,1,0:T(8,128)(2,1)} %collective-permute-done.6.refs_1_), channel_id=1, source_target_pairs={{0,1},{1,0},{2,3},{3,2},{4,5},{5,4},{6,7},{7,6},{8,9},{9,8},{10,11... | collective-permute-start | bytes 1671176 | tf_op jit(solution)/shard_map/ppermute | solution.py:44
  71.7 22.5 %collective-permute-start = (bf16[512,512]{1,0:T(8,128)(2,1)}, bf16[512,512]{1,0:T(8,128)(2,1)}, u32[]{:S(2)}, u32[]{:S(2)}) collective-permute-start(bf16[512,512]{1,0:T(8,128)(2,1)} %attend.2.a_ref), channel_id=1, source_target_pairs={{0,16},{16,32},{32,48},{48,0},{1,17},{17,33},{33,49},{49,1},{2,18}... | collective-permute-start | bytes 1572872 | tf_op jit(solution)/shard_map/ppermute | solution.py:44
  73.9 8.7 %collective-permute-start.9 = (bf16[2,136,512]{2,1,0:T(8,128)(2,1)S(1)}, bf16[2,136,512]{2,1,0:T(8,128)(2,1)S(1)}, u32[]{:S(2)}, u32[]{:S(2)}) collective-permute-start(bf16[2,136,512]{2,1,0:T(8,128)(2,1)S(1)} %slice.29), channel_id=1, source_target_pairs={{0,66},{2,0},{64,2},{66,64},{1,67},{3,1},{65,3},{67,65},{4,70},{6,... | collective-permute-start | bytes 835592 | tf_op jit(solution)/shard_map/ppermute | solution.py:44
  76.9 18.8 %collective-permute-start.12 = (bf16[4,136,512]{2,1,0:T(8,128)(2,1)}, bf16[4,136,512]{2,1,0:T(8,128)(2,1)}, u32[]{:S(2)}, u32[]{:S(2)}) collective-permute-start(bf16[4,136,512]{2,1,0:T(8,128)(2,1)} %collective-permute-done.7.refs_2_), channel_id=1, source_target_pairs={{0,1},{1,0},{2,3},{3,2},{4,5},{5,4},{6,7},{7,6},{8,9},{9,8},{10,11... | collective-permute-start | bytes 1671176 | tf_op jit(solution)/shard_map/ppermute | solution.py:44
  83.4 12.4 %collective-permute-start.13 = (bf16[4,136,512]{2,1,0:T(8,128)(2,1)}, bf16[4,136,512]{2,1,0:T(8,128)(2,1)}, u32[]{:S(2)}, u32[]{:S(2)}) collective-permute-start(bf16[4,136,512]{2,1,0:T(8,128)(2,1)} %constant_dynamic-update-slice_fusion.refs_3_), channel_id=1, source_target_pairs={{0,1},{1,0},{2,3},{3,2},{4,5},{5,4},{6,7},{7,6},{8,9},{9,8},{10,11... | collective-permute-start | bytes 1671176 | tf_op jit(solution)/shard_map/ppermute | solution.py:44
  91.5 13.8 %collective-permute-start.15 = (bf16[512,512]{1,0:T(8,128)(2,1)}, bf16[512,512]{1,0:T(8,128)(2,1)}, u32[]{:S(2)}, u32[]{:S(2)}) collective-permute-start(bf16[512,512]{1,0:T(8,128)(2,1)} %attend.3.a_ref), channel_id=1, source_target_pairs={{0,48},{16,0},{32,16},{48,32},{1,49},{17,1},{33,17},{49,33},{2,50}... | collective-permute-start | bytes 1572872 | tf_op jit(solution)/shard_map/ppermute | solution.py:44
  93.0 23.5 %collective-permute-start.1 = (bf16[512,512]{1,0:T(8,128)(2,1)}, bf16[512,512]{1,0:T(8,128)(2,1)}, u32[]{:S(2)}, u32[]{:S(2)}) collective-permute-start(bf16[512,512]{1,0:T(8,128)(2,1)} %attend.2.a_ref), channel_id=1, source_target_pairs={{0,48},{16,0},{32,16},{48,32},{1,49},{17,1},{33,17},{49,33},{2,50}... | collective-permute-start | bytes 1572872 | tf_op jit(solution)/shard_map/ppermute | solution.py:44
  94.2 22.3 %collective-permute-start.2 = (bf16[512,512]{1,0:T(8,128)(2,1)}, bf16[512,512]{1,0:T(8,128)(2,1)}, u32[]{:S(2)}, u32[]{:S(2)}) collective-permute-start(bf16[512,512]{1,0:T(8,128)(2,1)} %collective-permute-done.b_ref), channel_id=1, source_target_pairs={{0,16},{16,32},{32,48},{48,0},{1,17},{17,33},{33,49},{49,1},{2,18}... | collective-permute-start | bytes 1572872 | tf_op jit(solution)/shard_map/ppermute | solution.py:44
  101.1 32.2 %collective-permute-start.14 = (bf16[512,512]{1,0:T(8,128)(2,1)}, bf16[512,512]{1,0:T(8,128)(2,1)}, u32[]{:S(2)}, u32[]{:S(2)}) collective-permute-start(bf16[512,512]{1,0:T(8,128)(2,1)} %attend.3.a_ref), channel_id=1, source_target_pairs={{0,16},{16,32},{32,48},{48,0},{1,17},{17,33},{33,49},{49,1},{2,18}... | collective-permute-start | bytes 1572872 | tf_op jit(solution)/shard_map/ppermute | solution.py:44
  105.3 27.9 %collective-permute-start.16 = (bf16[512,512]{1,0:T(8,128)(2,1)}, bf16[512,512]{1,0:T(8,128)(2,1)}, u32[]{:S(2)}, u32[]{:S(2)}) collective-permute-start(bf16[512,512]{1,0:T(8,128)(2,1)} %collective-permute-done.15.c_ref), channel_id=1, source_target_pairs={{0,48},{16,0},{32,16},{48,32},{1,49},{17,1},{33,17},{49,33},{2,50}... | collective-permute-start | bytes 1572872 | tf_op jit(solution)/shard_map/ppermute | solution.py:44
  159.4 33.3 %collective-permute-start.20 = (bf16[8,2,136,512]{3,2,1,0:T(8,128)(2,1)}, bf16[8,2,136,512]{3,2,1,0:T(8,128)(2,1)}, u32[]{:S(2)}, u32[]{:S(2)}) collective-permute-start(bf16[8,2,136,512]{3,2,1,0:T(8,128)(2,1)} %get-tuple-element.22), channel_id=1, source_target_pairs={{0,1},{1,0},{2,3},{3,2},{4,5},{5,4},{6,7},{7,6},{8,9},{9,8},{10,11... | collective-permute-start | bytes 6684680 | tf_op jit(solution)/shard_map/ppermute | solution.py:44
  160.7 14.2 %collective-permute-start.17 = (f32[7,512]{1,0:T(8,128)}, f32[7,512]{1,0:T(8,128)S(1)}, u32[]{:S(2)}, u32[]{:S(2)}) collective-permute-start(f32[7,512]{1,0:T(8,128)} %param.22), channel_id=1, source_target_pairs={{0,64},{64,0},{1,65},{65,1},{2,66},{66,2},{3,67},{67,3},{4,68},{68... | collective-permute-start | bytes 43016 | tf_op jit(solution)/shard_map/ppermute | solution.py:44
  162.6 13.0 %collective-permute-start.18 = (bf16[512,256]{1,0:T(8,128)(2,1)}, bf16[512,256]{1,0:T(8,128)(2,1)S(1)}, u32[]{:S(2)}, u32[]{:S(2)}) collective-permute-start(bf16[512,256]{1,0:T(8,128)(2,1)} %param.21), channel_id=1, source_target_pairs={{0,64},{64,0},{1,65},{65,1},{2,66},{66,2},{3,67},{67,3},{4,68},{68... | collective-permute-start | bytes 786440 | tf_op jit(solution)/shard_map/ppermute | solution.py:44
  167.8 12.3 %all-to-all-start.2 = ((f32[16,2,128]{2,1,0:T(2,128)}), f32[16,2,128]{2,1,0:T(2,128)}, u32[]{:S(2)}, u32[]{:S(2)}) async-start(f32[16,2,128]{2,1,0:T(2,128)} %broadcast_in_dim.5), calls=%async_computation.2 | async-start | bytes 32768 | tf_op jit(solution)/shard_map/all_to_all | solution.py:48
  176.6 0.9 copy-start
  177.5 0.6 copy-start.1
  180.7 9.6 %all-to-all-start.1 = ((f32[8,8,256]{2,1,0:T(8,128)}), f32[8,8,256]{2,1,0:T(8,128)}, u32[]{:S(2)}, u32[]{:S(2)}) async-start(f32[8,8,256]{2,1,0:T(8,128)} %broadcast_in_dim.4), calls=%async_computation.1 | async-start | bytes 131072 | tf_op jit(solution)/shard_map/all_to_all | solution.py:48
  197.2 6.1 %copy-start.3 = (f32[2,8,128]{2,1,0:T(8,128)S(1)}, f32[2,8,128]{2,1,0:T(8,128)}, u32[]{:S(2)}) copy-start(f32[2,8,128]{2,1,0:T(8,128)} %get-tuple-element.18) | copy-start | bytes 24580
  197.2 39.0 %all-to-all-start.3 = ((bf16[16,152,512]{2,1,0:T(8,128)(2,1)}), bf16[16,152,512]{2,1,0:T(8,128)(2,1)S(1)}, u32[]{:S(2)}, u32[]{:S(2)}) async-start(bf16[16,152,512]{2,1,0:T(8,128)(2,1)} %bitcast.30), calls=%async_computation.3 | async-start | bytes 4980736 | tf_op jit(solution)/shard_map/all_to_all | solution.py:48
  203.4 32.8 %collective-permute-start.19 = (f32[1,7]{1,0:T(1,128)S(1)}, f32[1,7]{1,0:T(1,128)S(1)}, u32[]{:S(2)}, u32[]{:S(2)}) collective-permute-start(f32[1,7]{1,0:T(1,128)S(1)} %bitcast.36), channel_id=1, source_target_pairs={{0,64},{64,0},{1,65},{65,1},{2,66},{66,2},{3,67},{67,3},{4,68},{68... | collective-permute-start | bytes 92 | tf_op jit(solution)/shard_map/ppermute | solution.py:44
  236.4 3.8 %collective-permute-start.21 = (bf16[16,16,512]{2,0,1:T(8,128)(2,1)S(1)}, bf16[16,16,512]{2,0,1:T(8,128)(2,1)S(1)}, u32[]{:S(2)}, u32[]{:S(2)}) collective-permute-start(bf16[16,16,512]{2,0,1:T(8,128)(2,1)S(1)} %copy.31), channel_id=1, source_target_pairs={{0,1},{1,0},{2,3},{3,2},{4,5},{5,4},{6,7},{7,6},{8,9},{9,8},{10,11... | collective-permute-start | bytes 786440 | tf_op jit(solution)/shard_map/ppermute | solution.py:44

commit v2 on v1

v2 whole, which is shorter than its diff:
```python
import functools
import math

import jax
import jax.numpy as jnp
from jax import lax
from jax.experimental import pallas as pl
from jax.experimental.pallas import tpu as pltpu
from jax.sharding import Mesh
from jax.sharding import PartitionSpec as P


F32, BF16 = jnp.float32, jnp.bfloat16
HD = 128
HEADS_HERE = 4
COLS = 512
ATT = 2048
VIS = 2176
ROWS = 136
HID_HERE = 1024
SEQ = 1024
CHUNKS = 2
CH = SEQ // CHUNKS
NBINS = 256
SQRT_HALF = 0.7071067811865476
INV_ROOT_TAU = 0.3989422804014327
NEG_LARGE = -1e30
EXP2_SCALE = math.log2(math.e) / math.sqrt(HD)
VMEM_LIMIT = 67043328
SMALL = 14 * 1024 * 1024
VMEM = pl.BlockSpec(memory_space=pltpu.VMEM)
SMEM = pl.BlockSpec(memory_space=pltpu.SMEM)
ANY = pl.BlockSpec(memory_space=pl.ANY)
HBM = pl.BlockSpec(memory_space=pltpu.HBM)


def params(limit=VMEM_LIMIT):
    return pltpu.CompilerParams(dimension_semantics=("arbitrary",), vmem_limit_bytes=limit)


def local(limit=SMALL):
    return pltpu.CompilerParams(vmem_limit_bytes=limit)


def cost(flops, nbytes, trans=0):
    return pl.CostEstimate(flops=flops, bytes_accessed=nbytes, transcendentals=trans)


def shifted(x, axis, by):
    count = lax.axis_size(axis)
    return lax.ppermute(x, axis, [(i, (i + by) % count) for i in range(count)])


def across(x, by):
    pairs = [(2 * i + c, 2 * ((i + by) % 4) + 1 - c) for i in range(4) for c in range(2)]
    return lax.ppermute(x, ("y", "c"), pairs)


def dealt(x, axes):
    return lax.all_to_all(x, axes, 0, 0, tiled=True)


def pack_kernel(q_ref, k_ref, v_ref, o_ref):
    for i, ref in enumerate((q_ref, k_ref, v_ref)):
        for j in range(2):
            o_ref[j, i] = ref[0, :, j * COLS : (j + 1) * COLS]


def pack(q, k, v):
    spec = pl.BlockSpec((1, 128, 2 * COLS), lambda i: (i // 2, 0, i % 2))
    return pl.pallas_call(
        pack_kernel,
        out_shape=jax.ShapeDtypeStruct((8, 3, 128, COLS), BF16),
        grid=(4,),
        in_specs=[spec] * 3,
        out_specs=pl.BlockSpec((2, 3, 128, COLS), lambda i: (i, 0, 0, 0)),
        compiler_params=params(),
        cost_estimate=cost(0, 6 << 20),
        name="pack",
    )(q, k, v)


def attend_kernel(chunk, len_ref, got_ref, *rest):
    if chunk == 1:
        map_ref, o_ref, held_ref, sem = rest
        copy = pltpu.make_async_copy(map_ref, held_ref, sem)
        copy.start()
    else:
        o_ref = rest[-1]
    at = lax.broadcasted_iota(jnp.int32, (1, SEQ), 1)
    bias = jnp.where(at < len_ref[0], 0.0, NEG_LARGE)

    @pl.loop(0, HEADS_HERE)
    def _(h):
        lanes = pl.ds(pl.multiple_of(h * HD, HD), HD)
        k = got_ref[:, 1, :, lanes].reshape(SEQ, HD)
        v = got_ref[:, 2, :, lanes].reshape(SEQ, HD)
        for r in range(CH // 256):
            first = chunk * (CH // 128) + 2 * r
            q = got_ref[first : first + 2, 0, :, lanes].reshape(256, HD)
            s = lax.dot_general(q, k, (((1,), (1,)), ((), ())), preferred_element_type=F32)
            s = s + bias
            top = jnp.max(s, axis=-1, keepdims=True)
            p = jnp.exp2((s - top) * EXP2_SCALE)
            total = jnp.sum(p, axis=-1, keepdims=True)
            w = jnp.dot(p.astype(BF16), v, preferred_element_type=F32)
            o_ref[r * 256 : (r + 1) * 256, lanes] = (w / total).astype(BF16)

    if chunk == 1:
        copy.wait()


def attend(got, length, chunk, after):
    out = jax.ShapeDtypeStruct((CH, COLS), BF16)
    held = jax.ShapeDtypeStruct((ATT, VIS), BF16)
    return pl.pallas_call(
        functools.partial(attend_kernel, chunk),
        out_shape=(out, held) if chunk == 1 else out,
        in_specs=[SMEM, VMEM] + ([HBM] if chunk == 1 else [ANY] + [SMEM] * (len(after) - 1)),
        out_specs=(VMEM, VMEM) if chunk == 1 else VMEM,
        scratch_shapes=[pltpu.SemaphoreType.DMA] if chunk == 1 else [],
        compiler_params=local(37 * 1024 * 1024 if chunk == 1 else SMALL),
        cost_estimate=cost(4 * CH * SEQ * COLS, 3 << 20, 4 * CH * SEQ),
        name="attend",
    )(length, got, *after)


TILE = 256


def chunk_kernel(chunk, idx_ref, len_ref, a_ref, b_ref, c_ref, d_ref, fm_ref, w_ref, *rest):
    full, act = rest[-2:]
    rest = rest[:-2]
    if chunk == 0:
        o_ref, slope_ref, pool_ref = rest
    else:
        pool0_ref, ae_ref, ae_other_ref, hw_ref, hw_other_ref = rest[:5]
        o_ref, slope_ref, head_ref, part_ref = rest[5:]
    for i, ref in enumerate((a_ref, b_ref, c_ref, d_ref)):
        full[:, pl.ds(pl.multiple_of(idx_ref[i] * COLS, COLS), COLS)] = ref[...]

    @pl.loop(0, 3)
    def _(n):
        lanes = pl.ds(pl.multiple_of(n * 512, 512), 512)
        o_ref[:, lanes] = jnp.dot(
            full[...], fm_ref[:, lanes], preferred_element_type=F32
        ).astype(BF16)

    o_ref[:, 1536:] = jnp.dot(
        full[...], fm_ref[:, 1536:], preferred_element_type=F32
    ).astype(BF16)

    at = lax.broadcasted_iota(jnp.int32, (CH, 1), 0) + chunk * CH
    live = (at < len_ref[0]).astype(F32)
    tiles = HID_HERE // TILE
    pools = []
    for j in range(tiles + 1):
        if j < tiles:
            act[j % 2] = jnp.dot(
                o_ref[...], w_ref[:, j * TILE : (j + 1) * TILE], preferred_element_type=F32
            )
        if j > 0:
            t = act[(j - 1) % 2]
            cdf = 0.5 * (1.0 + lax.erf(t * SQRT_HALF))
            slope = cdf + t * jnp.exp(-0.5 * t * t) * INV_ROOT_TAU
            slope_ref[:, (j - 1) * TILE : j * TILE] = (live * slope).astype(BF16)
            pools.append(jnp.sum(live * (t * cdf), axis=0, keepdims=True))
    pool = jnp.concatenate(pools, axis=1)
    if chunk == 0:
        pool_ref[...] = jnp.broadcast_to(pool, pool_ref.shape)
        return
    pool_row = (pool + pool0_ref[0:1, :]) / len_ref[0].astype(F32)
    x = len_ref[1]
    part = jnp.zeros((8, NBINS), F32)
    for side, (e_ref, h_ref) in enumerate(((ae_ref, hw_ref), (ae_other_ref, hw_other_ref))):
        embed = jnp.concatenate([e_ref[...], jnp.zeros((1, COLS), F32)], axis=0)
        low, high = pool_row[:, :COLS], pool_row[:, COLS:]
        mine = jnp.where((x == 0) == (side == 0), low, high)
        head = (mine + embed).astype(BF16)
        place = x if side == 0 else 1 - x
        head_ref[:, pl.ds(pl.multiple_of(place * COLS, COLS), COLS)] = head
        part = part + jnp.dot(head, h_ref[...], preferred_element_type=F32)
    part_ref[...] = part


def chunk_of(idx, where, pieces, frame_map, weight, chunk, more):
    shapes = [
        jax.ShapeDtypeStruct((CH, VIS), BF16),
        jax.ShapeDtypeStruct((CH, HID_HERE), BF16),
    ]
    if chunk == 0:
        shapes += [jax.ShapeDtypeStruct((8, HID_HERE), F32)]
    else:
        shapes += [
            jax.ShapeDtypeStruct((8, HID_HERE), BF16),
            jax.ShapeDtypeStruct((8, NBINS), F32),
        ]
    return pl.pallas_call(
        functools.partial(chunk_kernel, chunk),
        out_shape=tuple(shapes),
        in_specs=[SMEM, SMEM] + [VMEM] * (6 + len(more)),
        out_specs=tuple([VMEM] * len(shapes)),
        scratch_shapes=[pltpu.VMEM((CH, ATT), BF16), pltpu.VMEM((2, CH, TILE), F32)],
        compiler_params=local(),
        cost_estimate=cost(2 * CH * VIS * (ATT + HID_HERE), 20 << 20, 2 * CH * HID_HERE),
        name="chunk",
    )(idx, where, *pieces, frame_map, weight, *more)


def assemble_kernel(z_ref, x_ref, core_ref, *refs):
    o_ref = refs[-1]
    lead = core_ref[0] == 0
    for k in range(4):
        x = x_ref[k]
        col = pl.multiple_of((x // 2) * COLS, COLS)
        for i in range(4):
            mine, other = refs[k][i].astype(F32), refs[4 + k][i].astype(F32)
            pair = [jnp.where(lead, mine, other), jnp.where(lead, other, mine)]
            row = pl.multiple_of((z_ref[i] * 2 + x % 2) * 2 * ROWS, 2 * ROWS)
            o_ref[pl.ds(row, 2 * ROWS), pl.ds(col, COLS)] = jnp.concatenate(pair, axis=0).astype(
                BF16
            )


def assemble(z_order, x_order, core, own, other):
    return pl.pallas_call(
        assemble_kernel,
        out_shape=jax.ShapeDtypeStruct((VIS, HID_HERE), BF16),
        in_specs=[SMEM] * 3 + [VMEM] * 8,
        out_specs=VMEM,
        compiler_params=local(),
        cost_estimate=cost(1 << 20, 9 << 20),
        name="assemble",
    )(z_order, x_order, core, *own, *other)


def grad_kernel(core_ref, f0_ref, s0_ref, f1_ref, s1_ref, keep_ref, send_ref, total):
    core = core_ref[0]

    @pl.loop(0, 2)
    def _(x):
        lanes = pl.ds(pl.multiple_of(x * COLS, COLS), COLS)
        for r in range(VIS // 128):
            rows = slice(r * 128, (r + 1) * 128)
            total[rows, :] = sum(
                lax.dot_general(
                    f[:, rows], s[:, lanes], (((0,), (0,)), ((), ())), preferred_element_type=F32
                )
                for f, s in ((f0_ref, s0_ref), (f1_ref, s1_ref))
            )
        for b in range(8):
            mine = pl.multiple_of((2 * b + core) * ROWS, 8)
            other = pl.multiple_of((2 * b + 1 - core) * ROWS, 8)
            keep_ref[b, x] = total[pl.ds(mine, ROWS), :].astype(BF16)
            send_ref[b, x] = total[pl.ds(other, ROWS), :].astype(BF16)


def grad_of(core, *parts):
    out = jax.ShapeDtypeStruct((8, 2, ROWS, COLS), BF16)
    return pl.pallas_call(
        grad_kernel,
        out_shape=(out, out),
        in_specs=[SMEM] + [VMEM] * 4,
        out_specs=(VMEM, VMEM),
        scratch_shapes=[pltpu.VMEM((VIS, COLS), F32)],
        compiler_params=local(),
        cost_estimate=cost(2 * SEQ * HID_HERE * VIS, 11 << 20),
        name="grad",
    )(core, *parts)


def logit_kernel(at_ref, *refs):
    parts, refs = refs[:8], refs[8:]
    near_ref, far_ref, hw_ref, other_ref, lp_ref, lg_ref, scale_ref = refs
    facts = jnp.concatenate([near_ref[...], far_ref[...]], axis=0)
    lane = lax.broadcasted_iota(jnp.int32, (1, 128), 1)
    line = lane.astype(F32)

    def column(rows, i):
        return jnp.sum(jnp.where(lane == i, rows, 0.0), axis=1, keepdims=True)

    gains, groups = column(facts, 0), column(facts, 1)
    member = (groups == line).astype(F32)
    sums = jnp.sum(member * gains, axis=0, keepdims=True)
    squares = jnp.sum(member * (gains * gains), axis=0, keepdims=True)
    sizes = jnp.maximum(jnp.sum(member, axis=0, keepdims=True), 1.0)
    mean = sums / sizes
    spread = jnp.sqrt(jnp.maximum(squares / sizes - mean * mean, 1.0))
    masks = jnp.where((lane >= 16) & (lane < 24), facts, 0.0)
    count = jnp.maximum(jnp.sum(jnp.sum(masks, axis=1, keepdims=True), axis=0, keepdims=True), 1.0)
    action = lax.broadcasted_iota(jnp.int32, (8, 128), 0)
    bins = lax.broadcasted_iota(jnp.int32, (8, NBINS), 1).astype(F32)
    for side in range(2):
        c = at_ref[0] if side == 0 else 1 - at_ref[0]
        here = near_ref[pl.ds(at_ref[1] + 2 * side, 1), :]
        own = (column(here, 1) == line).astype(F32)
        advantage = (column(here, 0) - jnp.sum(own * mean, axis=1, keepdims=True)) / jnp.sum(
            own * spread, axis=1, keepdims=True
        )
        rows = jnp.broadcast_to(here, (8, 128))
        act = jnp.sum(jnp.where(lane == action + 8, rows, 0.0), axis=1, keepdims=True)
        mask = jnp.sum(jnp.where(lane == action + 16, rows, 0.0), axis=1, keepdims=True)
        weight = -mask * advantage / count

        own4 = [ref[...] for ref in parts[4 * side : 4 * side + 4]]
        logits = (own4[0] + own4[1]) + (own4[2] + own4[3])
        down = logits - jnp.max(logits, axis=-1, keepdims=True)
        log_all = down - jnp.log(jnp.sum(jnp.exp(down), axis=-1, keepdims=True))
        picked = (bins == act).astype(F32)
        lp = jnp.sum(picked * log_all, axis=-1, keepdims=True)
        lp_ref[c] = jnp.broadcast_to(lp, lp_ref.shape[1:])
        grad = (weight * (picked - jnp.exp(log_all))).astype(BF16)
        lg_ref[c] = grad
        size = column(here, 2)
        for half, ref in enumerate((hw_ref, other_ref)):
            back = lax.dot_general(
                grad, ref[...], (((1,), (1,)), ((), ())), preferred_element_type=F32
            )
            pool = jnp.sum(back, axis=0, keepdims=True) / size
            place = at_ref[1] if half == 0 else 1 - at_ref[1]
            lanes = pl.ds(pl.multiple_of(place * COLS, COLS), COLS)
            scale_ref[c, :, lanes] = jnp.broadcast_to(pool, (8, COLS))


def logit_parts(at, *operands):
    return pl.pallas_call(
        logit_kernel,
        out_shape=(
            jax.ShapeDtypeStruct((2, 8, 128), F32),
            jax.ShapeDtypeStruct((2, 8, NBINS), BF16),
            jax.ShapeDtypeStruct((2, 8, HID_HERE), F32),
        ),
        in_specs=[SMEM] + [VMEM] * 12,
        out_specs=(VMEM, VMEM, VMEM),
        compiler_params=local(),
        cost_estimate=cost(8 << 20, 1 << 20, 8192),
        name="logit",
    )(at, *operands)


def scale_kernel(core_ref, keep_ref, got_ref, scale_ref, head_ref, lg_ref, o_ref):
    core = core_ref[0]
    mine = scale_ref[core][0:1]
    other = scale_ref[1 - core][0:1]
    lower = jnp.concatenate([lg_ref[core].astype(F32), jnp.zeros((8, NBINS), F32)], axis=1)
    for b in range(2):
        for x in range(2):
            cols = slice(x * COLS, (x + 1) * COLS)
            top = (
                keep_ref[b, x].astype(F32) * mine[:, cols]
                + got_ref[b, x].astype(F32) * other[:, cols]
            )
            o_ref[b, x] = jnp.concatenate(
                [top, head_ref[:, cols].astype(F32), lower], axis=0
            ).astype(BF16)


def scaled(core, keep, got, scale, head_input, lgrad):
    spec = pl.BlockSpec((2, 2, ROWS, COLS), lambda i, n: (i, 0, 0, 0))
    return pl.pallas_call(
        scale_kernel,
        out_shape=jax.ShapeDtypeStruct((8, 2, ROWS + 16, COLS), BF16),
        grid_spec=pltpu.PrefetchScalarGridSpec(
            num_scalar_prefetch=1,
            grid=(4,),
            in_specs=[
                spec,
                spec,
                pl.BlockSpec((2, 8, HID_HERE), lambda i, n: (0, 0, 0)),
                pl.BlockSpec((8, HID_HERE), lambda i, n: (0, 0)),
                pl.BlockSpec((2, 8, NBINS), lambda i, n: (0, 0, 0)),
            ],
            out_specs=pl.BlockSpec((2, 2, ROWS + 16, COLS), lambda i, n: (i, 0, 0, 0)),
        ),
        compiler_params=params(limit=SMALL),
        cost_estimate=cost(8 << 20, 7 << 20),
        name="scaled",
    )(core, keep, got, scale, head_input, lgrad)


def episode_facts(lengths, actions, action_mask, group_ids, rewards):
    three = jnp.stack([rewards, group_ids.astype(F32), lengths.astype(F32)], axis=1)
    return jnp.concatenate(
        [
            jnp.pad(three, ((0, 0), (0, 5))),
            jnp.pad(actions.astype(F32), ((0, 0), (0, 1))),
            jnp.pad(action_mask.astype(F32), ((0, 0), (0, 105))),
        ],
        axis=1,
    )


def per_device(
    queries,
    keys,
    values,
    lengths,
    frame_map,
    proj_weight,
    head_weight,
    act_embed,
    actions,
    action_mask,
    group_ids,
    rewards,
):
    xh = lax.axis_index("xh")
    y = lax.axis_index("y")
    z = lax.axis_index("z")
    xl = lax.axis_index("xl")
    core = lax.axis_index("c")
    core1 = core.reshape(1)
    length = lax.dynamic_slice_in_dim(lengths, xh, 1)

    got = dealt(pack(queries, keys, values), ("xh", "y"))

    x = xh * 2 + xl
    line = ("xh", "xl")
    row = [proj_weight] + [shifted(proj_weight, "z", by) for by in (1, -1, 2)]
    z_order = (z + jnp.array([0, 3, 1, 2], jnp.int32)) % 4
    block = jnp.stack(row)
    up, down = shifted(block, line, 1), shifted(block, line, -1)
    half = shifted(up, line, 1)
    x_order = (x + jnp.array([0, 3, 1, 2], jnp.int32)) % 4
    own = (block, up, down, half)
    other = [shifted(w, "c", 1) for w in own]
    weight = assemble(z_order, x_order, core1, own, other)

    first = xh == 0
    hw_other, ae_other = shifted(head_weight, "xh", 1), shifted(act_embed, "xh", 1)

    def both(mine, other, axis):
        return jnp.concatenate(
            [jnp.where(first, mine, other), jnp.where(first, other, mine)], axis=axis
        )

    facts = episode_facts(lengths, actions, action_mask, group_ids, rewards)
    facts = jnp.concatenate([facts, shifted(facts, "c", 1)])
    facts = jnp.concatenate([facts] + [shifted(facts, "z", by) for by in (1, 2, 3)])
    far_facts = shifted(facts, "xl", 1)
    places = jnp.stack([core, xh]).astype(jnp.int32)
    where = jnp.concatenate([length, xh.reshape(1)])
    idx = (y + jnp.array([0, 3, 1, 2], jnp.int32)) % 4
    a0 = attend(got, where, 0, (facts, idx, z_order, x_order, places, core1))
    a1, held_map = attend(got, where, 1, (frame_map,))
    b0 = shifted(a0, "y", 1)
    c0 = shifted(a0, "y", -1)
    b1 = shifted(a1, "y", 1)
    c1 = shifted(a1, "y", -1)
    d0 = shifted(b0, "y", 1)
    d1 = shifted(c1, "y", -1)

    frames0, slope0, pool0 = chunk_of(idx, where, (a0, b0, c0, d0), held_map, weight, 0, ())
    frames1, slope1, head_input, part = chunk_of(
        idx,
        where,
        (a1, b1, c1, d1),
        held_map,
        weight,
        1,
        (pool0, act_embed, ae_other, head_weight, hw_other),
    )
    near = [part] + [shifted(part, "y", by) for by in (2, 1, 3)]
    far = [across(part, by) for by in (0, 2, 1, 3)]
    keep, send = grad_of(core1, frames0, slope0, frames1, slope1)
    arrived = shifted(send, "c", 1)

    logprob, lgrad, scale = logit_parts(
        places, *near, *far, facts, far_facts, head_weight, hw_other
    )
    summed = scaled(core1, keep, arrived, scale, head_input, lgrad)
    dealt_out = dealt(summed.reshape(16, ROWS + 16, COLS), ("z", "xl", "xh"))
    grad_proj = jnp.sum(dealt_out[:, :ROWS].astype(F32), axis=0).astype(BF16)

    own_head = dealt_out[:, ROWS:]
    other_head = shifted(own_head, "c", 1)
    heads = jnp.stack([own_head, other_head])
    lefts = heads[:, :, :8].reshape(256, COLS)
    rights = heads[:, :, 8:, :NBINS].reshape(256, NBINS)
    grad_head = lax.dot_general(
        lefts, rights, (((0,), (0,)), ((), ())), preferred_element_type=F32
    ).astype(BF16)

    lp_mine = lax.dynamic_index_in_dim(logprob[:, :7, 0], core, 0)
    lp_other = shifted(lp_mine, "xh", 1)
    logprobs = both(lp_mine, lp_other, 0)
    return logprobs, grad_proj, grad_head


def solution(mesh):
    fine = Mesh(mesh.devices.reshape(2, 4, 4, 2, 2), ("xh", "y", "z", "xl", "c"))
    cp, grp = ("xh", "y"), ("z", "xl", "c")
    in_specs = (
        P(grp, cp, None),
        P(grp, cp, None),
        P(grp, cp, None),
        P(grp),
        P(),
        P(grp, cp),
        P(cp, None),
        P(None, cp),
        P(grp, None),
        P(grp, None),
        P(grp),
        P(grp),
    )
    out_specs = (P(grp, None), P(grp, cp), P(cp, None))
    return jax.shard_map(
        per_device, mesh=fine, in_specs=in_specs, out_specs=out_specs, check_vma=False
    )
```

time: 243 us -> 201 us (0.83)
  Pallas kernels: 73.2 us -> 45.5 us
  local copies, waits for them, and re-layouts: 7.96 us -> 1.25 us
  other arithmetic: 10.2 us -> 4.46 us
  waiting for transfers between devices: 91.2 us -> 86.4 us
  starting transfers between devices: 56.1 us -> 59.7 us
    pallas_call x5, Pallas kernels: 56.8 us -> 34.9 us  [the longest x2 19 us: chunk_of(): pl.pallas_call(functools.partial(chunk_kernel, chunk), out_shape=tuple(sh...]
    all_to_all x4 -> x2, starting transfers between devices: 24.8 us -> 14.1 us  [dealt(): return lax.all_to_all(x, axes, 0, 0, tiled=True)]
    ppermute x22 -> x29, starting transfers between devices: 31.3 us -> 40.1 us  [shifted(): return lax.ppermute(x, axis, [(i, (i + by) % count) for i in range(count)])]
    all_to_all x4 -> x2, waiting for transfers between devices: 6.25 us -> 0.01 us  [dealt(): return lax.all_to_all(x, axes, 0, 0, tiled=True)]
    ppermute x0 -> x4, starting transfers between devices: none -> 5.5 us  [across(): return lax.ppermute(x, ('y', 'c'), pairs)]
    slice x2 -> x0, local copies, waits for them, and re-layouts: 2.67 us -> none  [the longest x1 1.7 us: per_device(): up[:2]]
    ppermute x22 -> x29, waiting for transfers between devices: 84.9 us -> 85.1 us  [shifted(): return lax.ppermute(x, axis, [(i, (i + by) % count) for i in range(count)])]
  transfers between devices with their start and end apart: 26 -> 35, of which waited for: 9 -> 10; matrix products, arithmetic and copies ran while one was open for 7% -> 3% of each run, Pallas kernels for 16% -> 12%
where the time goes in v2:
time: 201 us; the launch traced here: 199 us
  waiting for transfers between devices  86.4 us (43%)
  starting transfers between devices  59.7 us (30%)
  Pallas kernels  45.5 us (23%)
  other arithmetic  4.46 us (2%)
    ppermute x29, waiting for transfers between devices, shifted(): return lax.ppermute(x, axis, [(i, (i + by) % count) for i in range(count)])  85.1 us
    ppermute x29, starting transfers between devices, shifted(): return lax.ppermute(x, axis, [(i, (i + by) % count) for i in range(count)])  40.1 us
    pallas_call x2, Pallas kernels, chunk_of(): pl.pallas_call(functools.partial(chunk_kernel, chunk), out_shape=tuple(sh...  19 us
    all_to_all x2, starting transfers between devices, dealt(): return lax.all_to_all(x, axes, 0, 0, tiled=True)  14.1 us
    pallas_call x2, Pallas kernels, attend(): pl.pallas_call(functools.partial(attend_kernel, chunk), out_shape=(out, h...  10.2 us
    pallas_call x1, Pallas kernels, grad_of(): pl.pallas_call(grad_kernel, out_shape=(out, out), in_specs=[SMEM] + [VMEM...  5.68 us
    ppermute x4, starting transfers between devices, across(): return lax.ppermute(x, ('y', 'c'), pairs)  5.5 us
    pallas_call x1, Pallas kernels, pack(): pl.pallas_call(pack_kernel, out_shape=jax.ShapeDtypeStruct((8, 3, 128, CO...  4.19 us
  transfers between devices with their start and end apart: 35, of which 10 were waited for; matrix products, arithmetic and copies ran while one was open for 3% of the time, Pallas kernels for 12%

profile of v2, /device:TPU:1, one launch (start us, length us, event | category | flops | bytes accessed | tf_op | source)
XLA Modules:
  0.0 199.2 jit_solution(9350404591282840851)
XLA Ops:
  0.6 4.2 %pack.1 = bf16[8,3,128,512]{3,2,1,0:T(8,128)(2,1)} custom-call(bf16[2,128,2048]{2,1,0:T(8,128)(2,1)} %q_ref.1, bf16[2,128,2048]{2,1,0:T(8,128)(2,1)} %k_ref.1, bf16[2,128,2048]{2,1,0:T(8,128)(2,1)} %v_ref.1), custom_call_target="tpu_custom_call" | custom-call | bytes 6291456 | tf_op jit(solution)/shard_map/pack/pallas_call | solution.py:71
  4.9 7.6 %all-to-all-start = ((bf16[8,3,128,512]{3,2,1,0:T(8,128)(2,1)}), bf16[8,3,128,512]{3,2,1,0:T(8,128)(2,1)S(1)}, u32[]{:S(2)}, u32[]{:S(2)}) async-start(bf16[8,3,128,512]{3,2,1,0:T(8,128)(2,1)} %pack.1), calls=%async_computation | async-start | bytes 6291456 | tf_op jit(solution)/shard_map/all_to_all | solution.py:60
  12.5 1.7 collective-permute-start.3
  14.2 2.2 %collective-permute-start.4 = (bf16[136,512]{1,0:T(8,128)(2,1)S(1)}, bf16[136,512]{1,0:T(8,128)(2,1)}, u32[]{:S(2)}, u32[]{:S(2)}) collective-permute-start(bf16[136,512]{1,0:T(8,128)(2,1)S(1)} %copy-done.2), channel_id=1, source_target_pairs={{0,12},{4,0},{8,4},{12,8},{1,13},{5,1},{9,5},{13,9},{2,14},{6,2},{... | collective-permute-start | bytes 417800 | tf_op jit(solution)/shard_map/ppermute | solution.py:51
  16.4 1.2 collective-permute-start.5
  18.0 1.4 collective-permute-done.3
  19.4 4.3 %collective-permute-done.5 = bf16[136,512]{1,0:T(8,128)(2,1)} collective-permute-done((bf16[136,512]{1,0:T(8,128)(2,1)S(1)}, bf16[136,512]{1,0:T(8,128)(2,1)}, u32[]{:S(2)}, u32[]{:S(2)}) %collective-permute-start.5) | collective-permute-done | bytes 139296 | tf_op jit(solution)/shard_map/ppermute | solution.py:51
  23.7 1.9 pad_maximum_fusion.refs_0_
  25.9 1.8 collective-permute-start.13
  28.4 0.7 pad_add_fusion.1.len_ref
  29.2 0.9 collective-permute-start.14
  30.0 1.9 collective-permute-start.15
  32.5 2.4 %collective-permute-start.7 = (bf16[4,136,512]{2,1,0:T(8,128)(2,1)}, bf16[4,136,512]{2,1,0:T(8,128)(2,1)}, u32[]{:S(2)}, u32[]{:S(2)}) collective-permute-start(bf16[4,136,512]{2,1,0:T(8,128)(2,1)} %pad_maximum_fusion.refs_0_), channel_id=1, source_target_pairs={{0,66},{2,0},{64,2},{66,64},{1,67},{3,1},{65,3},{67,65},{4,70},{6,... | collective-permute-start | bytes 1671176 | tf_op jit(solution)/shard_map/ppermute | solution.py:51
  34.9 27.8 %collective-permute-done.6.refs_1_ = bf16[4,136,512]{2,1,0:T(8,128)(2,1)} collective-permute-done((bf16[4,136,512]{2,1,0:T(8,128)(2,1)}, bf16[4,136,512]{2,1,0:T(8,128)(2,1)}, u32[]{:S(2)}, u32[]{:S(2)}) %collective-permute-start.6) | collective-permute-done | bytes 557088 | tf_op jit(solution)/shard_map/ppermute | solution.py:51
  63.4 5.1 %attend.3.a_ref = bf16[512,512]{1,0:T(8,128)(2,1)S(1)} custom-call(s32[2]{0:T(128)S(1)} %pad_add_fusion.1.len_ref, bf16[8,3,128,512]{3,2,1,0:T(8,128)(2,1)S(1)} %all-to-all-done.got_ref, f32[16,128]{1,0:T(8,128)S(1)} %concatenate.19.rest_0_.refs_8_, s32[4]{0:T(128)S(1)} %get-tuple-element.36.rest_1_.idx_ref, s32[4]{0:T(128)S(1)} %get-tuple-element.37.z_ref.rest_2_, ...), custom_call_target="tpu_custom_call" | custom-call | flops 1073741824 | bytes 3145728 | tf_op jit(solution)/shard_map/attend/pallas_call | solution.py:116
  68.6 1.2 collective-permute-start.17
  69.8 0.7 collective-permute-start.11
  70.5 7.4 %collective-permute-done.8.refs_3_ = bf16[4,136,512]{2,1,0:T(8,128)(2,1)} collective-permute-done((bf16[4,136,512]{2,1,0:T(8,128)(2,1)}, bf16[4,136,512]{2,1,0:T(8,128)(2,1)}, u32[]{:S(2)}, u32[]{:S(2)}) %collective-permute-start.8) | collective-permute-done | bytes 557088 | tf_op jit(solution)/shard_map/ppermute | solution.py:51
  77.9 1.3 collective-permute-start.12
  79.2 5.1 %attend.2 = (bf16[512,512]{1,0:T(8,128)(2,1)S(1)}, bf16[2048,2176]{1,0:T(8,128)(2,1)S(1)}) custom-call(s32[2]{0:T(128)S(1)} %pad_add_fusion.1.len_ref, bf16[8,3,128,512]{3,2,1,0:T(8,128)(2,1)S(1)} %all-to-all-done.got_ref, bf16[2048,2176]{1,0:T(8,128)(2,1)} %rest_0_.1), custom_call_target="tpu_custom_call" | custom-call | flops 1073741824 | bytes 3145728 | tf_op jit(solution)/shard_map/attend/pallas_call | solution.py:116
  84.3 2.4 %collective-permute-start.18 = (bf16[512,512]{1,0:T(8,128)(2,1)S(1)}, bf16[512,512]{1,0:T(8,128)(2,1)S(1)}, u32[]{:S(2)}, u32[]{:S(2)}) collective-permute-start(bf16[512,512]{1,0:T(8,128)(2,1)S(1)} %attend.3.a_ref), channel_id=1, source_target_pairs={{0,48},{16,0},{32,16},{48,32},{1,49},{17,1},{33,17},{49,33},{2,50}... | collective-permute-start | bytes 1572872 | tf_op jit(solution)/shard_map/ppermute | solution.py:51
  87.3 0.9 collective-permute-start.19
  88.2 3.0 %collective-permute-start.20 = (f32[7,512]{1,0:T(8,128)S(1)}, f32[7,512]{1,0:T(8,128)S(1)}, u32[]{:S(2)}, u32[]{:S(2)}) collective-permute-start(f32[7,512]{1,0:T(8,128)S(1)} %copy-done.1), channel_id=1, source_target_pairs={{0,64},{64,0},{1,65},{65,1},{2,66},{66,2},{3,67},{67,3},{4,68},{68... | collective-permute-start | bytes 43016 | tf_op jit(solution)/shard_map/ppermute | solution.py:51
  91.2 3.0 %assemble.1.w_ref = bf16[2176,1024]{1,0:T(8,128)(2,1)S(1)} custom-call(s32[4]{0:T(128)S(1)} %get-tuple-element.37.z_ref.rest_2_, s32[4]{0:T(128)S(1)} %get-tuple-element.35.x_ref.rest_3_, s32[1]{0:T(128)} %bitcast.core_ref.rest_5_, bf16[4,136,512]{2,1,0:T(8,128)(2,1)} %pad_maximum_fusion.refs_0_, bf16[4,136,512]{2,1,0:T(8,128)(2,1)} %collective-permute-done.6.refs_1_, ...), custom_call_target="tpu_custom_call" | custom-call | flops 1048576 | bytes 9437184 | tf_op jit(solution)/shard_map/assemble/pallas_call | solution.py:226
  94.1 3.9 %collective-permute-done.18.c_ref = bf16[512,512]{1,0:T(8,128)(2,1)S(1)} collective-permute-done((bf16[512,512]{1,0:T(8,128)(2,1)S(1)}, bf16[512,512]{1,0:T(8,128)(2,1)S(1)}, u32[]{:S(2)}, u32[]{:S(2)}) %collective-permute-start.18) | collective-permute-done | bytes 524320 | tf_op jit(solution)/shard_map/ppermute | solution.py:51
  98.0 1.0 collective-permute-start
  99.0 10.2 %collective-permute-done.1.c_ref = bf16[512,512]{1,0:T(8,128)(2,1)S(1)} collective-permute-done((bf16[512,512]{1,0:T(8,128)(2,1)S(1)}, bf16[512,512]{1,0:T(8,128)(2,1)S(1)}, u32[]{:S(2)}, u32[]{:S(2)}) %collective-permute-start.1) | collective-permute-done | bytes 524320 | tf_op jit(solution)/shard_map/ppermute | solution.py:51
  109.2 3.4 %collective-permute-start.2 = (bf16[512,512]{1,0:T(8,128)(2,1)S(1)}, bf16[512,512]{1,0:T(8,128)(2,1)S(1)}, u32[]{:S(2)}, u32[]{:S(2)}) collective-permute-start(bf16[512,512]{1,0:T(8,128)(2,1)S(1)} %collective-permute-done.1.c_ref), channel_id=1, source_target_pairs={{0,48},{16,0},{32,16},{48,32},{1,49},{17,1},{33,17},{49,33},{2,50}... | collective-permute-start | bytes 1572872 | tf_op jit(solution)/shard_map/ppermute | solution.py:51
  112.7 9.5 %chunk.2 = (bf16[512,2176]{1,0:T(8,128)(2,1)S(1)}, bf16[512,1024]{1,0:T(8,128)(2,1)S(1)}, f32[8,1024]{1,0:T(8,128)S(1)}) custom-call(s32[4]{0:T(128)S(1)} %get-tuple-element.36.rest_1_.idx_ref, s32[2]{0:T(128)S(1)} %pad_add_fusion.1.len_ref, bf16[512,512]{1,0:T(8,128)(2,1)S(1)} %attend.3.a_ref, bf16[512,512]{1,0:T(8,128)(2,1)S(1)} %collective-permute-done.17.b_ref, ...), custom_call_target="tpu_custom_call" | custom-call | flops 6845104128 | bytes 20971520 | tf_op jit(solution)/shard_map/chunk/pallas_call | solution.py:198
  122.2 0.9 collective-permute-done.2.d_ref
  123.1 9.5 %chunk.3 = (bf16[512,2176]{1,0:T(8,128)(2,1)S(1)}, bf16[512,1024]{1,0:T(8,128)(2,1)S(1)}, bf16[8,1024]{1,0:T(8,128)(2,1)S(1)}, f32[8,256]{1,0:T(8,128)S(1)}) custom-call(s32[4]{0:T(128)S(1)} %get-tuple-element.36.rest_1_.idx_ref, s32[2]{0:T(128)S(1)} %pad_add_fusion.1.len_ref, bf16[512,512]{1,0:T(8,128)(2,1)S(1)} %get-tuple-element.17.a_ref, ...), custom_call_target="tpu_custom_call" | custom-call | flops 6845104128 | bytes 20971520 | tf_op jit(solution)/shard_map/chunk/pallas_call | solution.py:198
  132.6 5.7 %grad.1 = (bf16[8,2,136,512]{3,2,1,0:T(8,128)(2,1)S(1)}, bf16[8,2,136,512]{3,2,1,0:T(8,128)(2,1)S(1)}) custom-call(s32[1]{0:T(128)} %bitcast.core_ref.rest_5_, bf16[512,2176]{1,0:T(8,128)(2,1)S(1)} %get-tuple-element.22.f0_ref, bf16[512,1024]{1,0:T(8,128)(2,1)S(1)} %get-tuple-element.23.s0_ref, bf16[512,2176]{1,0:T(8,128)(2,1)S(1)} %get-tuple-element.24.f1_ref, ...), custom_call_target="tpu_custom_call" | custom-call | flops 4563402752 | bytes 11534336 | tf_op jit(solution)/shard_map/grad/pallas_call | solution.py:260
  138.3 2.0 %collective-permute-start.31 = (bf16[8,2,136,512]{3,2,1,0:T(8,128)(2,1)S(1)}, bf16[8,2,136,512]{3,2,1,0:T(8,128)(2,1)S(1)}, u32[]{:S(2)}, u32[]{:S(2)}) collective-permute-start(bf16[8,2,136,512]{3,2,1,0:T(8,128)(2,1)S(1)} %get-tuple-element.27), channel_id=1, source_target_pairs={{0,1},{1,0},{2,3},{3,2},{4,5},{5,4},{6,7},{7,6},{8,9},{9,8},{10,11... | collective-permute-start | bytes 6684680 | tf_op jit(solution)/shard_map/ppermute | solution.py:51
  140.3 1.9 collective-permute-start.22
  142.2 2.1 %collective-permute-start.23 = (f32[8,256]{1,0:T(8,128)S(1)}, f32[8,256]{1,0:T(8,128)S(1)}, u32[]{:S(2)}, u32[]{:S(2)}) collective-permute-start(f32[8,256]{1,0:T(8,128)S(1)} %get-tuple-element.20.refs_0_), channel_id=1, source_target_pairs={{0,16},{16,32},{32,48},{48,0},{1,17},{17,33},{33,49},{49,1},{2,18}... | collective-permute-start | bytes 24584 | tf_op jit(solution)/shard_map/ppermute | solution.py:51
  144.9 1.0 collective-permute-start.25
  145.9 1.5 collective-permute-start.26
  147.5 1.1 collective-permute-start.27
  148.6 1.8 collective-permute-start.28
  150.5 1.2 collective-permute-done.27.refs_6_
  151.8 1.1 logit.1
  152.8 2.4 %scaled.1 = bf16[8,2,152,512]{3,2,1,0:T(8,128)(2,1)} custom-call(s32[1]{0:T(128)} %bitcast.core_ref.rest_5_, bf16[8,2,136,512]{3,2,1,0:T(8,128)(2,1)S(1)} %get-tuple-element.26.keep_ref, bf16[8,2,136,512]{3,2,1,0:T(8,128)(2,1)S(1)} %collective-permute-done.31.got_ref, f32[2,8,1024]{2,1,0:T(8,128)S(1)} %get-tuple-element.28.scale_ref, ...), custom_call_target="tpu_custom_call" | custom-call | flops 8388608 | bytes 7340032 | tf_op jit(solution)/shard_map/scaled/pallas_call | solution.py:360
  155.2 6.5 %all-to-all-start.1 = ((bf16[16,152,512]{2,1,0:T(8,128)(2,1)}), bf16[16,152,512]{2,1,0:T(8,128)(2,1)S(1)}, u32[]{:S(2)}, u32[]{:S(2)}) async-start(bf16[16,152,512]{2,1,0:T(8,128)(2,1)} %bitcast.9), calls=%async_computation.1 | async-start | bytes 4980736 | tf_op jit(solution)/shard_map/all_to_all | solution.py:60
  161.8 2.9 %collective-permute-start.30 = (f32[1,7]{1,0:T(1,128)S(1)}, f32[1,7]{1,0:T(1,128)S(1)}, u32[]{:S(2)}, u32[]{:S(2)}) collective-permute-start(f32[1,7]{1,0:T(1,128)S(1)} %bitcast.30), channel_id=1, source_target_pairs={{0,64},{64,0},{1,65},{65,1},{2,66},{66,2},{3,67},{67,3},{4,68},{68... | collective-permute-start | bytes 92 | tf_op jit(solution)/shard_map/ppermute | solution.py:51
  164.8 29.2 %collective-permute-done.30 = f32[1,7]{1,0:T(1,128)S(1)} collective-permute-done((f32[1,7]{1,0:T(1,128)S(1)}, f32[1,7]{1,0:T(1,128)S(1)}, u32[]{:S(2)}, u32[]{:S(2)}) %collective-permute-start.30) | collective-permute-done | bytes 60 | tf_op jit(solution)/shard_map/ppermute | solution.py:51
  194.2 2.4 %collective-permute-start.32 = (bf16[16,16,512]{2,0,1:T(8,128)(2,1)S(1)}, bf16[16,16,512]{2,0,1:T(8,128)(2,1)S(1)}, u32[]{:S(2)}, u32[]{:S(2)}) collective-permute-start(bf16[16,16,512]{2,0,1:T(8,128)(2,1)S(1)} %copy.34), channel_id=1, source_target_pairs={{0,1},{1,0},{2,3},{3,2},{4,5},{5,4},{6,7},{7,6},{8,9},{9,8},{10,11... | collective-permute-start | bytes 786440 | tf_op jit(solution)/shard_map/ppermute | solution.py:51
  197.2 1.0 slice_reduce_fusion
  198.2 1.0 fusion
  (74 shorter events, 5.1 us)
Async XLA Ops:
  4.8 7.7 %copy-start.2 = (bf16[136,512]{1,0:T(8,128)(2,1)S(1)}, bf16[136,512]{1,0:T(8,128)(2,1)}, u32[]{:S(2)}) copy-start(bf16[136,512]{1,0:T(8,128)(2,1)} %param.20) | copy-start | bytes 417796
  4.8 12.8 %copy-start.6 = (s32[2]{0:T(128)S(1)}, s32[2]{0:T(128)}, u32[]{:S(2)}) copy-start(s32[2]{0:T(128)} %param.25) | copy-start | bytes 28
  4.8 12.8 %copy-start.8 = (s32[2]{0:T(128)S(1)}, s32[2]{0:T(128)}, u32[]{:S(2)}) copy-start(s32[2]{0:T(128)} %param.18) | copy-start | bytes 28
  4.8 13.0 %copy-start.7 = (f32[2]{0:T(128)S(1)}, f32[2]{0:T(128)}, u32[]{:S(2)}) copy-start(f32[2]{0:T(128)} %param.26) | copy-start | bytes 28
  4.8 13.1 %copy-start.3 = (s32[2,7]{1,0:T(2,128)S(1)}, s32[2,7]{1,0:T(2,128)}, u32[]{:S(2)}) copy-start(s32[2,7]{1,0:T(2,128)} %param.23) | copy-start | bytes 172
  4.9 13.1 %copy-start.4 = (s32[2,7]{1,0:T(2,128)S(1)}, s32[2,7]{1,0:T(2,128)}, u32[]{:S(2)}) copy-start(s32[2,7]{1,0:T(2,128)} %param.24) | copy-start | bytes 172
  4.9 23.5 %copy-start.5 = (s32[4]{0:T(128)S(1)}, s32[4]{0:T(128)}, u32[]{:S(2)}) copy-start(s32[4]{0:T(128)} %constant.59.clone) | copy-start | bytes 52
  4.9 58.6 %all-to-all-start = ((bf16[8,3,128,512]{3,2,1,0:T(8,128)(2,1)}), bf16[8,3,128,512]{3,2,1,0:T(8,128)(2,1)S(1)}, u32[]{:S(2)}, u32[]{:S(2)}) async-start(bf16[8,3,128,512]{3,2,1,0:T(8,128)(2,1)} %pack.1), calls=%async_computation | async-start | bytes 6291456 | tf_op jit(solution)/shard_map/all_to_all | solution.py:60
  12.5 6.9 %collective-permute-start.3 = (bf16[136,512]{1,0:T(8,128)(2,1)S(1)}, bf16[136,512]{1,0:T(8,128)(2,1)S(1)}, u32[]{:S(2)}, u32[]{:S(2)}) collective-permute-start(bf16[136,512]{1,0:T(8,128)(2,1)S(1)} %copy-done.2), channel_id=1, source_target_pairs={{0,4},{4,8},{8,12},{12,0},{1,5},{5,9},{9,13},{13,1},{2,6},{6,10},{... | collective-permute-start | bytes 417800 | tf_op jit(solution)/shard_map/ppermute | solution.py:51
  14.2 5.2 %collective-permute-start.4 = (bf16[136,512]{1,0:T(8,128)(2,1)S(1)}, bf16[136,512]{1,0:T(8,128)(2,1)}, u32[]{:S(2)}, u32[]{:S(2)}) collective-permute-start(bf16[136,512]{1,0:T(8,128)(2,1)S(1)} %copy-done.2), channel_id=1, source_target_pairs={{0,12},{4,0},{8,4},{12,8},{1,13},{5,1},{9,5},{13,9},{2,14},{6,2},{... | collective-permute-start | bytes 417800 | tf_op jit(solution)/shard_map/ppermute | solution.py:51
  16.4 7.3 %collective-permute-start.5 = (bf16[136,512]{1,0:T(8,128)(2,1)S(1)}, bf16[136,512]{1,0:T(8,128)(2,1)}, u32[]{:S(2)}, u32[]{:S(2)}) collective-permute-start(bf16[136,512]{1,0:T(8,128)(2,1)S(1)} %copy-done.2), channel_id=1, source_target_pairs={{0,8},{4,12},{8,0},{12,4},{1,9},{5,13},{9,1},{13,5},{2,10},{6,14},... | collective-permute-start | bytes 417800 | tf_op jit(solution)/shard_map/ppermute | solution.py:51
  25.6 37.1 %collective-permute-start.6 = (bf16[4,136,512]{2,1,0:T(8,128)(2,1)}, bf16[4,136,512]{2,1,0:T(8,128)(2,1)}, u32[]{:S(2)}, u32[]{:S(2)}) collective-permute-start(bf16[4,136,512]{2,1,0:T(8,128)(2,1)} %pad_maximum_fusion.refs_0_), channel_id=1, source_target_pairs={{0,2},{2,64},{64,66},{66,0},{1,3},{3,65},{65,67},{67,1},{4,6},{6,6... | collective-permute-start | bytes 1671176 | tf_op jit(solution)/shard_map/ppermute | solution.py:51
  25.9 3.1 %collective-permute-start.13 = (f32[2,128]{1,0:T(2,128)S(1)}, f32[2,128]{1,0:T(2,128)S(1)}, u32[]{:S(2)}, u32[]{:S(2)}) collective-permute-start(f32[2,128]{1,0:T(2,128)S(1)} %pad_maximum_fusion.2), channel_id=1, source_target_pairs={{0,1},{1,0},{2,3},{3,2},{4,5},{5,4},{6,7},{7,6},{8,9},{9,8},{10,11... | collective-permute-start | bytes 3080 | tf_op jit(solution)/shard_map/ppermute | solution.py:51
  29.2 33.6 %collective-permute-start.14 = (f32[4,128]{1,0:T(4,128)S(1)}, f32[4,128]{1,0:T(4,128)S(1)}, u32[]{:S(2)}, u32[]{:S(2)}) collective-permute-start(f32[4,128]{1,0:T(4,128)S(1)} %pad_maximum_fusion.1), channel_id=1, source_target_pairs={{0,4},{4,8},{8,12},{12,0},{1,5},{5,9},{9,13},{13,1},{2,6},{6,10},{... | collective-permute-start | bytes 6152 | tf_op jit(solution)/shard_map/ppermute | solution.py:51
  30.0 32.7 %collective-permute-start.15 = (f32[4,128]{1,0:T(4,128)S(1)}, f32[4,128]{1,0:T(4,128)S(1)}, u32[]{:S(2)}, u32[]{:S(2)}) collective-permute-start(f32[4,128]{1,0:T(4,128)S(1)} %pad_maximum_fusion.1), channel_id=1, source_target_pairs={{0,8},{4,12},{8,0},{12,4},{1,9},{5,13},{9,1},{13,5},{2,10},{6,14},... | collective-permute-start | bytes 6152 | tf_op jit(solution)/shard_map/ppermute | solution.py:51
  31.9 30.8 %collective-permute-start.16 = (f32[4,128]{1,0:T(4,128)S(1)}, f32[4,128]{1,0:T(4,128)S(1)}, u32[]{:S(2)}, u32[]{:S(2)}) collective-permute-start(f32[4,128]{1,0:T(4,128)S(1)} %pad_maximum_fusion.1), channel_id=1, source_target_pairs={{0,12},{4,0},{8,4},{12,8},{1,13},{5,1},{9,5},{13,9},{2,14},{6,2},{... | collective-permute-start | bytes 6152 | tf_op jit(solution)/shard_map/ppermute | solution.py:51
  32.5 37.2 %collective-permute-start.7 = (bf16[4,136,512]{2,1,0:T(8,128)(2,1)}, bf16[4,136,512]{2,1,0:T(8,128)(2,1)}, u32[]{:S(2)}, u32[]{:S(2)}) collective-permute-start(bf16[4,136,512]{2,1,0:T(8,128)(2,1)} %pad_maximum_fusion.refs_0_), channel_id=1, source_target_pairs={{0,66},{2,0},{64,2},{66,64},{1,67},{3,1},{65,3},{67,65},{4,70},{6,... | collective-permute-start | bytes 1671176 | tf_op jit(solution)/shard_map/ppermute | solution.py:51
  62.6 15.2 %collective-permute-start.8 = (bf16[4,136,512]{2,1,0:T(8,128)(2,1)}, bf16[4,136,512]{2,1,0:T(8,128)(2,1)}, u32[]{:S(2)}, u32[]{:S(2)}) collective-permute-start(bf16[4,136,512]{2,1,0:T(8,128)(2,1)} %collective-permute-done.6.refs_1_), channel_id=1, source_target_pairs={{0,2},{2,64},{64,66},{66,0},{1,3},{3,65},{65,67},{67,1},{4,6},{6,6... | collective-permute-start | bytes 1671176 | tf_op jit(solution)/shard_map/ppermute | solution.py:51
  62.8 21.5 %collective-permute-start.9 = (bf16[4,136,512]{2,1,0:T(8,128)(2,1)}, bf16[4,136,512]{2,1,0:T(8,128)(2,1)}, u32[]{:S(2)}, u32[]{:S(2)}) collective-permute-start(bf16[4,136,512]{2,1,0:T(8,128)(2,1)} %pad_maximum_fusion.refs_0_), channel_id=1, source_target_pairs={{0,1},{1,0},{2,3},{3,2},{4,5},{5,4},{6,7},{7,6},{8,9},{9,8},{10,11... | collective-permute-start | bytes 1671176 | tf_op jit(solution)/shard_map/ppermute | solution.py:51
  63.3 23.4 %collective-permute-start.10 = (bf16[4,136,512]{2,1,0:T(8,128)(2,1)}, bf16[4,136,512]{2,1,0:T(8,128)(2,1)}, u32[]{:S(2)}, u32[]{:S(2)}) collective-permute-start(bf16[4,136,512]{2,1,0:T(8,128)(2,1)} %collective-permute-done.6.refs_1_), channel_id=1, source_target_pairs={{0,1},{1,0},{2,3},{3,2},{4,5},{5,4},{6,7},{7,6},{8,9},{9,8},{10,11... | collective-permute-start | bytes 1671176 | tf_op jit(solution)/shard_map/ppermute | solution.py:51
  68.5 19.7 %copy-start = (bf16[512,256]{1,0:T(8,128)(2,1)S(1)}, bf16[512,256]{1,0:T(8,128)(2,1)}, u32[]{:S(2)}) copy-start(bf16[512,256]{1,0:T(8,128)(2,1)} %refs_10_.1) | copy-start | bytes 786436
  68.5 19.7 %copy-start.1 = (f32[7,512]{1,0:T(8,128)S(1)}, f32[7,512]{1,0:T(8,128)}, u32[]{:S(2)}) copy-start(f32[7,512]{1,0:T(8,128)} %rest_1_.1) | copy-start | bytes 43012
  68.6 18.8 %collective-permute-start.17 = (bf16[512,512]{1,0:T(8,128)(2,1)S(1)}, bf16[512,512]{1,0:T(8,128)(2,1)S(1)}, u32[]{:S(2)}, u32[]{:S(2)}) collective-permute-start(bf16[512,512]{1,0:T(8,128)(2,1)S(1)} %attend.3.a_ref), channel_id=1, source_target_pairs={{0,16},{16,32},{32,48},{48,0},{1,17},{17,33},{33,49},{49,1},{2,18}... | collective-permute-start | bytes 1572872 | tf_op jit(solution)/shard_map/ppermute | solution.py:51
  69.8 18.4 %collective-permute-start.11 = (bf16[4,136,512]{2,1,0:T(8,128)(2,1)}, bf16[4,136,512]{2,1,0:T(8,128)(2,1)S(1)}, u32[]{:S(2)}, u32[]{:S(2)}) collective-permute-start(bf16[4,136,512]{2,1,0:T(8,128)(2,1)} %collective-permute-done.7.refs_2_), channel_id=1, source_target_pairs={{0,1},{1,0},{2,3},{3,2},{4,5},{5,4},{6,7},{7,6},{8,9},{9,8},{10,11... | collective-permute-start | bytes 1671176 | tf_op jit(solution)/shard_map/ppermute | solution.py:51
  77.9 10.4 %collective-permute-start.12 = (bf16[4,136,512]{2,1,0:T(8,128)(2,1)}, bf16[4,136,512]{2,1,0:T(8,128)(2,1)S(1)}, u32[]{:S(2)}, u32[]{:S(2)}) collective-permute-start(bf16[4,136,512]{2,1,0:T(8,128)(2,1)} %collective-permute-done.8.refs_3_), channel_id=1, source_target_pairs={{0,1},{1,0},{2,3},{3,2},{4,5},{5,4},{6,7},{7,6},{8,9},{9,8},{10,11... | collective-permute-start | bytes 1671176 | tf_op jit(solution)/shard_map/ppermute | solution.py:51
  84.3 13.7 %collective-permute-start.18 = (bf16[512,512]{1,0:T(8,128)(2,1)S(1)}, bf16[512,512]{1,0:T(8,128)(2,1)S(1)}, u32[]{:S(2)}, u32[]{:S(2)}) collective-permute-start(bf16[512,512]{1,0:T(8,128)(2,1)S(1)} %attend.3.a_ref), channel_id=1, source_target_pairs={{0,48},{16,0},{32,16},{48,32},{1,49},{17,1},{33,17},{49,33},{2,50}... | collective-permute-start | bytes 1572872 | tf_op jit(solution)/shard_map/ppermute | solution.py:51
  86.7 22.5 %collective-permute-start.1 = (bf16[512,512]{1,0:T(8,128)(2,1)S(1)}, bf16[512,512]{1,0:T(8,128)(2,1)S(1)}, u32[]{:S(2)}, u32[]{:S(2)}) collective-permute-start(bf16[512,512]{1,0:T(8,128)(2,1)S(1)} %get-tuple-element.17.a_ref), channel_id=1, source_target_pairs={{0,48},{16,0},{32,16},{48,32},{1,49},{17,1},{33,17},{49,33},{2,50}... | collective-permute-start | bytes 1572872 | tf_op jit(solution)/shard_map/ppermute | solution.py:51
  87.3 25.3 %collective-permute-start.19 = (bf16[512,512]{1,0:T(8,128)(2,1)S(1)}, bf16[512,512]{1,0:T(8,128)(2,1)S(1)}, u32[]{:S(2)}, u32[]{:S(2)}) collective-permute-start(bf16[512,512]{1,0:T(8,128)(2,1)S(1)} %collective-permute-done.17.b_ref), channel_id=1, source_target_pairs={{0,16},{16,32},{32,48},{48,0},{1,17},{17,33},{33,49},{49,1},{2,18}... | collective-permute-start | bytes 1572872 | tf_op jit(solution)/shard_map/ppermute | solution.py:51
  88.2 34.0 %collective-permute-start.21 = (bf16[512,256]{1,0:T(8,128)(2,1)S(1)}, bf16[512,256]{1,0:T(8,128)(2,1)S(1)}, u32[]{:S(2)}, u32[]{:S(2)}) collective-permute-start(bf16[512,256]{1,0:T(8,128)(2,1)S(1)} %copy-done), channel_id=1, source_target_pairs={{0,64},{64,0},{1,65},{65,1},{2,66},{66,2},{3,67},{67,3},{4,68},{68... | collective-permute-start | bytes 786440 | tf_op jit(solution)/shard_map/ppermute | solution.py:51
  88.2 34.0 %collective-permute-start.20 = (f32[7,512]{1,0:T(8,128)S(1)}, f32[7,512]{1,0:T(8,128)S(1)}, u32[]{:S(2)}, u32[]{:S(2)}) collective-permute-start(f32[7,512]{1,0:T(8,128)S(1)} %copy-done.1), channel_id=1, source_target_pairs={{0,64},{64,0},{1,65},{65,1},{2,66},{66,2},{3,67},{67,3},{4,68},{68... | collective-permute-start | bytes 43016 | tf_op jit(solution)/shard_map/ppermute | solution.py:51
  98.0 24.2 %collective-permute-start = (bf16[512,512]{1,0:T(8,128)(2,1)S(1)}, bf16[512,512]{1,0:T(8,128)(2,1)S(1)}, u32[]{:S(2)}, u32[]{:S(2)}) collective-permute-start(bf16[512,512]{1,0:T(8,128)(2,1)S(1)} %get-tuple-element.17.a_ref), channel_id=1, source_target_pairs={{0,16},{16,32},{32,48},{48,0},{1,17},{17,33},{33,49},{49,1},{2,18}... | collective-permute-start | bytes 1572872 | tf_op jit(solution)/shard_map/ppermute | solution.py:51
  109.2 13.8 %collective-permute-start.2 = (bf16[512,512]{1,0:T(8,128)(2,1)S(1)}, bf16[512,512]{1,0:T(8,128)(2,1)S(1)}, u32[]{:S(2)}, u32[]{:S(2)}) collective-permute-start(bf16[512,512]{1,0:T(8,128)(2,1)S(1)} %collective-permute-done.1.c_ref), channel_id=1, source_target_pairs={{0,48},{16,0},{32,16},{48,32},{1,49},{17,1},{33,17},{49,33},{2,50}... | collective-permute-start | bytes 1572872 | tf_op jit(solution)/shard_map/ppermute | solution.py:51
  138.3 14.5 %collective-permute-start.31 = (bf16[8,2,136,512]{3,2,1,0:T(8,128)(2,1)S(1)}, bf16[8,2,136,512]{3,2,1,0:T(8,128)(2,1)S(1)}, u32[]{:S(2)}, u32[]{:S(2)}) collective-permute-start(bf16[8,2,136,512]{3,2,1,0:T(8,128)(2,1)S(1)} %get-tuple-element.27), channel_id=1, source_target_pairs={{0,1},{1,0},{2,3},{3,2},{4,5},{5,4},{6,7},{7,6},{8,9},{9,8},{10,11... | collective-permute-start | bytes 6684680 | tf_op jit(solution)/shard_map/ppermute | solution.py:51
  140.3 4.6 %collective-permute-start.29 = (f32[16,128]{1,0:T(8,128)S(1)}, f32[16,128]{1,0:T(8,128)S(1)}, u32[]{:S(2)}, u32[]{:S(2)}) collective-permute-start(f32[16,128]{1,0:T(8,128)S(1)} %concatenate.19.rest_0_.refs_8_), channel_id=1, source_target_pairs={{0,2},{2,0},{1,3},{3,1},{4,6},{6,4},{5,7},{7,5},{8,10},{10,8},{9,1... | collective-permute-start | bytes 24584 | tf_op jit(solution)/shard_map/ppermute | solution.py:51
  140.3 5.6 %collective-permute-start.22 = (f32[8,256]{1,0:T(8,128)S(1)}, f32[8,256]{1,0:T(8,128)S(1)}, u32[]{:S(2)}, u32[]{:S(2)}) collective-permute-start(f32[8,256]{1,0:T(8,128)S(1)} %get-tuple-element.20.refs_0_), channel_id=1, source_target_pairs={{0,32},{16,48},{32,0},{48,16},{1,33},{17,49},{33,1},{49,17},{2,34}... | collective-permute-start | bytes 24584 | tf_op jit(solution)/shard_map/ppermute | solution.py:51
  142.2 5.2 %collective-permute-start.23 = (f32[8,256]{1,0:T(8,128)S(1)}, f32[8,256]{1,0:T(8,128)S(1)}, u32[]{:S(2)}, u32[]{:S(2)}) collective-permute-start(f32[8,256]{1,0:T(8,128)S(1)} %get-tuple-element.20.refs_0_), channel_id=1, source_target_pairs={{0,16},{16,32},{32,48},{48,0},{1,17},{17,33},{33,49},{49,1},{2,18}... | collective-permute-start | bytes 24584 | tf_op jit(solution)/shard_map/ppermute | solution.py:51
  144.3 4.3 %collective-permute-start.24 = (f32[8,256]{1,0:T(8,128)S(1)}, f32[8,256]{1,0:T(8,128)S(1)}, u32[]{:S(2)}, u32[]{:S(2)}) collective-permute-start(f32[8,256]{1,0:T(8,128)S(1)} %get-tuple-element.20.refs_0_), channel_id=1, source_target_pairs={{0,48},{16,0},{32,16},{48,32},{1,49},{17,1},{33,17},{49,33},{2,50}... | collective-permute-start | bytes 24584 | tf_op jit(solution)/shard_map/ppermute | solution.py:51
  144.9 5.5 %collective-permute-start.25 = (f32[8,256]{1,0:T(8,128)S(1)}, f32[8,256]{1,0:T(8,128)S(1)}, u32[]{:S(2)}, u32[]{:S(2)}) collective-permute-start(f32[8,256]{1,0:T(8,128)S(1)} %get-tuple-element.20.refs_0_), channel_id=1, source_target_pairs={{0,1},{1,0},{16,17},{17,16},{32,33},{33,32},{48,49},{49,48},{2,3},... | collective-permute-start | bytes 24584 | tf_op jit(solution)/shard_map/ppermute | solution.py:56
  145.9 4.6 %collective-permute-start.26 = (f32[8,256]{1,0:T(8,128)S(1)}, f32[8,256]{1,0:T(8,128)S(1)}, u32[]{:S(2)}, u32[]{:S(2)}) collective-permute-start(f32[8,256]{1,0:T(8,128)S(1)} %get-tuple-element.20.refs_0_), channel_id=1, source_target_pairs={{0,33},{1,32},{16,49},{17,48},{32,1},{33,0},{48,17},{49,16},{2,35}... | collective-permute-start | bytes 24584 | tf_op jit(solution)/shard_map/ppermute | solution.py:56
  147.5 4.3 %collective-permute-start.27 = (f32[8,256]{1,0:T(8,128)S(1)}, f32[8,256]{1,0:T(8,128)S(1)}, u32[]{:S(2)}, u32[]{:S(2)}) collective-permute-start(f32[8,256]{1,0:T(8,128)S(1)} %get-tuple-element.20.refs_0_), channel_id=1, source_target_pairs={{0,17},{1,16},{16,33},{17,32},{32,49},{33,48},{48,1},{49,0},{2,19}... | collective-permute-start | bytes 24584 | tf_op jit(solution)/shard_map/ppermute | solution.py:56
  148.6 3.2 %collective-permute-start.28 = (f32[8,256]{1,0:T(8,128)S(1)}, f32[8,256]{1,0:T(8,128)S(1)}, u32[]{:S(2)}, u32[]{:S(2)}) collective-permute-start(f32[8,256]{1,0:T(8,128)S(1)} %get-tuple-element.20.refs_0_), channel_id=1, source_target_pairs={{0,49},{1,48},{16,1},{17,0},{32,17},{33,16},{48,33},{49,32},{2,51}... | collective-permute-start | bytes 24584 | tf_op jit(solution)/shard_map/ppermute | solution.py:56
  155.2 38.8 %all-to-all-start.1 = ((bf16[16,152,512]{2,1,0:T(8,128)(2,1)}), bf16[16,152,512]{2,1,0:T(8,128)(2,1)S(1)}, u32[]{:S(2)}, u32[]{:S(2)}) async-start(bf16[16,152,512]{2,1,0:T(8,128)(2,1)} %bitcast.9), calls=%async_computation.1 | async-start | bytes 4980736 | tf_op jit(solution)/shard_map/all_to_all | solution.py:60
  161.8 32.2 %collective-permute-start.30 = (f32[1,7]{1,0:T(1,128)S(1)}, f32[1,7]{1,0:T(1,128)S(1)}, u32[]{:S(2)}, u32[]{:S(2)}) collective-permute-start(f32[1,7]{1,0:T(1,128)S(1)} %bitcast.30), channel_id=1, source_target_pairs={{0,64},{64,0},{1,65},{65,1},{2,66},{66,2},{3,67},{67,3},{4,68},{68... | collective-permute-start | bytes 92 | tf_op jit(solution)/shard_map/ppermute | solution.py:51
  194.2 4.0 %collective-permute-start.32 = (bf16[16,16,512]{2,0,1:T(8,128)(2,1)S(1)}, bf16[16,16,512]{2,0,1:T(8,128)(2,1)S(1)}, u32[]{:S(2)}, u32[]{:S(2)}) collective-permute-start(bf16[16,16,512]{2,0,1:T(8,128)(2,1)S(1)} %copy.34), channel_id=1, source_target_pairs={{0,1},{1,0},{2,3},{3,2},{4,5},{5,4},{6,7},{7,6},{8,9},{9,8},{10,11... | collective-permute-start | bytes 786440 | tf_op jit(solution)/shard_map/ppermute | solution.py:51

commit v3 on v2

--- a/solution.py
+++ b/solution.py
@@ -49,11 +49,6 @@
 def shifted(x, axis, by):
     count = lax.axis_size(axis)
     return lax.ppermute(x, axis, [(i, (i + by) % count) for i in range(count)])
-
-
-def across(x, by):
-    pairs = [(2 * i + c, 2 * ((i + by) % 4) + 1 - c) for i in range(4) for c in range(2)]
-    return lax.ppermute(x, ("y", "c"), pairs)
 
 
 def dealt(x, axes):
@@ -214,7 +209,8 @@
         x = x_ref[k]
         col = pl.multiple_of((x // 2) * COLS, COLS)
         for i in range(4):
-            mine, other = refs[k][i].astype(F32), refs[4 + k][i].astype(F32)
+            ref, j = (k, i) if k < 3 else (3 + i // 2, i % 2)
+            mine, other = refs[ref][j].astype(F32), refs[5 + ref][j].astype(F32)
             pair = [jnp.where(lead, mine, other), jnp.where(lead, other, mine)]
             row = pl.multiple_of((z_ref[i] * 2 + x % 2) * 2 * ROWS, 2 * ROWS)
             o_ref[pl.ds(row, 2 * ROWS), pl.ds(col, COLS)] = jnp.concatenate(pair, axis=0).astype(
@@ -226,7 +222,7 @@
     return pl.pallas_call(
         assemble_kernel,
         out_shape=jax.ShapeDtypeStruct((VIS, HID_HERE), BF16),
-        in_specs=[SMEM] * 3 + [VMEM] * 8,
+        in_specs=[SMEM] * 3 + [VMEM] * 10,
         out_specs=VMEM,
         compiler_params=local(),
         cost_estimate=cost(1 << 20, 9 << 20),
@@ -234,43 +230,40 @@
     )(z_order, x_order, core, *own, *other)
 
 
-def grad_kernel(core_ref, f0_ref, s0_ref, f1_ref, s1_ref, keep_ref, send_ref, total):
+def grad_kernel(half, core_ref, f0_ref, s0_ref, f1_ref, s1_ref, keep_ref, send_ref, total):
     core = core_ref[0]
-
-    @pl.loop(0, 2)
-    def _(x):
-        lanes = pl.ds(pl.multiple_of(x * COLS, COLS), COLS)
-        for r in range(VIS // 128):
-            rows = slice(r * 128, (r + 1) * 128)
-            total[rows, :] = sum(
-                lax.dot_general(
-                    f[:, rows], s[:, lanes], (((0,), (0,)), ((), ())), preferred_element_type=F32
-                )
-                for f, s in ((f0_ref, s0_ref), (f1_ref, s1_ref))
+    lanes = slice(half * COLS, (half + 1) * COLS)
+    for r in range(VIS // 128):
+        rows = slice(r * 128, (r + 1) * 128)
+        total[rows, :] = sum(
+            lax.dot_general(
+                f[:, rows], s[:, lanes], (((0,), (0,)), ((), ())), preferred_element_type=F32
             )
-        for b in range(8):
-            mine = pl.multiple_of((2 * b + core) * ROWS, 8)
-            other = pl.multiple_of((2 * b + 1 - core) * ROWS, 8)
-            keep_ref[b, x] = total[pl.ds(mine, ROWS), :].astype(BF16)
-            send_ref[b, x] = total[pl.ds(other, ROWS), :].astype(BF16)
-
-
-def grad_of(core, *parts):
-    out = jax.ShapeDtypeStruct((8, 2, ROWS, COLS), BF16)
-    return pl.pallas_call(
-        grad_kernel,
+            for f, s in ((f0_ref, s0_ref), (f1_ref, s1_ref))
+        )
+    for b in range(8):
+        mine = pl.multiple_of((2 * b + core) * ROWS, 8)
+        other = pl.multiple_of((2 * b + 1 - core) * ROWS, 8)
+        keep_ref[b] = total[pl.ds(mine, ROWS), :].astype(BF16)
+        send_ref[b] = total[pl.ds(other, ROWS), :].astype(BF16)
+
+
+def grad_of(half, core, *parts):
+    out = jax.ShapeDtypeStruct((8, ROWS, COLS), BF16)
+    return pl.pallas_call(
+        functools.partial(grad_kernel, half),
         out_shape=(out, out),
         in_specs=[SMEM] + [VMEM] * 4,
         out_specs=(VMEM, VMEM),
         scratch_shapes=[pltpu.VMEM((VIS, COLS), F32)],
         compiler_params=local(),
-        cost_estimate=cost(2 * SEQ * HID_HERE * VIS, 11 << 20),
+        cost_estimate=cost(SEQ * HID_HERE * VIS, 6 << 20),
         name="grad",
     )(core, *parts)
 
 
 def logit_kernel(at_ref, *refs):
-    parts, refs = refs[:8], refs[8:]
+    parts, refs = refs[:4], refs[4:]
     near_ref, far_ref, hw_ref, other_ref, lp_ref, lg_ref, scale_ref = refs
     facts = jnp.concatenate([near_ref[...], far_ref[...]], axis=0)
     lane = lax.broadcasted_iota(jnp.int32, (1, 128), 1)
@@ -290,47 +283,44 @@
     count = jnp.maximum(jnp.sum(jnp.sum(masks, axis=1, keepdims=True), axis=0, keepdims=True), 1.0)
     action = lax.broadcasted_iota(jnp.int32, (8, 128), 0)
     bins = lax.broadcasted_iota(jnp.int32, (8, NBINS), 1).astype(F32)
-    for side in range(2):
-        c = at_ref[0] if side == 0 else 1 - at_ref[0]
-        here = near_ref[pl.ds(at_ref[1] + 2 * side, 1), :]
-        own = (column(here, 1) == line).astype(F32)
-        advantage = (column(here, 0) - jnp.sum(own * mean, axis=1, keepdims=True)) / jnp.sum(
-            own * spread, axis=1, keepdims=True
+    here = near_ref[pl.ds(at_ref[0], 1), :]
+    own = (column(here, 1) == line).astype(F32)
+    advantage = (column(here, 0) - jnp.sum(own * mean, axis=1, keepdims=True)) / jnp.sum(
+        own * spread, axis=1, keepdims=True
+    )
+    rows = jnp.broadcast_to(here, (8, 128))
+    act = jnp.sum(jnp.where(lane == action + 8, rows, 0.0), axis=1, keepdims=True)
+    mask = jnp.sum(jnp.where(lane == action + 16, rows, 0.0), axis=1, keepdims=True)
+    weight = -mask * advantage / count
+
+    logits = (parts[0][...] + parts[1][...]) + (parts[2][...] + parts[3][...])
+    down = logits - jnp.max(logits, axis=-1, keepdims=True)
+    log_all = down - jnp.log(jnp.sum(jnp.exp(down), axis=-1, keepdims=True))
+    picked = (bins == act).astype(F32)
+    lp = jnp.sum(picked * log_all, axis=-1, keepdims=True)
+    lp_ref[...] = jnp.broadcast_to(lp, lp_ref.shape)
+    grad = (weight * (picked - jnp.exp(log_all))).astype(BF16)
+    lg_ref[...] = grad
+    size = column(here, 2)
+    for half, ref in enumerate((hw_ref, other_ref)):
+        back = lax.dot_general(
+            grad, ref[...], (((1,), (1,)), ((), ())), preferred_element_type=F32
         )
-        rows = jnp.broadcast_to(here, (8, 128))
-        act = jnp.sum(jnp.where(lane == action + 8, rows, 0.0), axis=1, keepdims=True)
-        mask = jnp.sum(jnp.where(lane == action + 16, rows, 0.0), axis=1, keepdims=True)
-        weight = -mask * advantage / count
-
-        own4 = [ref[...] for ref in parts[4 * side : 4 * side + 4]]
-        logits = (own4[0] + own4[1]) + (own4[2] + own4[3])
-        down = logits - jnp.max(logits, axis=-1, keepdims=True)
-        log_all = down - jnp.log(jnp.sum(jnp.exp(down), axis=-1, keepdims=True))
-        picked = (bins == act).astype(F32)
-        lp = jnp.sum(picked * log_all, axis=-1, keepdims=True)
-        lp_ref[c] = jnp.broadcast_to(lp, lp_ref.shape[1:])
-        grad = (weight * (picked - jnp.exp(log_all))).astype(BF16)
-        lg_ref[c] = grad
-        size = column(here, 2)
-        for half, ref in enumerate((hw_ref, other_ref)):
-            back = lax.dot_general(
-                grad, ref[...], (((1,), (1,)), ((), ())), preferred_element_type=F32
-            )
-            pool = jnp.sum(back, axis=0, keepdims=True) / size
-            place = at_ref[1] if half == 0 else 1 - at_ref[1]
-            lanes = pl.ds(pl.multiple_of(place * COLS, COLS), COLS)
-            scale_ref[c, :, lanes] = jnp.broadcast_to(pool, (8, COLS))
+        pool = jnp.sum(back, axis=0, keepdims=True) / size
+        place = at_ref[0] if half == 0 else 1 - at_ref[0]
+        lanes = pl.ds(pl.multiple_of(place * COLS, COLS), COLS)
+        scale_ref[:, lanes] = jnp.broadcast_to(pool, (8, COLS))
 
 
 def logit_parts(at, *operands):
     return pl.pallas_call(
         logit_kernel,
         out_shape=(
-            jax.ShapeDtypeStruct((2, 8, 128), F32),
-            jax.ShapeDtypeStruct((2, 8, NBINS), BF16),
-            jax.ShapeDtypeStruct((2, 8, HID_HERE), F32),
+            jax.ShapeDtypeStruct((8, 128), F32),
+            jax.ShapeDtypeStruct((8, NBINS), BF16),
+            jax.ShapeDtypeStruct((8, HID_HERE), F32),
         ),
-        in_specs=[SMEM] + [VMEM] * 12,
+        in_specs=[SMEM] + [VMEM] * 8,
         out_specs=(VMEM, VMEM, VMEM),
         compiler_params=local(),
         cost_estimate=cost(8 << 20, 1 << 20, 8192),
@@ -338,44 +328,33 @@
     )(at, *operands)
 
 
-def scale_kernel(core_ref, keep_ref, got_ref, scale_ref, head_ref, lg_ref, o_ref):
-    core = core_ref[0]
-    mine = scale_ref[core][0:1]
-    other = scale_ref[1 - core][0:1]
-    lower = jnp.concatenate([lg_ref[core].astype(F32), jnp.zeros((8, NBINS), F32)], axis=1)
-    for b in range(2):
-        for x in range(2):
-            cols = slice(x * COLS, (x + 1) * COLS)
-            top = (
-                keep_ref[b, x].astype(F32) * mine[:, cols]
-                + got_ref[b, x].astype(F32) * other[:, cols]
-            )
-            o_ref[b, x] = jnp.concatenate(
-                [top, head_ref[:, cols].astype(F32), lower], axis=0
-            ).astype(BF16)
-
-
-def scaled(core, keep, got, scale, head_input, lgrad):
-    spec = pl.BlockSpec((2, 2, ROWS, COLS), lambda i, n: (i, 0, 0, 0))
+def scale_kernel(keep0, keep1, got0, got1, mine_ref, other_ref, head_ref, lg_ref, o_ref):
+    lower = jnp.concatenate([lg_ref[...].astype(F32), jnp.zeros((8, NBINS), F32)], axis=1)
+    for x, (keep, got) in enumerate(((keep0, got0), (keep1, got1))):
+        cols = slice(x * COLS, (x + 1) * COLS)
+        mine, other = mine_ref[0:1, cols], other_ref[0:1, cols]
+        head = head_ref[:, cols].astype(F32)
+        for b in range(2):
+            top = keep[b].astype(F32) * mine + got[b].astype(F32) * other
+            o_ref[b, x] = jnp.concatenate([top, head, lower], axis=0).astype(BF16)
+
+
+def scaled(keeps, gots, mine, other, head_input, lgrad):
+    spec = pl.BlockSpec((2, ROWS, COLS), lambda i: (i, 0, 0))
+
+    def whole(columns):
+        return pl.BlockSpec((8, columns), lambda i: (0, 0))
+
     return pl.pallas_call(
         scale_kernel,
         out_shape=jax.ShapeDtypeStruct((8, 2, ROWS + 16, COLS), BF16),
-        grid_spec=pltpu.PrefetchScalarGridSpec(
-            num_scalar_prefetch=1,
-            grid=(4,),
-            in_specs=[
-                spec,
-                spec,
-                pl.BlockSpec((2, 8, HID_HERE), lambda i, n: (0, 0, 0)),
-                pl.BlockSpec((8, HID_HERE), lambda i, n: (0, 0)),
-                pl.BlockSpec((2, 8, NBINS), lambda i, n: (0, 0, 0)),
-            ],
-            out_specs=pl.BlockSpec((2, 2, ROWS + 16, COLS), lambda i, n: (i, 0, 0, 0)),
-        ),
+        grid=(4,),
+        in_specs=[spec] * 4 + [whole(HID_HERE)] * 3 + [whole(NBINS)],
+        out_specs=pl.BlockSpec((2, 2, ROWS + 16, COLS), lambda i: (i, 0, 0, 0)),
         compiler_params=params(limit=SMALL),
         cost_estimate=cost(8 << 20, 7 << 20),
         name="scaled",
-    )(core, keep, got, scale, head_input, lgrad)
+    )(*keeps, *gots, mine, other, head_input, lgrad)
 
 
 def episode_facts(lengths, actions, action_mask, group_ids, rewards):
@@ -420,9 +399,9 @@
     z_order = (z + jnp.array([0, 3, 1, 2], jnp.int32)) % 4
     block = jnp.stack(row)
     up, down = shifted(block, line, 1), shifted(block, line, -1)
-    half = shifted(up, line, 1)
+    half = (shifted(up[:2], line, 1), shifted(down[2:], line, -1))
     x_order = (x + jnp.array([0, 3, 1, 2], jnp.int32)) % 4
-    own = (block, up, down, half)
+    own = (block, up, down, *half)
     other = [shifted(w, "c", 1) for w in own]
     weight = assemble(z_order, x_order, core1, own, other)
 
@@ -438,7 +417,7 @@
     facts = jnp.concatenate([facts, shifted(facts, "c", 1)])
     facts = jnp.concatenate([facts] + [shifted(facts, "z", by) for by in (1, 2, 3)])
     far_facts = shifted(facts, "xl", 1)
-    places = jnp.stack([core, xh]).astype(jnp.int32)
+    places = xh.reshape(1)
     where = jnp.concatenate([length, xh.reshape(1)])
     idx = (y + jnp.array([0, 3, 1, 2], jnp.int32)) % 4
     a0 = attend(got, where, 0, (facts, idx, z_order, x_order, places, core1))
@@ -460,15 +439,17 @@
         1,
         (pool0, act_embed, ae_other, head_weight, hw_other),
     )
-    near = [part] + [shifted(part, "y", by) for by in (2, 1, 3)]
-    far = [across(part, by) for by in (0, 2, 1, 3)]
-    keep, send = grad_of(core1, frames0, slope0, frames1, slope1)
-    arrived = shifted(send, "c", 1)
-
+    parts = [part] + [shifted(part, "y", by) for by in (2, 1, 3)]
+    done = (frames0, slope0, frames1, slope1)
+    keep_a, send_a = grad_of(0, core1, *done)
+    got_a = shifted(send_a, "c", 1)
+    keep_b, send_b = grad_of(1, core1, *done)
+    got_b = shifted(send_b, "c", 1)
     logprob, lgrad, scale = logit_parts(
-        places, *near, *far, facts, far_facts, head_weight, hw_other
-    )
-    summed = scaled(core1, keep, arrived, scale, head_input, lgrad)
+        places, *parts, facts, far_facts, head_weight, hw_other
+    )
+    scale_other = shifted(scale, "c", 1)
+    summed = scaled((keep_a, keep_b), (got_a, got_b), scale, scale_other, head_input, lgrad)
     dealt_out = dealt(summed.reshape(16, ROWS + 16, COLS), ("z", "xl", "xh"))
     grad_proj = jnp.sum(dealt_out[:, :ROWS].astype(F32), axis=0).astype(BF16)
 
@@ -481,7 +462,7 @@
         lefts, rights, (((0,), (0,)), ((), ())), preferred_element_type=F32
     ).astype(BF16)
 
-    lp_mine = lax.dynamic_index_in_dim(logprob[:, :7, 0], core, 0)
+    lp_mine = logprob[:7, 0][None]
     lp_other = shifted(lp_mine, "xh", 1)
     logprobs = both(lp_mine, lp_other, 0)
     return logprobs, grad_proj, grad_head

time: 201 us -> 198 us (0.985)
  waiting for transfers between devices: 86.4 us -> 79.9 us
  local copies, waits for them, and re-layouts: 1.25 us -> 4.62 us
  starting transfers between devices: 59.7 us -> 62.6 us
    ppermute x4 -> x0, starting transfers between devices: 5.5 us -> none  [across(): return lax.ppermute(x, ('y', 'c'), pairs)]
    ppermute x29 -> x33, starting transfers between devices: 40.1 us -> 45.6 us  [shifted(): return lax.ppermute(x, axis, [(i, (i + by) % count) for i in range(count)])]
    ppermute x29 -> x33, waiting for transfers between devices: 85.1 us -> 79.9 us  [shifted(): return lax.ppermute(x, axis, [(i, (i + by) % count) for i in range(count)])]
    slice x0 -> x3, local copies, waits for them, and re-layouts: none -> 3.48 us  [the longest x2 3.37 us: per_device(): half = (shifted(up[:2], line, 1), shifted(down[2:], line, -1))]
    all_to_all x2, starting transfers between devices: 14.1 us -> 17 us  [dealt(): return lax.all_to_all(x, axes, 0, 0, tiled=True)]
    pallas_call x2 -> x3, Pallas kernels: 6.74 us -> 5.87 us  [the longest x2 5.49 us: grad_of(): pl.pallas_call(functools.partial(grad_kernel, half), out_shape=(out, out)...]
  transfers between devices with their start and end apart: 35 -> 35, of which waited for: 10 -> 13; matrix products, arithmetic and copies ran while one was open for 3% -> 4% of each run, Pallas kernels for 12% -> 12%
where the time goes in v3:
time: 198 us
  waiting for transfers between devices  79.9 us (40%)
  starting transfers between devices  62.6 us (32%)
  Pallas kernels  44.3 us (22%)
  local copies, waits for them, and re-layouts  4.62 us (2%)
  other arithmetic  4.38 us (2%)
    ppermute x33, waiting for transfers between devices, shifted(): return lax.ppermute(x, axis, [(i, (i + by) % count) for i in range(count)])  79.9 us
    ppermute x33, starting transfers between devices, shifted(): return lax.ppermute(x, axis, [(i, (i + by) % count) for i in range(count)])  45.6 us
    pallas_call x2, Pallas kernels, chunk_of(): pl.pallas_call(functools.partial(chunk_kernel, chunk), out_shape=tuple(sh...  19.1 us
    all_to_all x2, starting transfers between devices, dealt(): return lax.all_to_all(x, axes, 0, 0, tiled=True)  17 us
    pallas_call x2, Pallas kernels, attend(): pl.pallas_call(functools.partial(attend_kernel, chunk), out_shape=(out, h...  10.2 us
    pallas_call x2, Pallas kernels, grad_of(): pl.pallas_call(functools.partial(grad_kernel, half), out_shape=(out, out)...  5.49 us
    pallas_call x1, Pallas kernels, pack(): pl.pallas_call(pack_kernel, out_shape=jax.ShapeDtypeStruct((8, 3, 128, CO...  4.19 us
  transfers between devices with their start and end apart: 35, of which 13 were waited for; matrix products, arithmetic and copies ran while one was open for 4% of the time, Pallas kernels for 12%

profile of v3, /device:TPU:1, one launch (start us, length us, event | category | flops | bytes accessed | tf_op | source)
XLA Modules:
  0.0 197.6 jit_solution(11794033639812814697)
XLA Ops:
  0.6 4.2 %pack.1 = bf16[8,3,128,512]{3,2,1,0:T(8,128)(2,1)} custom-call(bf16[2,128,2048]{2,1,0:T(8,128)(2,1)} %q_ref.1, bf16[2,128,2048]{2,1,0:T(8,128)(2,1)} %k_ref.1, bf16[2,128,2048]{2,1,0:T(8,128)(2,1)} %v_ref.1), custom_call_target="tpu_custom_call" | custom-call | bytes 6291456 | tf_op jit(solution)/shard_map/pack/pallas_call | solution.py:66
  4.9 7.6 %all-to-all-start = ((bf16[8,3,128,512]{3,2,1,0:T(8,128)(2,1)}), bf16[8,3,128,512]{3,2,1,0:T(8,128)(2,1)S(1)}, u32[]{:S(2)}, u32[]{:S(2)}) async-start(bf16[8,3,128,512]{3,2,1,0:T(8,128)(2,1)} %pack.1), calls=%async_computation | async-start | bytes 6291456 | tf_op jit(solution)/shard_map/all_to_all | solution.py:55
  12.5 1.7 collective-permute-start.3
  14.2 2.2 %collective-permute-start.4 = (bf16[136,512]{1,0:T(8,128)(2,1)S(1)}, bf16[136,512]{1,0:T(8,128)(2,1)}, u32[]{:S(2)}, u32[]{:S(2)}) collective-permute-start(bf16[136,512]{1,0:T(8,128)(2,1)S(1)} %copy-done.2), channel_id=1, source_target_pairs={{0,12},{4,0},{8,4},{12,8},{1,13},{5,1},{9,5},{13,9},{2,14},{6,2},{... | collective-permute-start | bytes 417800 | tf_op jit(solution)/shard_map/ppermute | solution.py:51
  16.4 1.2 collective-permute-start.5
  18.0 1.4 collective-permute-done.3
  19.4 4.3 %collective-permute-done.5 = bf16[136,512]{1,0:T(8,128)(2,1)} collective-permute-done((bf16[136,512]{1,0:T(8,128)(2,1)S(1)}, bf16[136,512]{1,0:T(8,128)(2,1)}, u32[]{:S(2)}, u32[]{:S(2)}) %collective-permute-start.5) | collective-permute-done | bytes 139296 | tf_op jit(solution)/shard_map/ppermute | solution.py:51
  23.7 1.9 pad_maximum_fusion.refs_0_
  25.9 2.4 %collective-permute-start.7 = (bf16[4,136,512]{2,1,0:T(8,128)(2,1)}, bf16[4,136,512]{2,1,0:T(8,128)(2,1)}, u32[]{:S(2)}, u32[]{:S(2)}) collective-permute-start(bf16[4,136,512]{2,1,0:T(8,128)(2,1)} %pad_maximum_fusion.refs_0_), channel_id=1, source_target_pairs={{0,66},{2,0},{64,2},{66,64},{1,67},{3,1},{65,3},{67,65},{4,70},{6,... | collective-permute-start | bytes 1671176 | tf_op jit(solution)/shard_map/ppermute | solution.py:51
  28.3 2.1 %collective-permute-start.15 = (f32[2,128]{1,0:T(2,128)S(1)}, f32[2,128]{1,0:T(2,128)S(1)}, u32[]{:S(2)}, u32[]{:S(2)}) collective-permute-start(f32[2,128]{1,0:T(2,128)S(1)} %pad_maximum_fusion.2), channel_id=1, source_target_pairs={{0,1},{1,0},{2,3},{3,2},{4,5},{5,4},{6,7},{7,6},{8,9},{9,8},{10,11... | collective-permute-start | bytes 3080 | tf_op jit(solution)/shard_map/ppermute | solution.py:51
  31.3 0.9 collective-permute-start.16
  32.8 1.9 collective-permute-start.17
  35.2 1.2 collective-permute-start.10
  37.4 25.2 %collective-permute-done.6.refs_1_ = bf16[4,136,512]{2,1,0:T(8,128)(2,1)} collective-permute-done((bf16[4,136,512]{2,1,0:T(8,128)(2,1)}, bf16[4,136,512]{2,1,0:T(8,128)(2,1)}, u32[]{:S(2)}, u32[]{:S(2)}) %collective-permute-start.6) | collective-permute-done | bytes 557088 | tf_op jit(solution)/shard_map/ppermute | solution.py:51
  62.6 1.7 slice.28
  64.3 1.7 slice.29
  66.0 2.7 %collective-permute-start.9 = (bf16[2,136,512]{2,1,0:T(8,128)(2,1)}, bf16[2,136,512]{2,1,0:T(8,128)(2,1)}, u32[]{:S(2)}, u32[]{:S(2)}) collective-permute-start(bf16[2,136,512]{2,1,0:T(8,128)(2,1)} %slice.29), channel_id=1, source_target_pairs={{0,66},{2,0},{64,2},{66,64},{1,67},{3,1},{65,3},{67,65},{4,70},{6,... | collective-permute-start | bytes 835592 | tf_op jit(solution)/shard_map/ppermute | solution.py:51
  68.7 5.1 %attend.3.a_ref = bf16[512,512]{1,0:T(8,128)(2,1)S(1)} custom-call(s32[2]{0:T(128)S(1)} %pad_add_fusion.len_ref, bf16[8,3,128,512]{3,2,1,0:T(8,128)(2,1)S(1)} %all-to-all-done.got_ref, f32[16,128]{1,0:T(8,128)S(1)} %concatenate.19.rest_0_.refs_4_, s32[4]{0:T(128)S(1)} %get-tuple-element.40.rest_1_.idx_ref, s32[4]{0:T(128)S(1)} %get-tuple-element.41.z_ref.rest_2_, ...), custom_call_target="tpu_custom_call" | custom-call | flops 1073741824 | bytes 3145728 | tf_op jit(solution)/shard_map/attend/pallas_call | solution.py:111
  73.8 1.2 collective-permute-start.19
  75.0 1.3 collective-permute-start.13
  76.9 5.1 %attend.2 = (bf16[512,512]{1,0:T(8,128)(2,1)S(1)}, bf16[2048,2176]{1,0:T(8,128)(2,1)S(1)}) custom-call(s32[2]{0:T(128)S(1)} %pad_add_fusion.len_ref, bf16[8,3,128,512]{3,2,1,0:T(8,128)(2,1)S(1)} %all-to-all-done.got_ref, bf16[2048,2176]{1,0:T(8,128)(2,1)} %rest_0_.1), custom_call_target="tpu_custom_call" | custom-call | flops 1073741824 | bytes 3145728 | tf_op jit(solution)/shard_map/attend/pallas_call | solution.py:111
  82.0 1.9 collective-permute-start.20
  83.9 0.9 collective-permute-start.1
  84.8 2.7 %collective-permute-done.19.b_ref = bf16[512,512]{1,0:T(8,128)(2,1)S(1)} collective-permute-done((bf16[512,512]{1,0:T(8,128)(2,1)S(1)}, bf16[512,512]{1,0:T(8,128)(2,1)S(1)}, u32[]{:S(2)}, u32[]{:S(2)}) %collective-permute-start.19) | collective-permute-done | bytes 524320 | tf_op jit(solution)/shard_map/ppermute | solution.py:51
  87.6 2.9 %collective-permute-start.22 = (f32[7,512]{1,0:T(8,128)S(1)}, f32[7,512]{1,0:T(8,128)S(1)}, u32[]{:S(2)}, u32[]{:S(2)}) collective-permute-start(f32[7,512]{1,0:T(8,128)S(1)} %copy-done.1), channel_id=1, source_target_pairs={{0,64},{64,0},{1,65},{65,1},{2,66},{66,2},{3,67},{67,3},{4,68},{68... | collective-permute-start | bytes 43016 | tf_op jit(solution)/shard_map/ppermute | solution.py:51
  90.6 2.7 %assemble.1.w_ref = bf16[2176,1024]{1,0:T(8,128)(2,1)S(1)} custom-call(s32[4]{0:T(128)S(1)} %get-tuple-element.41.z_ref.rest_2_, s32[4]{0:T(128)S(1)} %get-tuple-element.39.x_ref.rest_3_, s32[1]{0:T(128)} %bitcast.1.core_ref.rest_5_, bf16[4,136,512]{2,1,0:T(8,128)(2,1)} %pad_maximum_fusion.refs_0_, bf16[4,136,512]{2,1,0:T(8,128)(2,1)} %collective-permute-done.6.refs_1_, ...), custom_call_target="tpu_custom_call" | custom-call | flops 1048576 | bytes 9437184 | tf_op jit(solution)/shard_map/assemble/pallas_call | solution.py:222
  93.3 1.9 collective-permute-done.20.c_ref
  95.2 1.2 collective-permute-start
  96.4 10.0 %collective-permute-done.1.c_ref = bf16[512,512]{1,0:T(8,128)(2,1)S(1)} collective-permute-done((bf16[512,512]{1,0:T(8,128)(2,1)S(1)}, bf16[512,512]{1,0:T(8,128)(2,1)S(1)}, u32[]{:S(2)}, u32[]{:S(2)}) %collective-permute-start.1) | collective-permute-done | bytes 524320 | tf_op jit(solution)/shard_map/ppermute | solution.py:51
  106.4 3.3 %collective-permute-start.2 = (bf16[512,512]{1,0:T(8,128)(2,1)S(1)}, bf16[512,512]{1,0:T(8,128)(2,1)S(1)}, u32[]{:S(2)}, u32[]{:S(2)}) collective-permute-start(bf16[512,512]{1,0:T(8,128)(2,1)S(1)} %collective-permute-done.1.c_ref), channel_id=1, source_target_pairs={{0,48},{16,0},{32,16},{48,32},{1,49},{17,1},{33,17},{49,33},{2,50}... | collective-permute-start | bytes 1572872 | tf_op jit(solution)/shard_map/ppermute | solution.py:51
  109.7 9.5 %chunk.2 = (bf16[512,2176]{1,0:T(8,128)(2,1)S(1)}, bf16[512,1024]{1,0:T(8,128)(2,1)S(1)}, f32[8,1024]{1,0:T(8,128)S(1)}) custom-call(s32[4]{0:T(128)S(1)} %get-tuple-element.40.rest_1_.idx_ref, s32[2]{0:T(128)S(1)} %pad_add_fusion.len_ref, bf16[512,512]{1,0:T(8,128)(2,1)S(1)} %attend.3.a_ref, bf16[512,512]{1,0:T(8,128)(2,1)S(1)} %collective-permute-done.19.b_ref, ...), custom_call_target="tpu_custom_call" | custom-call | flops 6845104128 | bytes 20971520 | tf_op jit(solution)/shard_map/chunk/pallas_call | solution.py:193
  119.9 9.5 %chunk.3 = (bf16[512,2176]{1,0:T(8,128)(2,1)S(1)}, bf16[512,1024]{1,0:T(8,128)(2,1)S(1)}, bf16[8,1024]{1,0:T(8,128)(2,1)S(1)}, f32[8,256]{1,0:T(8,128)S(1)}) custom-call(s32[4]{0:T(128)S(1)} %get-tuple-element.40.rest_1_.idx_ref, s32[2]{0:T(128)S(1)} %pad_add_fusion.len_ref, bf16[512,512]{1,0:T(8,128)(2,1)S(1)} %get-tuple-element.19.a_ref, ...), custom_call_target="tpu_custom_call" | custom-call | flops 6845104128 | bytes 20971520 | tf_op jit(solution)/shard_map/chunk/pallas_call | solution.py:193
  129.5 2.7 %grad.3 = (bf16[8,136,512]{2,1,0:T(8,128)(2,1)S(1)}, bf16[8,136,512]{2,1,0:T(8,128)(2,1)S(1)}) custom-call(s32[1]{0:T(128)} %bitcast.1.core_ref.rest_5_, bf16[512,2176]{1,0:T(8,128)(2,1)S(1)} %get-tuple-element.24.f0_ref, bf16[512,1024]{1,0:T(8,128)(2,1)S(1)} %get-tuple-element.25.s0_ref, bf16[512,2176]{1,0:T(8,128)(2,1)S(1)} %get-tuple-element.26.f1_ref, ...), custom_call_target="tpu_custom_call" | custom-call | flops 2281701376 | bytes 6291456 | tf_op jit(solution)/shard_map/grad/pallas_call | solution.py:253
  132.2 2.7 %grad.2 = (bf16[8,136,512]{2,1,0:T(8,128)(2,1)S(1)}, bf16[8,136,512]{2,1,0:T(8,128)(2,1)S(1)}) custom-call(s32[1]{0:T(128)} %bitcast.1.core_ref.rest_5_, bf16[512,2176]{1,0:T(8,128)(2,1)S(1)} %get-tuple-element.24.f0_ref, bf16[512,1024]{1,0:T(8,128)(2,1)S(1)} %get-tuple-element.25.s0_ref, bf16[512,2176]{1,0:T(8,128)(2,1)S(1)} %get-tuple-element.26.f1_ref, ...), custom_call_target="tpu_custom_call" | custom-call | flops 2281701376 | bytes 6291456 | tf_op jit(solution)/shard_map/grad/pallas_call | solution.py:253
  135.0 2.0 collective-permute-start.30
  137.0 1.9 collective-permute-start.24
  138.9 2.1 %collective-permute-start.25 = (f32[8,256]{1,0:T(8,128)S(1)}, f32[8,256]{1,0:T(8,128)S(1)}, u32[]{:S(2)}, u32[]{:S(2)}) collective-permute-start(f32[8,256]{1,0:T(8,128)S(1)} %get-tuple-element.22.refs_0_), channel_id=1, source_target_pairs={{0,16},{16,32},{32,48},{48,0},{1,17},{17,33},{33,49},{49,1},{2,18}... | collective-permute-start | bytes 24584 | tf_op jit(solution)/shard_map/ppermute | solution.py:51
  141.0 1.9 collective-permute-start.26
  142.9 0.9 collective-permute-done.26.refs_3_
  144.2 2.4 %collective-permute-start.31 = (f32[8,1024]{1,0:T(8,128)S(1)}, f32[8,1024]{1,0:T(8,128)S(1)}, u32[]{:S(2)}, u32[]{:S(2)}) collective-permute-start(f32[8,1024]{1,0:T(8,128)S(1)} %get-tuple-element.32.mine_ref), channel_id=1, source_target_pairs={{0,1},{1,0},{2,3},{3,2},{4,5},{5,4},{6,7},{7,6},{8,9},{9,8},{10,11... | collective-permute-start | bytes 98312 | tf_op jit(solution)/shard_map/ppermute | solution.py:51
  146.6 0.9 collective-permute-done.31.other_ref
  147.5 2.3 %scaled.1 = bf16[8,2,152,512]{3,2,1,0:T(8,128)(2,1)} custom-call(bf16[8,136,512]{2,1,0:T(8,128)(2,1)S(1)} %get-tuple-element.28.keep0, bf16[8,136,512]{2,1,0:T(8,128)(2,1)S(1)} %get-tuple-element.29.keep1, bf16[8,136,512]{2,1,0:T(8,128)(2,1)S(1)} %collective-permute-done.29.got0, bf16[8,136,512]{2,1,0:T(8,128)(2,1)S(1)} %collective-permute-done.30.got1, ...), custom_call_target="tpu_custom_call" | custom-call | flops 8388608 | bytes 7340032 | tf_op jit(solution)/shard_map/scaled/pallas_call | solution.py:348
  149.8 9.4 %all-to-all-start.1 = ((bf16[16,152,512]{2,1,0:T(8,128)(2,1)}), bf16[16,152,512]{2,1,0:T(8,128)(2,1)S(1)}, u32[]{:S(2)}, u32[]{:S(2)}) async-start(bf16[16,152,512]{2,1,0:T(8,128)(2,1)} %bitcast.9), calls=%async_computation.1 | async-start | bytes 4980736 | tf_op jit(solution)/shard_map/all_to_all | solution.py:55
  159.3 2.9 %collective-permute-start.28 = (f32[1,7]{1,0:T(1,128)S(1)}, f32[1,7]{1,0:T(1,128)S(1)}, u32[]{:S(2)}, u32[]{:S(2)}) collective-permute-start(f32[1,7]{1,0:T(1,128)S(1)} %bitcast.28), channel_id=1, source_target_pairs={{0,64},{64,0},{1,65},{65,1},{2,66},{66,2},{3,67},{67,3},{4,68},{68... | collective-permute-start | bytes 92 | tf_op jit(solution)/shard_map/ppermute | solution.py:51
  162.2 30.8 %collective-permute-done.28 = f32[1,7]{1,0:T(1,128)S(1)} collective-permute-done((f32[1,7]{1,0:T(1,128)S(1)}, f32[1,7]{1,0:T(1,128)S(1)}, u32[]{:S(2)}, u32[]{:S(2)}) %collective-permute-start.28) | collective-permute-done | bytes 60 | tf_op jit(solution)/shard_map/ppermute | solution.py:51
  193.3 1.8 collective-permute-start.32
  195.7 1.0 slice_reduce_fusion
  196.7 1.0 fusion
  (76 shorter events, 6.7 us)
Async XLA Ops:
  4.8 7.7 %copy-start.2 = (bf16[136,512]{1,0:T(8,128)(2,1)S(1)}, bf16[136,512]{1,0:T(8,128)(2,1)}, u32[]{:S(2)}) copy-start(bf16[136,512]{1,0:T(8,128)(2,1)} %param.20) | copy-start | bytes 417796
  4.8 12.8 %copy-start.6 = (s32[2]{0:T(128)S(1)}, s32[2]{0:T(128)}, u32[]{:S(2)}) copy-start(s32[2]{0:T(128)} %param.25) | copy-start | bytes 28
  4.8 12.8 %copy-start.8 = (s32[2]{0:T(128)S(1)}, s32[2]{0:T(128)}, u32[]{:S(2)}) copy-start(s32[2]{0:T(128)} %param.18) | copy-start | bytes 28
  4.8 13.0 %copy-start.7 = (f32[2]{0:T(128)S(1)}, f32[2]{0:T(128)}, u32[]{:S(2)}) copy-start(f32[2]{0:T(128)} %param.26) | copy-start | bytes 28
  4.8 13.1 %copy-start.3 = (s32[2,7]{1,0:T(2,128)S(1)}, s32[2,7]{1,0:T(2,128)}, u32[]{:S(2)}) copy-start(s32[2,7]{1,0:T(2,128)} %param.23) | copy-start | bytes 172
  4.8 13.1 %copy-start.4 = (s32[2,7]{1,0:T(2,128)S(1)}, s32[2,7]{1,0:T(2,128)}, u32[]{:S(2)}) copy-start(s32[2,7]{1,0:T(2,128)} %param.24) | copy-start | bytes 172
  4.9 27.3 %copy-start.5 = (s32[4]{0:T(128)S(1)}, s32[4]{0:T(128)}, u32[]{:S(2)}) copy-start(s32[4]{0:T(128)} %constant.54.clone) | copy-start | bytes 52
  4.9 63.8 %all-to-all-start = ((bf16[8,3,128,512]{3,2,1,0:T(8,128)(2,1)}), bf16[8,3,128,512]{3,2,1,0:T(8,128)(2,1)S(1)}, u32[]{:S(2)}, u32[]{:S(2)}) async-start(bf16[8,3,128,512]{3,2,1,0:T(8,128)(2,1)} %pack.1), calls=%async_computation | async-start | bytes 6291456 | tf_op jit(solution)/shard_map/all_to_all | solution.py:55
  12.5 6.9 %collective-permute-start.3 = (bf16[136,512]{1,0:T(8,128)(2,1)S(1)}, bf16[136,512]{1,0:T(8,128)(2,1)S(1)}, u32[]{:S(2)}, u32[]{:S(2)}) collective-permute-start(bf16[136,512]{1,0:T(8,128)(2,1)S(1)} %copy-done.2), channel_id=1, source_target_pairs={{0,4},{4,8},{8,12},{12,0},{1,5},{5,9},{9,13},{13,1},{2,6},{6,10},{... | collective-permute-start | bytes 417800 | tf_op jit(solution)/shard_map/ppermute | solution.py:51
  14.2 5.2 %collective-permute-start.4 = (bf16[136,512]{1,0:T(8,128)(2,1)S(1)}, bf16[136,512]{1,0:T(8,128)(2,1)}, u32[]{:S(2)}, u32[]{:S(2)}) collective-permute-start(bf16[136,512]{1,0:T(8,128)(2,1)S(1)} %copy-done.2), channel_id=1, source_target_pairs={{0,12},{4,0},{8,4},{12,8},{1,13},{5,1},{9,5},{13,9},{2,14},{6,2},{... | collective-permute-start | bytes 417800 | tf_op jit(solution)/shard_map/ppermute | solution.py:51
  16.4 7.3 %collective-permute-start.5 = (bf16[136,512]{1,0:T(8,128)(2,1)S(1)}, bf16[136,512]{1,0:T(8,128)(2,1)}, u32[]{:S(2)}, u32[]{:S(2)}) collective-permute-start(bf16[136,512]{1,0:T(8,128)(2,1)S(1)} %copy-done.2), channel_id=1, source_target_pairs={{0,8},{4,12},{8,0},{12,4},{1,9},{5,13},{9,1},{13,5},{2,10},{6,14},... | collective-permute-start | bytes 417800 | tf_op jit(solution)/shard_map/ppermute | solution.py:51
  25.6 37.1 %collective-permute-start.6 = (bf16[4,136,512]{2,1,0:T(8,128)(2,1)}, bf16[4,136,512]{2,1,0:T(8,128)(2,1)}, u32[]{:S(2)}, u32[]{:S(2)}) collective-permute-start(bf16[4,136,512]{2,1,0:T(8,128)(2,1)} %pad_maximum_fusion.refs_0_), channel_id=1, source_target_pairs={{0,2},{2,64},{64,66},{66,0},{1,3},{3,65},{65,67},{67,1},{4,6},{6,6... | collective-permute-start | bytes 1671176 | tf_op jit(solution)/shard_map/ppermute | solution.py:51
  25.9 38.5 %collective-permute-start.7 = (bf16[4,136,512]{2,1,0:T(8,128)(2,1)}, bf16[4,136,512]{2,1,0:T(8,128)(2,1)}, u32[]{:S(2)}, u32[]{:S(2)}) collective-permute-start(bf16[4,136,512]{2,1,0:T(8,128)(2,1)} %pad_maximum_fusion.refs_0_), channel_id=1, source_target_pairs={{0,66},{2,0},{64,2},{66,64},{1,67},{3,1},{65,3},{67,65},{4,70},{6,... | collective-permute-start | bytes 1671176 | tf_op jit(solution)/shard_map/ppermute | solution.py:51
  28.3 2.9 %collective-permute-start.15 = (f32[2,128]{1,0:T(2,128)S(1)}, f32[2,128]{1,0:T(2,128)S(1)}, u32[]{:S(2)}, u32[]{:S(2)}) collective-permute-start(f32[2,128]{1,0:T(2,128)S(1)} %pad_maximum_fusion.2), channel_id=1, source_target_pairs={{0,1},{1,0},{2,3},{3,2},{4,5},{5,4},{6,7},{7,6},{8,9},{9,8},{10,11... | collective-permute-start | bytes 3080 | tf_op jit(solution)/shard_map/ppermute | solution.py:51
  31.3 3.9 %collective-permute-start.16 = (f32[4,128]{1,0:T(4,128)S(1)}, f32[4,128]{1,0:T(4,128)S(1)}, u32[]{:S(2)}, u32[]{:S(2)}) collective-permute-start(f32[4,128]{1,0:T(4,128)S(1)} %pad_maximum_fusion.1), channel_id=1, source_target_pairs={{0,4},{4,8},{8,12},{12,0},{1,5},{5,9},{9,13},{13,1},{2,6},{6,10},{... | collective-permute-start | bytes 6152 | tf_op jit(solution)/shard_map/ppermute | solution.py:51
  32.8 4.4 %collective-permute-start.17 = (f32[4,128]{1,0:T(4,128)S(1)}, f32[4,128]{1,0:T(4,128)S(1)}, u32[]{:S(2)}, u32[]{:S(2)}) collective-permute-start(f32[4,128]{1,0:T(4,128)S(1)} %pad_maximum_fusion.1), channel_id=1, source_target_pairs={{0,8},{4,12},{8,0},{12,4},{1,9},{5,13},{9,1},{13,5},{2,10},{6,14},... | collective-permute-start | bytes 6152 | tf_op jit(solution)/shard_map/ppermute | solution.py:51
  34.7 2.7 %collective-permute-start.18 = (f32[4,128]{1,0:T(4,128)S(1)}, f32[4,128]{1,0:T(4,128)S(1)}, u32[]{:S(2)}, u32[]{:S(2)}) collective-permute-start(f32[4,128]{1,0:T(4,128)S(1)} %pad_maximum_fusion.1), channel_id=1, source_target_pairs={{0,12},{4,0},{8,4},{12,8},{1,13},{5,1},{9,5},{13,9},{2,14},{6,2},{... | collective-permute-start | bytes 6152 | tf_op jit(solution)/shard_map/ppermute | solution.py:51
  35.2 41.6 %collective-permute-start.10 = (bf16[4,136,512]{2,1,0:T(8,128)(2,1)}, bf16[4,136,512]{2,1,0:T(8,128)(2,1)}, u32[]{:S(2)}, u32[]{:S(2)}) collective-permute-start(bf16[4,136,512]{2,1,0:T(8,128)(2,1)} %pad_maximum_fusion.refs_0_), channel_id=1, source_target_pairs={{0,1},{1,0},{2,3},{3,2},{4,5},{5,4},{6,7},{7,6},{8,9},{9,8},{10,11... | collective-permute-start | bytes 1671176 | tf_op jit(solution)/shard_map/ppermute | solution.py:51
  64.3 10.7 %collective-permute-start.8 = (bf16[2,136,512]{2,1,0:T(8,128)(2,1)}, bf16[2,136,512]{2,1,0:T(8,128)(2,1)S(1)}, u32[]{:S(2)}, u32[]{:S(2)}) collective-permute-start(bf16[2,136,512]{2,1,0:T(8,128)(2,1)} %slice.28), channel_id=1, source_target_pairs={{0,2},{2,64},{64,66},{66,0},{1,3},{3,65},{65,67},{67,1},{4,6},{6,6... | collective-permute-start | bytes 835592 | tf_op jit(solution)/shard_map/ppermute | solution.py:51
  66.0 10.3 %collective-permute-start.9 = (bf16[2,136,512]{2,1,0:T(8,128)(2,1)}, bf16[2,136,512]{2,1,0:T(8,128)(2,1)}, u32[]{:S(2)}, u32[]{:S(2)}) collective-permute-start(bf16[2,136,512]{2,1,0:T(8,128)(2,1)} %slice.29), channel_id=1, source_target_pairs={{0,66},{2,0},{64,2},{66,64},{1,67},{3,1},{65,3},{67,65},{4,70},{6,... | collective-permute-start | bytes 835592 | tf_op jit(solution)/shard_map/ppermute | solution.py:51
  73.8 13.7 %copy-start = (bf16[512,256]{1,0:T(8,128)(2,1)S(1)}, bf16[512,256]{1,0:T(8,128)(2,1)}, u32[]{:S(2)}) copy-start(bf16[512,256]{1,0:T(8,128)(2,1)} %refs_6_.1) | copy-start | bytes 786436
  73.8 13.8 %copy-start.1 = (f32[7,512]{1,0:T(8,128)S(1)}, f32[7,512]{1,0:T(8,128)}, u32[]{:S(2)}) copy-start(f32[7,512]{1,0:T(8,128)} %rest_1_.1) | copy-start | bytes 43012
  73.8 13.7 %collective-permute-start.19 = (bf16[512,512]{1,0:T(8,128)(2,1)S(1)}, bf16[512,512]{1,0:T(8,128)(2,1)S(1)}, u32[]{:S(2)}, u32[]{:S(2)}) collective-permute-start(bf16[512,512]{1,0:T(8,128)(2,1)S(1)} %attend.3.a_ref), channel_id=1, source_target_pairs={{0,16},{16,32},{32,48},{48,0},{1,17},{17,33},{33,49},{49,1},{2,18}... | collective-permute-start | bytes 1572872 | tf_op jit(solution)/shard_map/ppermute | solution.py:51
  75.0 7.0 %collective-permute-start.13 = (bf16[2,136,512]{2,1,0:T(8,128)(2,1)S(1)}, bf16[2,136,512]{2,1,0:T(8,128)(2,1)S(1)}, u32[]{:S(2)}, u32[]{:S(2)}) collective-permute-start(bf16[2,136,512]{2,1,0:T(8,128)(2,1)S(1)} %collective-permute-done.8.refs_3_), channel_id=1, source_target_pairs={{0,1},{1,0},{2,3},{3,2},{4,5},{5,4},{6,7},{7,6},{8,9},{9,8},{10,11... | collective-permute-start | bytes 835592 | tf_op jit(solution)/shard_map/ppermute | solution.py:51
  76.3 7.6 %collective-permute-start.14 = (bf16[2,136,512]{2,1,0:T(8,128)(2,1)}, bf16[2,136,512]{2,1,0:T(8,128)(2,1)S(1)}, u32[]{:S(2)}, u32[]{:S(2)}) collective-permute-start(bf16[2,136,512]{2,1,0:T(8,128)(2,1)} %collective-permute-done.9.refs_4_), channel_id=1, source_target_pairs={{0,1},{1,0},{2,3},{3,2},{4,5},{5,4},{6,7},{7,6},{8,9},{9,8},{10,11... | collective-permute-start | bytes 835592 | tf_op jit(solution)/shard_map/ppermute | solution.py:51
  76.4 11.1 %collective-permute-start.11 = (bf16[4,136,512]{2,1,0:T(8,128)(2,1)}, bf16[4,136,512]{2,1,0:T(8,128)(2,1)S(1)}, u32[]{:S(2)}, u32[]{:S(2)}) collective-permute-start(bf16[4,136,512]{2,1,0:T(8,128)(2,1)} %collective-permute-done.6.refs_1_), channel_id=1, source_target_pairs={{0,1},{1,0},{2,3},{3,2},{4,5},{5,4},{6,7},{7,6},{8,9},{9,8},{10,11... | collective-permute-start | bytes 1671176 | tf_op jit(solution)/shard_map/ppermute | solution.py:51
  76.9 10.8 %collective-permute-start.12 = (bf16[4,136,512]{2,1,0:T(8,128)(2,1)}, bf16[4,136,512]{2,1,0:T(8,128)(2,1)S(1)}, u32[]{:S(2)}, u32[]{:S(2)}) collective-permute-start(bf16[4,136,512]{2,1,0:T(8,128)(2,1)} %collective-permute-done.7.refs_2_), channel_id=1, source_target_pairs={{0,1},{1,0},{2,3},{3,2},{4,5},{5,4},{6,7},{7,6},{8,9},{9,8},{10,11... | collective-permute-start | bytes 1671176 | tf_op jit(solution)/shard_map/ppermute | solution.py:51
  82.0 13.1 %collective-permute-start.20 = (bf16[512,512]{1,0:T(8,128)(2,1)S(1)}, bf16[512,512]{1,0:T(8,128)(2,1)S(1)}, u32[]{:S(2)}, u32[]{:S(2)}) collective-permute-start(bf16[512,512]{1,0:T(8,128)(2,1)S(1)} %attend.3.a_ref), channel_id=1, source_target_pairs={{0,48},{16,0},{32,16},{48,32},{1,49},{17,1},{33,17},{49,33},{2,50}... | collective-permute-start | bytes 1572872 | tf_op jit(solution)/shard_map/ppermute | solution.py:51
  83.9 22.5 %collective-permute-start.1 = (bf16[512,512]{1,0:T(8,128)(2,1)S(1)}, bf16[512,512]{1,0:T(8,128)(2,1)S(1)}, u32[]{:S(2)}, u32[]{:S(2)}) collective-permute-start(bf16[512,512]{1,0:T(8,128)(2,1)S(1)} %get-tuple-element.19.a_ref), channel_id=1, source_target_pairs={{0,48},{16,0},{32,16},{48,32},{1,49},{17,1},{33,17},{49,33},{2,50}... | collective-permute-start | bytes 1572872 | tf_op jit(solution)/shard_map/ppermute | solution.py:51
  87.5 22.1 %collective-permute-start.21 = (bf16[512,512]{1,0:T(8,128)(2,1)S(1)}, bf16[512,512]{1,0:T(8,128)(2,1)S(1)}, u32[]{:S(2)}, u32[]{:S(2)}) collective-permute-start(bf16[512,512]{1,0:T(8,128)(2,1)S(1)} %collective-permute-done.19.b_ref), channel_id=1, source_target_pairs={{0,16},{16,32},{32,48},{48,0},{1,17},{17,33},{33,49},{49,1},{2,18}... | collective-permute-start | bytes 1572872 | tf_op jit(solution)/shard_map/ppermute | solution.py:51
  87.5 31.7 %collective-permute-start.23 = (bf16[512,256]{1,0:T(8,128)(2,1)S(1)}, bf16[512,256]{1,0:T(8,128)(2,1)S(1)}, u32[]{:S(2)}, u32[]{:S(2)}) collective-permute-start(bf16[512,256]{1,0:T(8,128)(2,1)S(1)} %copy-done), channel_id=1, source_target_pairs={{0,64},{64,0},{1,65},{65,1},{2,66},{66,2},{3,67},{67,3},{4,68},{68... | collective-permute-start | bytes 786440 | tf_op jit(solution)/shard_map/ppermute | solution.py:51
  87.6 31.6 %collective-permute-start.22 = (f32[7,512]{1,0:T(8,128)S(1)}, f32[7,512]{1,0:T(8,128)S(1)}, u32[]{:S(2)}, u32[]{:S(2)}) collective-permute-start(f32[7,512]{1,0:T(8,128)S(1)} %copy-done.1), channel_id=1, source_target_pairs={{0,64},{64,0},{1,65},{65,1},{2,66},{66,2},{3,67},{67,3},{4,68},{68... | collective-permute-start | bytes 43016 | tf_op jit(solution)/shard_map/ppermute | solution.py:51
  95.2 24.0 %collective-permute-start = (bf16[512,512]{1,0:T(8,128)(2,1)S(1)}, bf16[512,512]{1,0:T(8,128)(2,1)S(1)}, u32[]{:S(2)}, u32[]{:S(2)}) collective-permute-start(bf16[512,512]{1,0:T(8,128)(2,1)S(1)} %get-tuple-element.19.a_ref), channel_id=1, source_target_pairs={{0,16},{16,32},{32,48},{48,0},{1,17},{17,33},{33,49},{49,1},{2,18}... | collective-permute-start | bytes 1572872 | tf_op jit(solution)/shard_map/ppermute | solution.py:51
  106.4 13.5 %collective-permute-start.2 = (bf16[512,512]{1,0:T(8,128)(2,1)S(1)}, bf16[512,512]{1,0:T(8,128)(2,1)S(1)}, u32[]{:S(2)}, u32[]{:S(2)}) collective-permute-start(bf16[512,512]{1,0:T(8,128)(2,1)S(1)} %collective-permute-done.1.c_ref), channel_id=1, source_target_pairs={{0,48},{16,0},{32,16},{48,32},{1,49},{17,1},{33,17},{49,33},{2,50}... | collective-permute-start | bytes 1572872 | tf_op jit(solution)/shard_map/ppermute | solution.py:51
  135.0 12.5 %collective-permute-start.30 = (bf16[8,136,512]{2,1,0:T(8,128)(2,1)S(1)}, bf16[8,136,512]{2,1,0:T(8,128)(2,1)S(1)}, u32[]{:S(2)}, u32[]{:S(2)}) collective-permute-start(bf16[8,136,512]{2,1,0:T(8,128)(2,1)S(1)} %get-tuple-element.31), channel_id=1, source_target_pairs={{0,1},{1,0},{2,3},{3,2},{4,5},{5,4},{6,7},{7,6},{8,9},{9,8},{10,11... | collective-permute-start | bytes 3342344 | tf_op jit(solution)/shard_map/ppermute | solution.py:51
  136.9 10.6 %collective-permute-start.29 = (bf16[8,136,512]{2,1,0:T(8,128)(2,1)S(1)}, bf16[8,136,512]{2,1,0:T(8,128)(2,1)S(1)}, u32[]{:S(2)}, u32[]{:S(2)}) collective-permute-start(bf16[8,136,512]{2,1,0:T(8,128)(2,1)S(1)} %get-tuple-element.30), channel_id=1, source_target_pairs={{0,1},{1,0},{2,3},{3,2},{4,5},{5,4},{6,7},{7,6},{8,9},{9,8},{10,11... | collective-permute-start | bytes 3342344 | tf_op jit(solution)/shard_map/ppermute | solution.py:51
  137.0 4.0 %collective-permute-start.27 = (f32[16,128]{1,0:T(8,128)S(1)}, f32[16,128]{1,0:T(8,128)S(1)}, u32[]{:S(2)}, u32[]{:S(2)}) collective-permute-start(f32[16,128]{1,0:T(8,128)S(1)} %concatenate.19.rest_0_.refs_4_), channel_id=1, source_target_pairs={{0,2},{2,0},{1,3},{3,1},{4,6},{6,4},{5,7},{7,5},{8,10},{10,8},{9,1... | collective-permute-start | bytes 24584 | tf_op jit(solution)/shard_map/ppermute | solution.py:51
  137.0 5.9 %collective-permute-start.24 = (f32[8,256]{1,0:T(8,128)S(1)}, f32[8,256]{1,0:T(8,128)S(1)}, u32[]{:S(2)}, u32[]{:S(2)}) collective-permute-start(f32[8,256]{1,0:T(8,128)S(1)} %get-tuple-element.22.refs_0_), channel_id=1, source_target_pairs={{0,32},{16,48},{32,0},{48,16},{1,33},{17,49},{33,1},{49,17},{2,34}... | collective-permute-start | bytes 24584 | tf_op jit(solution)/shard_map/ppermute | solution.py:51
  138.9 4.0 %collective-permute-start.25 = (f32[8,256]{1,0:T(8,128)S(1)}, f32[8,256]{1,0:T(8,128)S(1)}, u32[]{:S(2)}, u32[]{:S(2)}) collective-permute-start(f32[8,256]{1,0:T(8,128)S(1)} %get-tuple-element.22.refs_0_), channel_id=1, source_target_pairs={{0,16},{16,32},{32,48},{48,0},{1,17},{17,33},{33,49},{49,1},{2,18}... | collective-permute-start | bytes 24584 | tf_op jit(solution)/shard_map/ppermute | solution.py:51
  141.0 2.8 %collective-permute-start.26 = (f32[8,256]{1,0:T(8,128)S(1)}, f32[8,256]{1,0:T(8,128)S(1)}, u32[]{:S(2)}, u32[]{:S(2)}) collective-permute-start(f32[8,256]{1,0:T(8,128)S(1)} %get-tuple-element.22.refs_0_), channel_id=1, source_target_pairs={{0,48},{16,0},{32,16},{48,32},{1,49},{17,1},{33,17},{49,33},{2,50}... | collective-permute-start | bytes 24584 | tf_op jit(solution)/shard_map/ppermute | solution.py:51
  144.2 3.3 %collective-permute-start.31 = (f32[8,1024]{1,0:T(8,128)S(1)}, f32[8,1024]{1,0:T(8,128)S(1)}, u32[]{:S(2)}, u32[]{:S(2)}) collective-permute-start(f32[8,1024]{1,0:T(8,128)S(1)} %get-tuple-element.32.mine_ref), channel_id=1, source_target_pairs={{0,1},{1,0},{2,3},{3,2},{4,5},{5,4},{6,7},{7,6},{8,9},{9,8},{10,11... | collective-permute-start | bytes 98312 | tf_op jit(solution)/shard_map/ppermute | solution.py:51
  149.8 43.3 %all-to-all-start.1 = ((bf16[16,152,512]{2,1,0:T(8,128)(2,1)}), bf16[16,152,512]{2,1,0:T(8,128)(2,1)S(1)}, u32[]{:S(2)}, u32[]{:S(2)}) async-start(bf16[16,152,512]{2,1,0:T(8,128)(2,1)} %bitcast.9), calls=%async_computation.1 | async-start | bytes 4980736 | tf_op jit(solution)/shard_map/all_to_all | solution.py:55
  159.3 33.8 %collective-permute-start.28 = (f32[1,7]{1,0:T(1,128)S(1)}, f32[1,7]{1,0:T(1,128)S(1)}, u32[]{:S(2)}, u32[]{:S(2)}) collective-permute-start(f32[1,7]{1,0:T(1,128)S(1)} %bitcast.28), channel_id=1, source_target_pairs={{0,64},{64,0},{1,65},{65,1},{2,66},{66,2},{3,67},{67,3},{4,68},{68... | collective-permute-start | bytes 92 | tf_op jit(solution)/shard_map/ppermute | solution.py:51
  193.3 3.4 %collective-permute-start.32 = (bf16[16,16,512]{2,0,1:T(8,128)(2,1)S(1)}, bf16[16,16,512]{2,0,1:T(8,128)(2,1)S(1)}, u32[]{:S(2)}, u32[]{:S(2)}) collective-permute-start(bf16[16,16,512]{2,0,1:T(8,128)(2,1)S(1)} %copy.34), channel_id=1, source_target_pairs={{0,1},{1,0},{2,3},{3,2},{4,5},{5,4},{6,7},{7,6},{8,9},{9,8},{10,11... | collective-permute-start | bytes 786440 | tf_op jit(solution)/shard_map/ppermute | solution.py:51

commit v4 on v3

--- a/solution.py
+++ b/solution.py
@@ -55,33 +55,56 @@
     return lax.all_to_all(x, axes, 0, 0, tiled=True)
 
 
-def pack_kernel(q_ref, k_ref, v_ref, o_ref):
-    for i, ref in enumerate((q_ref, k_ref, v_ref)):
-        for j in range(2):
-            o_ref[j, i] = ref[0, :, j * COLS : (j + 1) * COLS]
-
-
-def pack(q, k, v):
-    spec = pl.BlockSpec((1, 128, 2 * COLS), lambda i: (i // 2, 0, i % 2))
+def pack_kernel(place_ref, q_ref, k_ref, v_ref, *rest):
+    outs, sems = rest[:8], rest[8]
+    copies = []
+    for k in range(8):
+        xh = lax.rem(place_ref[0] + k // 4, 2)
+        cols = pl.ds(pl.multiple_of(lax.rem(place_ref[1] + k % 4, 4) * COLS, COLS), COLS)
+        for i, ref in enumerate((q_ref, k_ref, v_ref)):
+            copies.append(
+                pltpu.make_async_copy(ref.at[xh, :, cols], outs[k].at[i], sems.at[3 * k + i])
+            )
+    for k in FAR_FIRST:
+        for i in range(3):
+            copies[3 * k + i].start()
+    for copy in copies:
+        copy.wait()
+
+
+FAR_FIRST = (6, 2, 5, 7, 4, 1, 3, 0)
+
+
+def pack(place, q, k, v):
     return pl.pallas_call(
         pack_kernel,
-        out_shape=jax.ShapeDtypeStruct((8, 3, 128, COLS), BF16),
-        grid=(4,),
-        in_specs=[spec] * 3,
-        out_specs=pl.BlockSpec((2, 3, 128, COLS), lambda i: (i, 0, 0, 0)),
-        compiler_params=params(),
+        out_shape=tuple([jax.ShapeDtypeStruct((3, 128, COLS), BF16)] * 8),
+        in_specs=[SMEM, HBM, HBM, HBM],
+        out_specs=tuple([VMEM] * 8),
+        scratch_shapes=[pltpu.SemaphoreType.DMA((24,))],
+        compiler_params=local(61952 * 1024),
         cost_estimate=cost(0, 6 << 20),
         name="pack",
-    )(q, k, v)
-
-
-def attend_kernel(chunk, len_ref, got_ref, *rest):
+    )(place, q, k, v)
+
+
+def to_peer(x, k):
+    pairs = [
+        (i, (i // 4 + k // 4) % 2 * 4 + (i % 4 + k % 4) % 4) for i in range(8)
+    ]
+    return lax.ppermute(x, ("xh", "y"), pairs)
+
+
+def attend_kernel(chunk, len_ref, *rest):
     if chunk == 1:
-        map_ref, o_ref, held_ref, sem = rest
+        got_ref, map_ref, o_ref, held_ref, sem = rest
         copy = pltpu.make_async_copy(map_ref, held_ref, sem)
         copy.start()
     else:
-        o_ref = rest[-1]
+        src_ref, pieces = rest[0], rest[1:9]
+        o_ref, got_ref = rest[-2:]
+        for k in range(8):
+            got_ref[src_ref[k]] = pieces[k][...]
     at = lax.broadcasted_iota(jnp.int32, (1, SEQ), 1)
     bias = jnp.where(at < len_ref[0], 0.0, NEG_LARGE)
 
@@ -105,19 +128,24 @@
         copy.wait()
 
 
-def attend(got, length, chunk, after):
+def attend(chunk, where, *operands):
     out = jax.ShapeDtypeStruct((CH, COLS), BF16)
-    held = jax.ShapeDtypeStruct((ATT, VIS), BF16)
+    if chunk == 0:
+        more = jax.ShapeDtypeStruct((8, 3, 128, COLS), BF16)
+        specs = [SMEM] + [VMEM] * 8 + [SMEM] * (len(operands) - 9)
+    else:
+        more = jax.ShapeDtypeStruct((ATT, VIS), BF16)
+        specs = [VMEM, HBM]
     return pl.pallas_call(
         functools.partial(attend_kernel, chunk),
-        out_shape=(out, held) if chunk == 1 else out,
-        in_specs=[SMEM, VMEM] + ([HBM] if chunk == 1 else [ANY] + [SMEM] * (len(after) - 1)),
-        out_specs=(VMEM, VMEM) if chunk == 1 else VMEM,
+        out_shape=(out, more),
+        in_specs=[SMEM] + specs,
+        out_specs=(VMEM, VMEM),
         scratch_shapes=[pltpu.SemaphoreType.DMA] if chunk == 1 else [],
         compiler_params=local(37 * 1024 * 1024 if chunk == 1 else SMALL),
         cost_estimate=cost(4 * CH * SEQ * COLS, 3 << 20, 4 * CH * SEQ),
         name="attend",
-    )(length, got, *after)
+    )(where, *operands)
 
 
 TILE = 256
@@ -203,7 +231,7 @@
 
 
 def assemble_kernel(z_ref, x_ref, core_ref, *refs):
-    o_ref = refs[-1]
+    o_ref, fact_ref = refs[-2:]
     lead = core_ref[0] == 0
     for k in range(4):
         x = x_ref[k]
@@ -211,6 +239,10 @@
         for i in range(4):
             ref, j = (k, i) if k < 3 else (3 + i // 2, i % 2)
             mine, other = refs[ref][j].astype(F32), refs[5 + ref][j].astype(F32)
+            for n, block in enumerate((mine, other)):
+                first = (8 * k + 2 * i + n) * 8
+                fact_ref[first : first + 8, :] = block[ROWS:, :128]
+            mine, other = mine[:ROWS], other[:ROWS]
             pair = [jnp.where(lead, mine, other), jnp.where(lead, other, mine)]
             row = pl.multiple_of((z_ref[i] * 2 + x % 2) * 2 * ROWS, 2 * ROWS)
             o_ref[pl.ds(row, 2 * ROWS), pl.ds(col, COLS)] = jnp.concatenate(pair, axis=0).astype(
@@ -221,9 +253,12 @@
 def assemble(z_order, x_order, core, own, other):
     return pl.pallas_call(
         assemble_kernel,
-        out_shape=jax.ShapeDtypeStruct((VIS, HID_HERE), BF16),
+        out_shape=(
+            jax.ShapeDtypeStruct((VIS, HID_HERE), BF16),
+            jax.ShapeDtypeStruct((256, 128), F32),
+        ),
         in_specs=[SMEM] * 3 + [VMEM] * 10,
-        out_specs=VMEM,
+        out_specs=(VMEM, VMEM),
         compiler_params=local(),
         cost_estimate=cost(1 << 20, 9 << 20),
         name="assemble",
@@ -264,28 +299,31 @@
 
 def logit_kernel(at_ref, *refs):
     parts, refs = refs[:4], refs[4:]
-    near_ref, far_ref, hw_ref, other_ref, lp_ref, lg_ref, scale_ref = refs
-    facts = jnp.concatenate([near_ref[...], far_ref[...]], axis=0)
+    fact_ref, hw_ref, other_ref, lp_ref, lg_ref, scale_ref = refs
+    facts = fact_ref[...]
     lane = lax.broadcasted_iota(jnp.int32, (1, 128), 1)
     line = lane.astype(F32)
 
     def column(rows, i):
         return jnp.sum(jnp.where(lane == i, rows, 0.0), axis=1, keepdims=True)
 
-    gains, groups = column(facts, 0), column(facts, 1)
-    member = (groups == line).astype(F32)
+    gains = column(facts, 0) + column(facts, 1) + column(facts, 2)
+    groups, valid = column(facts, 3), column(facts, 6)
+    member = (groups == line).astype(F32) * (0.5 * valid)
     sums = jnp.sum(member * gains, axis=0, keepdims=True)
     squares = jnp.sum(member * (gains * gains), axis=0, keepdims=True)
     sizes = jnp.maximum(jnp.sum(member, axis=0, keepdims=True), 1.0)
     mean = sums / sizes
     spread = jnp.sqrt(jnp.maximum(squares / sizes - mean * mean, 1.0))
     masks = jnp.where((lane >= 16) & (lane < 24), facts, 0.0)
-    count = jnp.maximum(jnp.sum(jnp.sum(masks, axis=1, keepdims=True), axis=0, keepdims=True), 1.0)
+    count = 0.5 * jnp.sum(jnp.sum(masks, axis=1, keepdims=True), axis=0, keepdims=True)
+    count = jnp.maximum(count, 1.0)
     action = lax.broadcasted_iota(jnp.int32, (8, 128), 0)
     bins = lax.broadcasted_iota(jnp.int32, (8, NBINS), 1).astype(F32)
-    here = near_ref[pl.ds(at_ref[0], 1), :]
-    own = (column(here, 1) == line).astype(F32)
-    advantage = (column(here, 0) - jnp.sum(own * mean, axis=1, keepdims=True)) / jnp.sum(
+    here = fact_ref[pl.ds(at_ref[0], 1), :]
+    own = (column(here, 3) == line).astype(F32)
+    gain = column(here, 0) + column(here, 1) + column(here, 2)
+    advantage = (gain - jnp.sum(own * mean, axis=1, keepdims=True)) / jnp.sum(
         own * spread, axis=1, keepdims=True
     )
     rows = jnp.broadcast_to(here, (8, 128))
@@ -301,7 +339,7 @@
     lp_ref[...] = jnp.broadcast_to(lp, lp_ref.shape)
     grad = (weight * (picked - jnp.exp(log_all))).astype(BF16)
     lg_ref[...] = grad
-    size = column(here, 2)
+    size = column(here, 4) * 64.0 + column(here, 5)
     for half, ref in enumerate((hw_ref, other_ref)):
         back = lax.dot_general(
             grad, ref[...], (((1,), (1,)), ((), ())), preferred_element_type=F32
@@ -320,7 +358,7 @@
             jax.ShapeDtypeStruct((8, NBINS), BF16),
             jax.ShapeDtypeStruct((8, HID_HERE), F32),
         ),
-        in_specs=[SMEM] + [VMEM] * 8,
+        in_specs=[SMEM] + [VMEM] * 7,
         out_specs=(VMEM, VMEM, VMEM),
         compiler_params=local(),
         cost_estimate=cost(8 << 20, 1 << 20, 8192),
@@ -358,15 +396,19 @@
 
 
 def episode_facts(lengths, actions, action_mask, group_ids, rewards):
-    three = jnp.stack([rewards, group_ids.astype(F32), lengths.astype(F32)], axis=1)
-    return jnp.concatenate(
+    high = lax.reduce_precision(rewards, 8, 7)
+    middle = lax.reduce_precision(rewards - high, 8, 7)
+    low = lax.reduce_precision((rewards - high) - middle, 8, 7)
+    columns = [high, middle, low, group_ids, lengths // 64, lengths % 64, jnp.ones((2,), F32)]
+    wide = jnp.concatenate(
         [
-            jnp.pad(three, ((0, 0), (0, 5))),
+            jnp.pad(jnp.stack([c.astype(F32) for c in columns], axis=1), ((0, 0), (0, 1))),
             jnp.pad(actions.astype(F32), ((0, 0), (0, 1))),
-            jnp.pad(action_mask.astype(F32), ((0, 0), (0, 105))),
+            jnp.pad(action_mask.astype(F32), ((0, 0), (0, COLS - 23))),
         ],
         axis=1,
     )
+    return jnp.pad(wide, ((0, 6), (0, 0))).astype(BF16)
 
 
 def per_device(
@@ -391,11 +433,19 @@
     core1 = core.reshape(1)
     length = lax.dynamic_slice_in_dim(lengths, xh, 1)
 
-    got = dealt(pack(queries, keys, values), ("xh", "y"))
+    place = jnp.stack([xh, y]).astype(jnp.int32)
+    blocks = pack(place, queries, keys, values)
+    got = {k: to_peer(blocks[k], k) for k in FAR_FIRST if k}
+    got = [blocks[0]] + [got[k] for k in range(1, 8)]
+    steps = jnp.arange(8, dtype=jnp.int32)
+    source = (xh + steps // 4) % 2 * 4 + (y + 4 - steps % 4) % 4
 
     x = xh * 2 + xl
     line = ("xh", "xl")
-    row = [proj_weight] + [shifted(proj_weight, "z", by) for by in (1, -1, 2)]
+    shard = jnp.concatenate(
+        [proj_weight, episode_facts(lengths, actions, action_mask, group_ids, rewards)]
+    )
+    row = [shard] + [shifted(shard, "z", by) for by in (1, -1, 2)]
     z_order = (z + jnp.array([0, 3, 1, 2], jnp.int32)) % 4
     block = jnp.stack(row)
     up, down = shifted(block, line, 1), shifted(block, line, -1)
@@ -403,7 +453,7 @@
     x_order = (x + jnp.array([0, 3, 1, 2], jnp.int32)) % 4
     own = (block, up, down, *half)
     other = [shifted(w, "c", 1) for w in own]
-    weight = assemble(z_order, x_order, core1, own, other)
+    weight, facts = assemble(z_order, x_order, core1, own, other)
 
     first = xh == 0
     hw_other, ae_other = shifted(head_weight, "xh", 1), shifted(act_embed, "xh", 1)
@@ -413,15 +463,13 @@
             [jnp.where(first, mine, other), jnp.where(first, other, mine)], axis=axis
         )
 
-    facts = episode_facts(lengths, actions, action_mask, group_ids, rewards)
-    facts = jnp.concatenate([facts, shifted(facts, "c", 1)])
-    facts = jnp.concatenate([facts] + [shifted(facts, "z", by) for by in (1, 2, 3)])
-    far_facts = shifted(facts, "xl", 1)
     places = xh.reshape(1)
     where = jnp.concatenate([length, xh.reshape(1)])
     idx = (y + jnp.array([0, 3, 1, 2], jnp.int32)) % 4
-    a0 = attend(got, where, 0, (facts, idx, z_order, x_order, places, core1))
-    a1, held_map = attend(got, where, 1, (frame_map,))
+    a0, got = attend(
+        0, where, source, *got, idx, z_order, x_order, places, core1
+    )
+    a1, held_map = attend(1, where, got, frame_map)
     b0 = shifted(a0, "y", 1)
     c0 = shifted(a0, "y", -1)
     b1 = shifted(a1, "y", 1)
@@ -446,7 +494,7 @@
     keep_b, send_b = grad_of(1, core1, *done)
     got_b = shifted(send_b, "c", 1)
     logprob, lgrad, scale = logit_parts(
-        places, *parts, facts, far_facts, head_weight, hw_other
+        places, *parts, facts, head_weight, hw_other
     )
     scale_other = shifted(scale, "c", 1)
     summed = scaled((keep_a, keep_b), (got_a, got_b), scale, scale_other, head_input, lgrad)

time: 198 us -> 200 us (1.010)
  waiting for transfers between devices: 79.9 us -> 72 us
  starting transfers between devices: 62.6 us -> 68 us
  other arithmetic: 4.38 us -> 6.66 us
    ppermute x33 -> x28, waiting for transfers between devices: 79.9 us -> 52.6 us  [shifted(): return lax.ppermute(x, axis, [(i, (i + by) % count) for i in range(count)])]
    ppermute x0 -> x7, waiting for transfers between devices: none -> 19.4 us  [to_peer(): return lax.ppermute(x, ('xh', 'y'), pairs)]
    all_to_all x2 -> x1, starting transfers between devices: 17 us -> 3.73 us  [dealt(): return lax.all_to_all(x, axes, 0, 0, tiled=True)]
    ppermute x0 -> x7, starting transfers between devices: none -> 12.3 us  [to_peer(): return lax.ppermute(x, ('xh', 'y'), pairs)]
    ppermute x33 -> x28, starting transfers between devices: 45.6 us -> 51.9 us  [shifted(): return lax.ppermute(x, axis, [(i, (i + by) % count) for i in range(count)])]
    unnamed x18, local copies, waits for them, and re-layouts: 0.05 us -> 4.5 us
    slice x2, local copies, waits for them, and re-layouts: 3.37 us -> 0.04 us  [per_device(): half = (shifted(up[:2], line, 1), shifted(down[2:], line, -1))]
    another operation x3 -> x5, other arithmetic: 0.08 us -> 3.27 us  [the longest x3 1.99 us: episode_facts(): jnp.stack([c.astype(F32) for c in columns], axis=1)]
  transfers between devices with their start and end apart: 35 -> 36, of which waited for: 13 -> 10; matrix products, arithmetic and copies ran while one was open for 4% -> 2% of each run, Pallas kernels for 12% -> 14%
where the time goes in v4:
time: 200 us; the launch traced here: 199 us
  waiting for transfers between devices  72 us (36%)
  starting transfers between devices  68 us (34%)
  Pallas kernels  44.8 us (22%)
  other arithmetic  6.66 us (3%)
  local copies, waits for them, and re-layouts  6.16 us (3%)
    ppermute x28, waiting for transfers between devices, shifted(): return lax.ppermute(x, axis, [(i, (i + by) % count) for i in range(count)])  52.6 us
    ppermute x28, starting transfers between devices, shifted(): return lax.ppermute(x, axis, [(i, (i + by) % count) for i in range(count)])  51.9 us
    pallas_call x2, Pallas kernels, chunk_of(): pl.pallas_call(functools.partial(chunk_kernel, chunk), out_shape=tuple(sh...  19.4 us
    ppermute x7, waiting for transfers between devices, to_peer(): return lax.ppermute(x, ('xh', 'y'), pairs)  19.4 us
    ppermute x7, starting transfers between devices, to_peer(): return lax.ppermute(x, ('xh', 'y'), pairs)  12.3 us
    pallas_call x2, Pallas kernels, attend(): pl.pallas_call(functools.partial(attend_kernel, chunk), out_shape=(out, m...  10.9 us
    pallas_call x2, Pallas kernels, grad_of(): pl.pallas_call(functools.partial(grad_kernel, half), out_shape=(out, out)...  5.49 us
    unnamed x18, local copies, waits for them, and re-layouts  4.5 us
  transfers between devices with their start and end apart: 36, of which 10 were waited for; matrix products, arithmetic and copies ran while one was open for 2% of the time, Pallas kernels for 14%

profile of v4, /device:TPU:1, one launch (start us, length us, event | category | flops | bytes accessed | tf_op | source)
XLA Modules:
  0.0 199.4 jit_solution(17184923791565916851)
XLA Ops:
  5.1 2.5 %collective-permute-start.10 = (bf16[144,512]{1,0:T(8,128)(2,1)S(1)}, bf16[144,512]{1,0:T(8,128)(2,1)S(1)}, u32[]{:S(2)}, u32[]{:S(2)}) collective-permute-start(bf16[144,512]{1,0:T(8,128)(2,1)S(1)} %get-tuple-element.62), channel_id=1, source_target_pairs={{0,4},{4,8},{8,12},{12,0},{1,5},{5,9},{9,13},{13,1},{2,6},{6,10},{... | collective-permute-start | bytes 442376 | tf_op jit(solution)/shard_map/ppermute | solution.py:51
  7.6 2.2 %collective-permute-start.11 = (bf16[144,512]{1,0:T(8,128)(2,1)S(1)}, bf16[144,512]{1,0:T(8,128)(2,1)S(1)}, u32[]{:S(2)}, u32[]{:S(2)}) collective-permute-start(bf16[144,512]{1,0:T(8,128)(2,1)S(1)} %get-tuple-element.62), channel_id=1, source_target_pairs={{0,12},{4,0},{8,4},{12,8},{1,13},{5,1},{9,5},{13,9},{2,14},{6,2},{... | collective-permute-start | bytes 442376 | tf_op jit(solution)/shard_map/ppermute | solution.py:51
  9.8 1.2 collective-permute-start.12
  11.6 4.5 %pack.1 = (bf16[3,128,512]{2,1,0:T(8,128)(2,1)}, bf16[3,128,512]{2,1,0:T(8,128)(2,1)}, bf16[3,128,512]{2,1,0:T(8,128)(2,1)}, bf16[3,128,512]{2,1,0:T(8,128)(2,1)...) custom-call(s32[2]{0:T(128)} %pad_add_fusion.1.place_ref, ...), custom_call_target="tpu_custom_call" | custom-call | bytes 6291456 | tf_op jit(solution)/shard_map/pack/pallas_call | solution.py:79
  16.1 1.4 collective-permute-start
  17.5 2.6 %collective-permute-start.1 = (bf16[3,128,512]{2,1,0:T(8,128)(2,1)}, bf16[3,128,512]{2,1,0:T(8,128)(2,1)S(1)}, u32[]{:S(2)}, u32[]{:S(2)}) collective-permute-start(bf16[3,128,512]{2,1,0:T(8,128)(2,1)} %get-tuple-element.33), channel_id=1, source_target_pairs={{0,32},{16,48},{32,0},{48,16},{64,96},{80,112},{96,64},{112,80},{1... | collective-permute-start | bytes 1179656 | tf_op jit(solution)/shard_map/ppermute | solution.py:95
  20.1 1.1 collective-permute-start.2
  21.2 2.7 %collective-permute-start.3 = (bf16[3,128,512]{2,1,0:T(8,128)(2,1)}, bf16[3,128,512]{2,1,0:T(8,128)(2,1)S(1)}, u32[]{:S(2)}, u32[]{:S(2)}) collective-permute-start(bf16[3,128,512]{2,1,0:T(8,128)(2,1)} %get-tuple-element.35), channel_id=1, source_target_pairs={{0,64},{16,80},{32,96},{48,112},{64,0},{80,16},{96,32},{112,48},{1... | collective-permute-start | bytes 1179656 | tf_op jit(solution)/shard_map/ppermute | solution.py:95
  25.6 1.3 collective-permute-done.rest_2_
  26.9 4.1 %collective-permute-start.5 = (bf16[3,128,512]{2,1,0:T(8,128)(2,1)}, bf16[3,128,512]{2,1,0:T(8,128)(2,1)}, u32[]{:S(2)}, u32[]{:S(2)}) collective-permute-start(bf16[3,128,512]{2,1,0:T(8,128)(2,1)} %get-tuple-element.37), channel_id=1, source_target_pairs={{0,96},{16,112},{32,64},{48,80},{64,32},{80,48},{96,0},{112,16},{1... | collective-permute-start | bytes 1179656 | tf_op jit(solution)/shard_map/ppermute | solution.py:95
  31.0 18.0 %collective-permute-done.1.rest_3_ = bf16[3,128,512]{2,1,0:T(8,128)(2,1)S(1)} collective-permute-done((bf16[3,128,512]{2,1,0:T(8,128)(2,1)}, bf16[3,128,512]{2,1,0:T(8,128)(2,1)S(1)}, u32[]{:S(2)}, u32[]{:S(2)}) %collective-permute-start.1) | collective-permute-done | bytes 393248 | tf_op jit(solution)/shard_map/ppermute | solution.py:95
  49.2 1.3 collective-permute-start.13
  51.2 1.5 collective-permute-start.14
  53.4 6.1 %collective-permute-start.17 = (bf16[4,144,512]{2,1,0:T(8,128)(2,1)S(1)}, bf16[4,144,512]{2,1,0:T(8,128)(2,1)S(1)}, u32[]{:S(2)}, u32[]{:S(2)}) collective-permute-start(bf16[4,144,512]{2,1,0:T(8,128)(2,1)S(1)} %pad_maximum_fusion.refs_0_), channel_id=1, source_target_pairs={{0,1},{1,0},{2,3},{3,2},{4,5},{5,4},{6,7},{7,6},{8,9},{9,8},{10,11... | collective-permute-start | bytes 1769480 | tf_op jit(solution)/shard_map/ppermute | solution.py:51
  60.6 1.0 copy-done.3
  61.6 1.0 copy-done.5
  62.6 5.8 %attend.2 = (bf16[512,512]{1,0:T(8,128)(2,1)S(1)}, bf16[8,3,128,512]{3,2,1,0:T(8,128)(2,1)S(1)}) custom-call(s32[2]{0:T(128)S(1)} %pad_add_fusion.len_ref, s32[8]{0:T(128)S(1)} %fusion.12.rest_0_, bf16[3,128,512]{2,1,0:T(8,128)(2,1)S(1)} %copy-done.1, bf16[3,128,512]{2,1,0:T(8,128)(2,1)S(1)} %collective-permute-done.rest_2_, ...), custom_call_target="tpu_custom_call" | custom-call | flops 1073741824 | bytes 3145728 | tf_op jit(solution)/shard_map/attend/pallas_call | solution.py:139
  68.5 1.8 collective-permute-start.22
  70.2 7.7 %collective-permute-done.13.refs_1_ = bf16[4,144,512]{2,1,0:T(8,128)(2,1)S(1)} collective-permute-done((bf16[4,144,512]{2,1,0:T(8,128)(2,1)S(1)}, bf16[4,144,512]{2,1,0:T(8,128)(2,1)S(1)}, u32[]{:S(2)}, u32[]{:S(2)}) %collective-permute-start.13) | collective-permute-done | bytes 589856 | tf_op jit(solution)/shard_map/ppermute | solution.py:51
  78.0 3.8 %collective-permute-start.18 = (bf16[4,144,512]{2,1,0:T(8,128)(2,1)S(1)}, bf16[4,144,512]{2,1,0:T(8,128)(2,1)S(1)}, u32[]{:S(2)}, u32[]{:S(2)}) collective-permute-start(bf16[4,144,512]{2,1,0:T(8,128)(2,1)S(1)} %collective-permute-done.13.refs_1_), channel_id=1, source_target_pairs={{0,1},{1,0},{2,3},{3,2},{4,5},{5,4},{6,7},{7,6},{8,9},{9,8},{10,11... | collective-permute-start | bytes 1769480 | tf_op jit(solution)/shard_map/ppermute | solution.py:51
  82.3 2.4 %collective-permute-start.16 = (bf16[2,144,512]{2,1,0:T(8,128)(2,1)S(1)}, bf16[2,144,512]{2,1,0:T(8,128)(2,1)S(1)}, u32[]{:S(2)}, u32[]{:S(2)}) collective-permute-start(bf16[2,144,512]{2,1,0:T(8,128)(2,1)S(1)} %slice.29), channel_id=1, source_target_pairs={{0,66},{2,0},{64,2},{66,64},{1,67},{3,1},{65,3},{67,65},{4,70},{6,... | collective-permute-start | bytes 884744 | tf_op jit(solution)/shard_map/ppermute | solution.py:51
  84.7 5.1 %attend.3 = (bf16[512,512]{1,0:T(8,128)(2,1)S(1)}, bf16[2048,2176]{1,0:T(8,128)(2,1)S(1)}) custom-call(s32[2]{0:T(128)S(1)} %pad_add_fusion.len_ref, bf16[8,3,128,512]{3,2,1,0:T(8,128)(2,1)S(1)} %get-tuple-element.39.rest_0_, bf16[2048,2176]{1,0:T(8,128)(2,1)} %rest_1_.2), custom_call_target="tpu_custom_call" | custom-call | flops 1073741824 | bytes 3145728 | tf_op jit(solution)/shard_map/attend/pallas_call | solution.py:139
  89.8 2.5 %collective-permute-start.23 = (bf16[512,512]{1,0:T(8,128)(2,1)S(1)}, bf16[512,512]{1,0:T(8,128)(2,1)S(1)}, u32[]{:S(2)}, u32[]{:S(2)}) collective-permute-start(bf16[512,512]{1,0:T(8,128)(2,1)S(1)} %get-tuple-element.43.a_ref), channel_id=1, source_target_pairs={{0,48},{16,0},{32,16},{48,32},{1,49},{17,1},{33,17},{49,33},{2,50}... | collective-permute-start | bytes 1572872 | tf_op jit(solution)/shard_map/ppermute | solution.py:51
  92.3 1.6 collective-permute-start.8
  94.0 1.6 collective-permute-start.20
  95.7 1.1 collective-permute-done.20.refs_8_
  96.8 1.3 collective-permute-start.26
  98.1 1.7 collective-permute-start.25
  99.8 1.6 assemble.1
  101.4 1.2 collective-permute-done.23.c_ref
  102.6 2.0 %collective-permute-start.7 = (bf16[512,512]{1,0:T(8,128)(2,1)S(1)}, bf16[512,512]{1,0:T(8,128)(2,1)S(1)}, u32[]{:S(2)}, u32[]{:S(2)}) collective-permute-start(bf16[512,512]{1,0:T(8,128)(2,1)S(1)} %get-tuple-element.40.a_ref), channel_id=1, source_target_pairs={{0,16},{16,32},{32,48},{48,0},{1,17},{17,33},{33,49},{49,1},{2,18}... | collective-permute-start | bytes 1572872 | tf_op jit(solution)/shard_map/ppermute | solution.py:51
  104.7 9.2 %collective-permute-done.8.c_ref = bf16[512,512]{1,0:T(8,128)(2,1)S(1)} collective-permute-done((bf16[512,512]{1,0:T(8,128)(2,1)S(1)}, bf16[512,512]{1,0:T(8,128)(2,1)S(1)}, u32[]{:S(2)}, u32[]{:S(2)}) %collective-permute-start.8) | collective-permute-done | bytes 524320 | tf_op jit(solution)/shard_map/ppermute | solution.py:51
  113.9 3.4 %collective-permute-start.9 = (bf16[512,512]{1,0:T(8,128)(2,1)S(1)}, bf16[512,512]{1,0:T(8,128)(2,1)S(1)}, u32[]{:S(2)}, u32[]{:S(2)}) collective-permute-start(bf16[512,512]{1,0:T(8,128)(2,1)S(1)} %collective-permute-done.8.c_ref), channel_id=1, source_target_pairs={{0,48},{16,0},{32,16},{48,32},{1,49},{17,1},{33,17},{49,33},{2,50}... | collective-permute-start | bytes 1572872 | tf_op jit(solution)/shard_map/ppermute | solution.py:51
  117.3 9.6 %chunk.2 = (bf16[512,2176]{1,0:T(8,128)(2,1)S(1)}, bf16[512,1024]{1,0:T(8,128)(2,1)S(1)}, f32[8,1024]{1,0:T(8,128)S(1)}) custom-call(s32[4]{0:T(128)S(1)} %get-tuple-element.71.rest_9_.idx_ref, s32[2]{0:T(128)S(1)} %pad_add_fusion.len_ref, bf16[512,512]{1,0:T(8,128)(2,1)S(1)} %get-tuple-element.43.a_ref, bf16[512,512]{1,0:T(8,128)(2,1)S(1)} %collective-permute-done.22.b_ref, ...), custom_call_target="tpu_custom_call" | custom-call | flops 6845104128 | bytes 20971520 | tf_op jit(solution)/shard_map/chunk/pallas_call | solution.py:221
  126.9 9.8 %chunk.3 = (bf16[512,2176]{1,0:T(8,128)(2,1)S(1)}, bf16[512,1024]{1,0:T(8,128)(2,1)S(1)}, bf16[8,1024]{1,0:T(8,128)(2,1)S(1)}, f32[8,256]{1,0:T(8,128)S(1)}) custom-call(s32[4]{0:T(128)S(1)} %get-tuple-element.71.rest_9_.idx_ref, s32[2]{0:T(128)S(1)} %pad_add_fusion.len_ref, bf16[512,512]{1,0:T(8,128)(2,1)S(1)} %get-tuple-element.40.a_ref, ...), custom_call_target="tpu_custom_call" | custom-call | flops 6845104128 | bytes 20971520 | tf_op jit(solution)/shard_map/chunk/pallas_call | solution.py:221
  136.7 2.8 %grad.3 = (bf16[8,136,512]{2,1,0:T(8,128)(2,1)S(1)}, bf16[8,136,512]{2,1,0:T(8,128)(2,1)S(1)}) custom-call(s32[1]{0:T(128)} %bitcast.2.rest_13_.core_ref, bf16[512,2176]{1,0:T(8,128)(2,1)S(1)} %get-tuple-element.48.f0_ref, bf16[512,1024]{1,0:T(8,128)(2,1)S(1)} %get-tuple-element.49.s0_ref, bf16[512,2176]{1,0:T(8,128)(2,1)S(1)} %get-tuple-element.50.f1_ref, ...), custom_call_target="tpu_custom_call" | custom-call | flops 2281701376 | bytes 6291456 | tf_op jit(solution)/shard_map/grad/pallas_call | solution.py:288
  139.5 2.7 %grad.2 = (bf16[8,136,512]{2,1,0:T(8,128)(2,1)S(1)}, bf16[8,136,512]{2,1,0:T(8,128)(2,1)S(1)}) custom-call(s32[1]{0:T(128)} %bitcast.2.rest_13_.core_ref, bf16[512,2176]{1,0:T(8,128)(2,1)S(1)} %get-tuple-element.48.f0_ref, bf16[512,1024]{1,0:T(8,128)(2,1)S(1)} %get-tuple-element.49.s0_ref, bf16[512,2176]{1,0:T(8,128)(2,1)S(1)} %get-tuple-element.50.f1_ref, ...), custom_call_target="tpu_custom_call" | custom-call | flops 2281701376 | bytes 6291456 | tf_op jit(solution)/shard_map/grad/pallas_call | solution.py:288
  142.2 2.6 %collective-permute-start.32 = (bf16[8,136,512]{2,1,0:T(8,128)(2,1)S(1)}, bf16[8,136,512]{2,1,0:T(8,128)(2,1)S(1)}, u32[]{:S(2)}, u32[]{:S(2)}) collective-permute-start(bf16[8,136,512]{2,1,0:T(8,128)(2,1)S(1)} %get-tuple-element.55), channel_id=1, source_target_pairs={{0,1},{1,0},{2,3},{3,2},{4,5},{5,4},{6,7},{7,6},{8,9},{9,8},{10,11... | collective-permute-start | bytes 3342344 | tf_op jit(solution)/shard_map/ppermute | solution.py:51
  144.9 2.3 %collective-permute-start.27 = (f32[8,256]{1,0:T(8,128)S(1)}, f32[8,256]{1,0:T(8,128)S(1)}, u32[]{:S(2)}, u32[]{:S(2)}) collective-permute-start(f32[8,256]{1,0:T(8,128)S(1)} %get-tuple-element.45.refs_0_), channel_id=1, source_target_pairs={{0,32},{16,48},{32,0},{48,16},{1,33},{17,49},{33,1},{49,17},{2,34}... | collective-permute-start | bytes 24584 | tf_op jit(solution)/shard_map/ppermute | solution.py:51
  147.2 1.7 collective-permute-start.28
  148.9 1.0 collective-permute-start.29
  149.9 1.0 collective-permute-done.28.refs_2_
  151.9 2.2 %collective-permute-start.33 = (f32[8,1024]{1,0:T(8,128)S(1)}, f32[8,1024]{1,0:T(8,128)S(1)}, u32[]{:S(2)}, u32[]{:S(2)}) collective-permute-start(f32[8,1024]{1,0:T(8,128)S(1)} %get-tuple-element.56.mine_ref), channel_id=1, source_target_pairs={{0,1},{1,0},{2,3},{3,2},{4,5},{5,4},{6,7},{7,6},{8,9},{9,8},{10,11... | collective-permute-start | bytes 98312 | tf_op jit(solution)/shard_map/ppermute | solution.py:51
  155.0 2.3 %scaled.1 = bf16[8,2,152,512]{3,2,1,0:T(8,128)(2,1)} custom-call(bf16[8,136,512]{2,1,0:T(8,128)(2,1)S(1)} %get-tuple-element.52.keep0, bf16[8,136,512]{2,1,0:T(8,128)(2,1)S(1)} %get-tuple-element.53.keep1, bf16[8,136,512]{2,1,0:T(8,128)(2,1)S(1)} %collective-permute-done.31.got0, bf16[8,136,512]{2,1,0:T(8,128)(2,1)S(1)} %collective-permute-done.32.got1, ...), custom_call_target="tpu_custom_call" | custom-call | flops 8388608 | bytes 7340032 | tf_op jit(solution)/shard_map/scaled/pallas_call | solution.py:386
  157.4 3.7 %all-to-all-start = ((bf16[16,152,512]{2,1,0:T(8,128)(2,1)}), bf16[16,152,512]{2,1,0:T(8,128)(2,1)S(1)}, u32[]{:S(2)}, u32[]{:S(2)}) async-start(bf16[16,152,512]{2,1,0:T(8,128)(2,1)} %bitcast.13), calls=%async_computation | async-start | bytes 4980736 | tf_op jit(solution)/shard_map/all_to_all | solution.py:55
  161.2 2.8 %collective-permute-start.30 = (f32[1,7]{1,0:T(1,128)S(1)}, f32[1,7]{1,0:T(1,128)S(1)}, u32[]{:S(2)}, u32[]{:S(2)}) collective-permute-start(f32[1,7]{1,0:T(1,128)S(1)} %bitcast.38), channel_id=1, source_target_pairs={{0,64},{64,0},{1,65},{65,1},{2,66},{66,2},{3,67},{67,3},{4,68},{68... | collective-permute-start | bytes 92 | tf_op jit(solution)/shard_map/ppermute | solution.py:51
  164.0 31.0 %collective-permute-done.30 = f32[1,7]{1,0:T(1,128)S(1)} collective-permute-done((f32[1,7]{1,0:T(1,128)S(1)}, f32[1,7]{1,0:T(1,128)S(1)}, u32[]{:S(2)}, u32[]{:S(2)}) %collective-permute-start.30) | collective-permute-done | bytes 60 | tf_op jit(solution)/shard_map/ppermute | solution.py:51
  195.2 1.7 collective-permute-start.34
  (81 shorter events, 14.7 us)
Async XLA Ops:
  0.6 23.7 %copy-start.8 = (s32[2]{0:T(128)S(1)}, s32[2]{0:T(128)}, u32[]{:S(2)}) copy-start(s32[2]{0:T(128)} %param.18) | copy-start | bytes 28
  5.1 54.5 %copy-start.7 = (s32[4]{0:T(128)S(1)}, s32[4]{0:T(128)}, u32[]{:S(2)}) copy-start(s32[4]{0:T(128)} %constant.119.clone) | copy-start | bytes 52
  5.1 15.0 %collective-permute-start.10 = (bf16[144,512]{1,0:T(8,128)(2,1)S(1)}, bf16[144,512]{1,0:T(8,128)(2,1)S(1)}, u32[]{:S(2)}, u32[]{:S(2)}) collective-permute-start(bf16[144,512]{1,0:T(8,128)(2,1)S(1)} %get-tuple-element.62), channel_id=1, source_target_pairs={{0,4},{4,8},{8,12},{12,0},{1,5},{5,9},{9,13},{13,1},{2,6},{6,10},{... | collective-permute-start | bytes 442376 | tf_op jit(solution)/shard_map/ppermute | solution.py:51
  7.6 13.6 %collective-permute-start.11 = (bf16[144,512]{1,0:T(8,128)(2,1)S(1)}, bf16[144,512]{1,0:T(8,128)(2,1)S(1)}, u32[]{:S(2)}, u32[]{:S(2)}) collective-permute-start(bf16[144,512]{1,0:T(8,128)(2,1)S(1)} %get-tuple-element.62), channel_id=1, source_target_pairs={{0,12},{4,0},{8,4},{12,8},{1,13},{5,1},{9,5},{13,9},{2,14},{6,2},{... | collective-permute-start | bytes 442376 | tf_op jit(solution)/shard_map/ppermute | solution.py:51
  9.8 14.1 %collective-permute-start.12 = (bf16[144,512]{1,0:T(8,128)(2,1)S(1)}, bf16[144,512]{1,0:T(8,128)(2,1)S(1)}, u32[]{:S(2)}, u32[]{:S(2)}) collective-permute-start(bf16[144,512]{1,0:T(8,128)(2,1)S(1)} %get-tuple-element.62), channel_id=1, source_target_pairs={{0,8},{4,12},{8,0},{12,4},{1,9},{5,13},{9,1},{13,5},{2,10},{6,14},... | collective-permute-start | bytes 442376 | tf_op jit(solution)/shard_map/ppermute | solution.py:51
  16.1 10.8 %collective-permute-start = (bf16[3,128,512]{2,1,0:T(8,128)(2,1)}, bf16[3,128,512]{2,1,0:T(8,128)(2,1)S(1)}, u32[]{:S(2)}, u32[]{:S(2)}) collective-permute-start(bf16[3,128,512]{2,1,0:T(8,128)(2,1)} %get-tuple-element.32), channel_id=1, source_target_pairs={{0,16},{16,32},{32,48},{48,0},{64,80},{80,96},{96,112},{112,64},{1... | collective-permute-start | bytes 1179656 | tf_op jit(solution)/shard_map/ppermute | solution.py:95
  17.5 31.6 %collective-permute-start.1 = (bf16[3,128,512]{2,1,0:T(8,128)(2,1)}, bf16[3,128,512]{2,1,0:T(8,128)(2,1)S(1)}, u32[]{:S(2)}, u32[]{:S(2)}) collective-permute-start(bf16[3,128,512]{2,1,0:T(8,128)(2,1)} %get-tuple-element.33), channel_id=1, source_target_pairs={{0,32},{16,48},{32,0},{48,16},{64,96},{80,112},{96,64},{112,80},{1... | collective-permute-start | bytes 1179656 | tf_op jit(solution)/shard_map/ppermute | solution.py:95
  20.1 29.0 %collective-permute-start.2 = (bf16[3,128,512]{2,1,0:T(8,128)(2,1)}, bf16[3,128,512]{2,1,0:T(8,128)(2,1)S(1)}, u32[]{:S(2)}, u32[]{:S(2)}) collective-permute-start(bf16[3,128,512]{2,1,0:T(8,128)(2,1)} %get-tuple-element.34), channel_id=1, source_target_pairs={{0,48},{16,0},{32,16},{48,32},{64,112},{80,64},{96,80},{112,96},{1... | collective-permute-start | bytes 1179656 | tf_op jit(solution)/shard_map/ppermute | solution.py:95
  21.2 29.3 %collective-permute-start.3 = (bf16[3,128,512]{2,1,0:T(8,128)(2,1)}, bf16[3,128,512]{2,1,0:T(8,128)(2,1)S(1)}, u32[]{:S(2)}, u32[]{:S(2)}) collective-permute-start(bf16[3,128,512]{2,1,0:T(8,128)(2,1)} %get-tuple-element.35), channel_id=1, source_target_pairs={{0,64},{16,80},{32,96},{48,112},{64,0},{80,16},{96,32},{112,48},{1... | collective-permute-start | bytes 1179656 | tf_op jit(solution)/shard_map/ppermute | solution.py:95
  23.9 28.7 %collective-permute-start.4 = (bf16[3,128,512]{2,1,0:T(8,128)(2,1)}, bf16[3,128,512]{2,1,0:T(8,128)(2,1)S(1)}, u32[]{:S(2)}, u32[]{:S(2)}) collective-permute-start(bf16[3,128,512]{2,1,0:T(8,128)(2,1)} %get-tuple-element.36), channel_id=1, source_target_pairs={{0,80},{16,96},{32,112},{48,64},{64,16},{80,32},{96,48},{112,0},{1... | collective-permute-start | bytes 1179656 | tf_op jit(solution)/shard_map/ppermute | solution.py:95
  26.9 32.7 %collective-permute-start.5 = (bf16[3,128,512]{2,1,0:T(8,128)(2,1)}, bf16[3,128,512]{2,1,0:T(8,128)(2,1)}, u32[]{:S(2)}, u32[]{:S(2)}) collective-permute-start(bf16[3,128,512]{2,1,0:T(8,128)(2,1)} %get-tuple-element.37), channel_id=1, source_target_pairs={{0,96},{16,112},{32,64},{48,80},{64,32},{80,48},{96,0},{112,16},{1... | collective-permute-start | bytes 1179656 | tf_op jit(solution)/shard_map/ppermute | solution.py:95
  49.1 10.6 %collective-permute-start.6 = (bf16[3,128,512]{2,1,0:T(8,128)(2,1)}, bf16[3,128,512]{2,1,0:T(8,128)(2,1)}, u32[]{:S(2)}, u32[]{:S(2)}) collective-permute-start(bf16[3,128,512]{2,1,0:T(8,128)(2,1)} %get-tuple-element.38), channel_id=1, source_target_pairs={{0,112},{16,64},{32,80},{48,96},{64,48},{80,0},{96,16},{112,32},{1... | collective-permute-start | bytes 1179656 | tf_op jit(solution)/shard_map/ppermute | solution.py:95
  49.2 28.8 %collective-permute-start.13 = (bf16[4,144,512]{2,1,0:T(8,128)(2,1)S(1)}, bf16[4,144,512]{2,1,0:T(8,128)(2,1)S(1)}, u32[]{:S(2)}, u32[]{:S(2)}) collective-permute-start(bf16[4,144,512]{2,1,0:T(8,128)(2,1)S(1)} %pad_maximum_fusion.refs_0_), channel_id=1, source_target_pairs={{0,2},{2,64},{64,66},{66,0},{1,3},{3,65},{65,67},{67,1},{4,6},{6,6... | collective-permute-start | bytes 1769480 | tf_op jit(solution)/shard_map/ppermute | solution.py:51
  50.5 0.8 copy-start.2
  51.2 30.6 %collective-permute-start.14 = (bf16[4,144,512]{2,1,0:T(8,128)(2,1)S(1)}, bf16[4,144,512]{2,1,0:T(8,128)(2,1)S(1)}, u32[]{:S(2)}, u32[]{:S(2)}) collective-permute-start(bf16[4,144,512]{2,1,0:T(8,128)(2,1)S(1)} %pad_maximum_fusion.refs_0_), channel_id=1, source_target_pairs={{0,66},{2,0},{64,2},{66,64},{1,67},{3,1},{65,3},{67,65},{4,70},{6,... | collective-permute-start | bytes 1769480 | tf_op jit(solution)/shard_map/ppermute | solution.py:51
  52.7 0.8 copy-start.4
  53.4 28.9 %collective-permute-start.17 = (bf16[4,144,512]{2,1,0:T(8,128)(2,1)S(1)}, bf16[4,144,512]{2,1,0:T(8,128)(2,1)S(1)}, u32[]{:S(2)}, u32[]{:S(2)}) collective-permute-start(bf16[4,144,512]{2,1,0:T(8,128)(2,1)S(1)} %pad_maximum_fusion.refs_0_), channel_id=1, source_target_pairs={{0,1},{1,0},{2,3},{3,2},{4,5},{5,4},{6,7},{7,6},{8,9},{9,8},{10,11... | collective-permute-start | bytes 1769480 | tf_op jit(solution)/shard_map/ppermute | solution.py:51
  59.6 1.0 copy-start.1
  60.6 1.0 copy-start.3
  61.6 1.0 copy-start.5
  68.5 21.3 %collective-permute-start.22 = (bf16[512,512]{1,0:T(8,128)(2,1)S(1)}, bf16[512,512]{1,0:T(8,128)(2,1)S(1)}, u32[]{:S(2)}, u32[]{:S(2)}) collective-permute-start(bf16[512,512]{1,0:T(8,128)(2,1)S(1)} %get-tuple-element.43.a_ref), channel_id=1, source_target_pairs={{0,16},{16,32},{32,48},{48,0},{1,17},{17,33},{33,49},{49,1},{2,18}... | collective-permute-start | bytes 1572872 | tf_op jit(solution)/shard_map/ppermute | solution.py:51
  78.0 16.0 %collective-permute-start.18 = (bf16[4,144,512]{2,1,0:T(8,128)(2,1)S(1)}, bf16[4,144,512]{2,1,0:T(8,128)(2,1)S(1)}, u32[]{:S(2)}, u32[]{:S(2)}) collective-permute-start(bf16[4,144,512]{2,1,0:T(8,128)(2,1)S(1)} %collective-permute-done.13.refs_1_), channel_id=1, source_target_pairs={{0,1},{1,0},{2,3},{3,2},{4,5},{5,4},{6,7},{7,6},{8,9},{9,8},{10,11... | collective-permute-start | bytes 1769480 | tf_op jit(solution)/shard_map/ppermute | solution.py:51
  81.8 13.8 %collective-permute-start.19 = (bf16[4,144,512]{2,1,0:T(8,128)(2,1)S(1)}, bf16[4,144,512]{2,1,0:T(8,128)(2,1)S(1)}, u32[]{:S(2)}, u32[]{:S(2)}) collective-permute-start(bf16[4,144,512]{2,1,0:T(8,128)(2,1)S(1)} %collective-permute-done.14.refs_2_), channel_id=1, source_target_pairs={{0,1},{1,0},{2,3},{3,2},{4,5},{5,4},{6,7},{7,6},{8,9},{9,8},{10,11... | collective-permute-start | bytes 1769480 | tf_op jit(solution)/shard_map/ppermute | solution.py:51
  81.9 10.5 %collective-permute-start.15 = (bf16[2,144,512]{2,1,0:T(8,128)(2,1)S(1)}, bf16[2,144,512]{2,1,0:T(8,128)(2,1)S(1)}, u32[]{:S(2)}, u32[]{:S(2)}) collective-permute-start(bf16[2,144,512]{2,1,0:T(8,128)(2,1)S(1)} %slice.28), channel_id=1, source_target_pairs={{0,2},{2,64},{64,66},{66,0},{1,3},{3,65},{65,67},{67,1},{4,6},{6,6... | collective-permute-start | bytes 884744 | tf_op jit(solution)/shard_map/ppermute | solution.py:51
  82.3 11.7 %collective-permute-start.16 = (bf16[2,144,512]{2,1,0:T(8,128)(2,1)S(1)}, bf16[2,144,512]{2,1,0:T(8,128)(2,1)S(1)}, u32[]{:S(2)}, u32[]{:S(2)}) collective-permute-start(bf16[2,144,512]{2,1,0:T(8,128)(2,1)S(1)} %slice.29), channel_id=1, source_target_pairs={{0,66},{2,0},{64,2},{66,64},{1,67},{3,1},{65,3},{67,65},{4,70},{6,... | collective-permute-start | bytes 884744 | tf_op jit(solution)/shard_map/ppermute | solution.py:51
  84.7 12.1 %copy-start = (bf16[512,256]{1,0:T(8,128)(2,1)S(1)}, bf16[512,256]{1,0:T(8,128)(2,1)}, u32[]{:S(2)}) copy-start(bf16[512,256]{1,0:T(8,128)(2,1)} %refs_5_.1) | copy-start | bytes 786436
  84.7 13.4 %copy-start.6 = (f32[7,512]{1,0:T(8,128)S(1)}, f32[7,512]{1,0:T(8,128)}, u32[]{:S(2)}) copy-start(f32[7,512]{1,0:T(8,128)} %rest_1_.3) | copy-start | bytes 43012
  89.8 12.8 %collective-permute-start.23 = (bf16[512,512]{1,0:T(8,128)(2,1)S(1)}, bf16[512,512]{1,0:T(8,128)(2,1)S(1)}, u32[]{:S(2)}, u32[]{:S(2)}) collective-permute-start(bf16[512,512]{1,0:T(8,128)(2,1)S(1)} %get-tuple-element.43.a_ref), channel_id=1, source_target_pairs={{0,48},{16,0},{32,16},{48,32},{1,49},{17,1},{33,17},{49,33},{2,50}... | collective-permute-start | bytes 1572872 | tf_op jit(solution)/shard_map/ppermute | solution.py:51
  92.3 21.5 %collective-permute-start.8 = (bf16[512,512]{1,0:T(8,128)(2,1)S(1)}, bf16[512,512]{1,0:T(8,128)(2,1)S(1)}, u32[]{:S(2)}, u32[]{:S(2)}) collective-permute-start(bf16[512,512]{1,0:T(8,128)(2,1)S(1)} %get-tuple-element.40.a_ref), channel_id=1, source_target_pairs={{0,48},{16,0},{32,16},{48,32},{1,49},{17,1},{33,17},{49,33},{2,50}... | collective-permute-start | bytes 1572872 | tf_op jit(solution)/shard_map/ppermute | solution.py:51
  94.0 23.3 %collective-permute-start.24 = (bf16[512,512]{1,0:T(8,128)(2,1)S(1)}, bf16[512,512]{1,0:T(8,128)(2,1)S(1)}, u32[]{:S(2)}, u32[]{:S(2)}) collective-permute-start(bf16[512,512]{1,0:T(8,128)(2,1)S(1)} %collective-permute-done.22.b_ref), channel_id=1, source_target_pairs={{0,16},{16,32},{32,48},{48,0},{1,17},{17,33},{33,49},{49,1},{2,18}... | collective-permute-start | bytes 1572872 | tf_op jit(solution)/shard_map/ppermute | solution.py:51
  94.0 2.9 %collective-permute-start.20 = (bf16[2,144,512]{2,1,0:T(8,128)(2,1)S(1)}, bf16[2,144,512]{2,1,0:T(8,128)(2,1)S(1)}, u32[]{:S(2)}, u32[]{:S(2)}) collective-permute-start(bf16[2,144,512]{2,1,0:T(8,128)(2,1)S(1)} %collective-permute-done.15.refs_3_), channel_id=1, source_target_pairs={{0,1},{1,0},{2,3},{3,2},{4,5},{5,4},{6,7},{7,6},{8,9},{9,8},{10,11... | collective-permute-start | bytes 884744 | tf_op jit(solution)/shard_map/ppermute | solution.py:51
  95.6 2.5 %collective-permute-start.21 = (bf16[2,144,512]{2,1,0:T(8,128)(2,1)S(1)}, bf16[2,144,512]{2,1,0:T(8,128)(2,1)S(1)}, u32[]{:S(2)}, u32[]{:S(2)}) collective-permute-start(bf16[2,144,512]{2,1,0:T(8,128)(2,1)S(1)} %collective-permute-done.16.refs_4_), channel_id=1, source_target_pairs={{0,1},{1,0},{2,3},{3,2},{4,5},{5,4},{6,7},{7,6},{8,9},{9,8},{10,11... | collective-permute-start | bytes 884744 | tf_op jit(solution)/shard_map/ppermute | solution.py:51
  96.8 30.1 %collective-permute-start.26 = (bf16[512,256]{1,0:T(8,128)(2,1)S(1)}, bf16[512,256]{1,0:T(8,128)(2,1)S(1)}, u32[]{:S(2)}, u32[]{:S(2)}) collective-permute-start(bf16[512,256]{1,0:T(8,128)(2,1)S(1)} %copy-done), channel_id=1, source_target_pairs={{0,64},{64,0},{1,65},{65,1},{2,66},{66,2},{3,67},{67,3},{4,68},{68... | collective-permute-start | bytes 786440 | tf_op jit(solution)/shard_map/ppermute | solution.py:51
  98.1 28.8 %collective-permute-start.25 = (f32[7,512]{1,0:T(8,128)S(1)}, f32[7,512]{1,0:T(8,128)S(1)}, u32[]{:S(2)}, u32[]{:S(2)}) collective-permute-start(f32[7,512]{1,0:T(8,128)S(1)} %copy-done.6), channel_id=1, source_target_pairs={{0,64},{64,0},{1,65},{65,1},{2,66},{66,2},{3,67},{67,3},{4,68},{68... | collective-permute-start | bytes 43016 | tf_op jit(solution)/shard_map/ppermute | solution.py:51
  102.6 24.3 %collective-permute-start.7 = (bf16[512,512]{1,0:T(8,128)(2,1)S(1)}, bf16[512,512]{1,0:T(8,128)(2,1)S(1)}, u32[]{:S(2)}, u32[]{:S(2)}) collective-permute-start(bf16[512,512]{1,0:T(8,128)(2,1)S(1)} %get-tuple-element.40.a_ref), channel_id=1, source_target_pairs={{0,16},{16,32},{32,48},{48,0},{1,17},{17,33},{33,49},{49,1},{2,18}... | collective-permute-start | bytes 1572872 | tf_op jit(solution)/shard_map/ppermute | solution.py:51
  113.9 13.0 %collective-permute-start.9 = (bf16[512,512]{1,0:T(8,128)(2,1)S(1)}, bf16[512,512]{1,0:T(8,128)(2,1)S(1)}, u32[]{:S(2)}, u32[]{:S(2)}) collective-permute-start(bf16[512,512]{1,0:T(8,128)(2,1)S(1)} %collective-permute-done.8.c_ref), channel_id=1, source_target_pairs={{0,48},{16,0},{32,16},{48,32},{1,49},{17,1},{33,17},{49,33},{2,50}... | collective-permute-start | bytes 1572872 | tf_op jit(solution)/shard_map/ppermute | solution.py:51
  142.2 12.8 %collective-permute-start.32 = (bf16[8,136,512]{2,1,0:T(8,128)(2,1)S(1)}, bf16[8,136,512]{2,1,0:T(8,128)(2,1)S(1)}, u32[]{:S(2)}, u32[]{:S(2)}) collective-permute-start(bf16[8,136,512]{2,1,0:T(8,128)(2,1)S(1)} %get-tuple-element.55), channel_id=1, source_target_pairs={{0,1},{1,0},{2,3},{3,2},{4,5},{5,4},{6,7},{7,6},{8,9},{9,8},{10,11... | collective-permute-start | bytes 3342344 | tf_op jit(solution)/shard_map/ppermute | solution.py:51
  144.8 10.2 %collective-permute-start.31 = (bf16[8,136,512]{2,1,0:T(8,128)(2,1)S(1)}, bf16[8,136,512]{2,1,0:T(8,128)(2,1)S(1)}, u32[]{:S(2)}, u32[]{:S(2)}) collective-permute-start(bf16[8,136,512]{2,1,0:T(8,128)(2,1)S(1)} %get-tuple-element.54), channel_id=1, source_target_pairs={{0,1},{1,0},{2,3},{3,2},{4,5},{5,4},{6,7},{7,6},{8,9},{9,8},{10,11... | collective-permute-start | bytes 3342344 | tf_op jit(solution)/shard_map/ppermute | solution.py:51
  144.9 5.0 %collective-permute-start.27 = (f32[8,256]{1,0:T(8,128)S(1)}, f32[8,256]{1,0:T(8,128)S(1)}, u32[]{:S(2)}, u32[]{:S(2)}) collective-permute-start(f32[8,256]{1,0:T(8,128)S(1)} %get-tuple-element.45.refs_0_), channel_id=1, source_target_pairs={{0,32},{16,48},{32,0},{48,16},{1,33},{17,49},{33,1},{49,17},{2,34}... | collective-permute-start | bytes 24584 | tf_op jit(solution)/shard_map/ppermute | solution.py:51
  147.2 3.7 %collective-permute-start.28 = (f32[8,256]{1,0:T(8,128)S(1)}, f32[8,256]{1,0:T(8,128)S(1)}, u32[]{:S(2)}, u32[]{:S(2)}) collective-permute-start(f32[8,256]{1,0:T(8,128)S(1)} %get-tuple-element.45.refs_0_), channel_id=1, source_target_pairs={{0,16},{16,32},{32,48},{48,0},{1,17},{17,33},{33,49},{49,1},{2,18}... | collective-permute-start | bytes 24584 | tf_op jit(solution)/shard_map/ppermute | solution.py:51
  148.9 2.5 %collective-permute-start.29 = (f32[8,256]{1,0:T(8,128)S(1)}, f32[8,256]{1,0:T(8,128)S(1)}, u32[]{:S(2)}, u32[]{:S(2)}) collective-permute-start(f32[8,256]{1,0:T(8,128)S(1)} %get-tuple-element.45.refs_0_), channel_id=1, source_target_pairs={{0,48},{16,0},{32,16},{48,32},{1,49},{17,1},{33,17},{49,33},{2,50}... | collective-permute-start | bytes 24584 | tf_op jit(solution)/shard_map/ppermute | solution.py:51
  151.9 3.1 %collective-permute-start.33 = (f32[8,1024]{1,0:T(8,128)S(1)}, f32[8,1024]{1,0:T(8,128)S(1)}, u32[]{:S(2)}, u32[]{:S(2)}) collective-permute-start(f32[8,1024]{1,0:T(8,128)S(1)} %get-tuple-element.56.mine_ref), channel_id=1, source_target_pairs={{0,1},{1,0},{2,3},{3,2},{4,5},{5,4},{6,7},{7,6},{8,9},{9,8},{10,11... | collective-permute-start | bytes 98312 | tf_op jit(solution)/shard_map/ppermute | solution.py:51
  157.4 37.7 %all-to-all-start = ((bf16[16,152,512]{2,1,0:T(8,128)(2,1)}), bf16[16,152,512]{2,1,0:T(8,128)(2,1)S(1)}, u32[]{:S(2)}, u32[]{:S(2)}) async-start(bf16[16,152,512]{2,1,0:T(8,128)(2,1)} %bitcast.13), calls=%async_computation | async-start | bytes 4980736 | tf_op jit(solution)/shard_map/all_to_all | solution.py:55
  161.2 33.8 %collective-permute-start.30 = (f32[1,7]{1,0:T(1,128)S(1)}, f32[1,7]{1,0:T(1,128)S(1)}, u32[]{:S(2)}, u32[]{:S(2)}) collective-permute-start(f32[1,7]{1,0:T(1,128)S(1)} %bitcast.38), channel_id=1, source_target_pairs={{0,64},{64,0},{1,65},{65,1},{2,66},{66,2},{3,67},{67,3},{4,68},{68... | collective-permute-start | bytes 92 | tf_op jit(solution)/shard_map/ppermute | solution.py:51
  195.2 3.2 %collective-permute-start.34 = (bf16[16,16,512]{2,0,1:T(8,128)(2,1)S(1)}, bf16[16,16,512]{2,0,1:T(8,128)(2,1)S(1)}, u32[]{:S(2)}, u32[]{:S(2)}) collective-permute-start(bf16[16,16,512]{2,0,1:T(8,128)(2,1)S(1)} %copy.43), channel_id=1, source_target_pairs={{0,1},{1,0},{2,3},{3,2},{4,5},{5,4},{6,7},{7,6},{8,9},{9,8},{10,11... | collective-permute-start | bytes 786440 | tf_op jit(solution)/shard_map/ppermute | solution.py:51
